TPU v7x, 32 devices: a whole 2x2x4 slice. The times are simulated.
32 devices in a mesh: dp: 4 (over z), ctx: 8 (over y, x, core).
Axes of the slice: x: 2, y: 2, z: 4, core: 2. Of those that a mesh axis runs over, the one named last changes fastest.
Arguments:
- query_stream: bfloat16 [4, 3072, 4096], P('dp', 'ctx'), may hold values from -6 to 6
- key_stream: bfloat16 [4, 3072, 4096], P('dp', 'ctx'), may hold values from -6 to 6
- value_stream: bfloat16 [4, 3072, 4096], P('dp', 'ctx'), may hold values from -6 to 6
- pole_rate: float32 [256, 16], replicated, may hold values from 6.4778646e-06 to 0.0401
- residue: float32 [256, 16], replicated, may hold values from -0.21220275 to 0.21220275
- skip_gain: float32 [4096], replicated, may hold values from 0.5 to 1.5
- out_weight: bfloat16 [4096, 4096], P(('dp', 'ctx')), may hold values from -0.09375 to 0.09375
Outputs:
- projected: bfloat16 [4, 3072, 4096], P('dp', 'ctx')
All inputs are finite; a program needn't handle non-finite values.
Results may differ from a plain program's by a relative error of at most 0.007.
Values may be sent and summed in bfloat16 or wider, within the bound.
No kernel may reach another device: no remote copies, remote signals or barrier semaphores. Data moves between devices by JAX's collectives and lax.ppermute only.
A program may use at most 192 MiB of HBM per device.

v0:
```python
import jax
import jax.numpy as jnp
import numpy as np
from jax import lax
from jax.experimental import pallas as pl
from jax.experimental.pallas import tpu as pltpu
from jax.sharding import PartitionSpec as P

BLOCK = 128
LANES = 128
COLS = 256
F32 = jnp.float32
BF16 = jnp.bfloat16
AXES = ("dp", "ctx")
fence = lax.optimization_barrier


def params(mib):
    return pltpu.CompilerParams(vmem_limit_bytes=mib << 20, dimension_semantics=("arbitrary",))


def split(a):
    high = a.astype(BF16)
    return high, (a - high.astype(F32)).astype(BF16)


def iota(shape, axis):
    return lax.broadcasted_iota(jnp.int32, shape, axis)


def state_kernel(members, poles, blocks, k_ref, v_ref, col_ref, lane_ref, d_ref, bs_ref, slab_ref):
    per = LANES // members
    for sub in range(k_ref.shape[1] // LANES):
        at = slice(sub * LANES, (sub + 1) * LANES)
        d = (k_ref[:, at].astype(F32) * v_ref[:, at].astype(F32)).astype(BF16)
        d_ref[:, at] = d
        rate = col_ref[sub * per * poles : (sub + 1) * per * poles, 0:1]
        back = (BLOCK - 1 - iota((per * poles, BLOCK), 1)).astype(F32)
        ending = jnp.concatenate(split(jnp.exp(-rate * back)), axis=0)
        tiles = jnp.concatenate([d[b * BLOCK : (b + 1) * BLOCK] for b in range(blocks)], axis=1)
        part = jnp.dot(ending, tiles, preferred_element_type=F32)
        part = part[: per * poles] + part[per * poles :]
        same = iota(part.shape, 0) // poles == (iota(part.shape, 1) % LANES) // members
        state = jnp.where(same, part, 0.0).reshape(per, poles, blocks * LANES).sum(axis=0)
        decay = jnp.exp(-lane_ref[:, at] * BLOCK)
        slab = None
        for b in range(blocks):
            one = state[:, b * LANES : (b + 1) * LANES]
            bs_ref[b * poles : (b + 1) * poles, at] = one
            slab = one if slab is None else slab * decay + one
        slab_ref[:, at] = slab


def conv_kernel(
    members, poles, blocks, d_ref, q_ref, col_ref, row_ref, bs_ref, inc_ref, lane_ref, skip_ref, g_ref
):
    per = LANES // members
    wide = per * poles
    for sub in range(d_ref.shape[1] // LANES):
        at = slice(sub * LANES, (sub + 1) * LANES)
        rate = col_ref[sub * wide : (sub + 1) * wide, 0:1]
        residue = col_ref[sub * wide : (sub + 1) * wide, 1:2]
        lag = ((BLOCK - iota((wide, BLOCK), 1)) % BLOCK).astype(F32)
        base = (residue * jnp.exp(-rate * lag)).reshape(per, poles, BLOCK).sum(axis=1)
        base = base.astype(BF16).astype(F32)
        causal = iota((BLOCK, BLOCK), 1) <= iota((BLOCK, BLOCK), 0)
        left = []
        for g in range(per):
            rows = jnp.broadcast_to(base[g : g + 1], (BLOCK, BLOCK))
            rows = pltpu.roll(rows, 0, 1, stride=1, stride_axis=0)
            left.append(jnp.where(causal, rows, 0.0).astype(BF16))
        ahead = (iota((BLOCK, wide), 0) + 1).astype(F32)
        at_row = slice(sub * wide, (sub + 1) * wide)
        reach = row_ref[1:2, at_row] * jnp.exp(-row_ref[0:1, at_row] * ahead)
        high, low = split(reach)
        left = jnp.concatenate(left + [high, low, high], axis=1)
        decay = jnp.exp(-lane_ref[:, at] * BLOCK)
        same = iota((wide, LANES), 0) // poles == iota((wide, LANES), 1) // members
        owner = iota((1, LANES), 1) // members
        state = inc_ref[:, at]
        right = []
        for b in range(blocks):
            tile = d_ref[b * BLOCK : (b + 1) * BLOCK, at]
            spread = jnp.where(same, jnp.concatenate([state] * per, axis=0), 0.0)
            s_high, s_low = split(spread)
            masked = [tile * jnp.where(owner == g, 1.0, 0.0).astype(BF16) for g in range(per)]
            right.append(jnp.concatenate(masked + [s_high, s_high, s_low], axis=0))
            if b + 1 < blocks:
                state = state * decay + bs_ref[b * poles : (b + 1) * poles, at]
        conv = jnp.dot(left, jnp.concatenate(right, axis=1), preferred_element_type=F32)
        for b in range(blocks):
            rows = slice(b * BLOCK, (b + 1) * BLOCK)
            whole = conv[:, b * LANES : (b + 1) * LANES] + skip_ref[:, at] * d_ref[rows, at].astype(F32)
            g_ref[sub, rows, :] = (q_ref[rows, at].astype(F32) * whole).astype(BF16)


def states(key, value, col, lane, members, poles):
    rows, width = key.shape
    blocks = rows // BLOCK
    step = 2 * LANES
    seq = pl.BlockSpec((rows, step), lambda i: (0, i))
    wide = step // members * poles
    return pl.pallas_call(
        lambda *refs: state_kernel(members, poles, blocks, *refs),
        grid=(width // step,),
        in_specs=[
            seq,
            seq,
            pl.BlockSpec((wide, 2), lambda i: (i, 0)),
            pl.BlockSpec((poles, step), lambda i: (0, i)),
        ],
        out_specs=[
            seq,
            pl.BlockSpec((blocks * poles, step), lambda i: (0, i)),
            pl.BlockSpec((poles, step), lambda i: (0, i)),
        ],
        out_shape=[
            jax.ShapeDtypeStruct((rows, width), BF16),
            jax.ShapeDtypeStruct((blocks * poles, width), F32),
            jax.ShapeDtypeStruct((poles, width), F32),
        ],
        compiler_params=params(32),
        name="states",
    )(key, value, col, lane)


def convolve(driven, query, col, row, block_state, incoming, lane, skip, members, poles):
    rows, width = driven.shape
    blocks = rows // BLOCK
    step = 2 * LANES
    seq = pl.BlockSpec((rows, step), lambda i: (0, i))
    wide = step // members * poles
    return pl.pallas_call(
        lambda *refs: conv_kernel(members, poles, blocks, *refs),
        grid=(width // step,),
        in_specs=[
            seq,
            seq,
            pl.BlockSpec((wide, 2), lambda i: (i, 0)),
            pl.BlockSpec((2, wide), lambda i: (0, i)),
            pl.BlockSpec((blocks * poles, step), lambda i: (0, i)),
            pl.BlockSpec((poles, step), lambda i: (0, i)),
            pl.BlockSpec((poles, step), lambda i: (0, i)),
            pl.BlockSpec((1, step), lambda i: (0, i)),
        ],
        out_specs=pl.BlockSpec((step // LANES, rows, LANES), lambda i: (i, 0, 0)),
        out_shape=jax.ShapeDtypeStruct((width // LANES, rows, LANES), BF16),
        compiler_params=params(32),
        name="convolve",
    )(driven, query, col, row, block_state, incoming, lane, skip)


def incoming_state(total, lane, rows, slabs):
    place = lax.axis_index("ctx")
    before = jnp.zeros_like(total)
    width = 1
    while width < slabs:
        other = lax.ppermute(total, "ctx", [(i, i ^ width) for i in range(slabs)])
        upper = (place // width) % 2 == 1
        offset = (place % width).astype(F32) * rows
        before = jnp.where(upper, before + other * jnp.exp(-lane * offset), before)
        decay = jnp.exp(-lane * float(rows * width))
        total = jnp.where(upper, other * decay + total, total * decay + other)
        width *= 2
    return before


def project_kernel(count, started, idx_ref, own_ref, peer_ref, *refs):
    pieces, refs = refs[:count], refs[count:]
    sums = None
    if started:
        sums = [refs[0][...], refs[1][...]]
        refs = refs[2:]
    for p in range(0, count, 2):
        weight = jnp.concatenate([pieces[p][0], pieces[p + 1][0]], axis=0)
        first, second = idx_ref[p], idx_ref[p + 1]
        parts = []
        for g_ref in (own_ref, peer_ref):
            gated = jnp.concatenate([g_ref[first], g_ref[second]], axis=1)
            parts.append(jnp.dot(gated, weight, preferred_element_type=F32))
        sums = parts if sums is None else [a + b for a, b in zip(sums, parts)]
    for o_ref, s in zip(refs, sums):
        o_ref[...] = s.astype(o_ref.dtype)


def project(idx, own, peer, pieces, wide, sums=None, dtype=F32):
    shards, rows, depth = own.shape
    count = len(pieces)
    whole = pl.BlockSpec((shards, rows, depth), lambda b, i: (0, 0, 0), pipeline_mode=pl.Buffered(1))
    block = pl.BlockSpec((rows, COLS), lambda b, i: (0, b))
    specs = [pl.BlockSpec((1, depth, COLS), lambda b, i, s=s: (s + b, 0, 0)) for _, s in pieces]
    started = sums is not None
    return pl.pallas_call(
        lambda *refs: project_kernel(count, started, *refs),
        grid_spec=pltpu.PrefetchScalarGridSpec(
            num_scalar_prefetch=1,
            grid=(wide // COLS,),
            in_specs=[whole, whole] + specs + [block] * (2 * started),
            out_specs=[block, block],
        ),
        out_shape=[jax.ShapeDtypeStruct((rows, wide), dtype)] * 2,
        compiler_params=params(48),
        name="project",
    )(idx, own, peer, *[a for a, _ in pieces], *(sums or ()))


def swap(a, devices, bit):
    return lax.ppermute(a, AXES, [(i, i ^ bit) for i in range(devices)])


def ahead(a, devices):
    return lax.ppermute(a, AXES, [(i, (i + 8) % devices) for i in range(devices)])


def local(mesh_shape, query_stream, key_stream, value_stream, pole_rate, residue, skip_gain, out_weight):
    seqs, rows, width = query_stream.shape
    groups, poles = pole_rate.shape
    members = width // groups
    slabs = mesh_shape["ctx"]
    devices = mesh_shape["dp"] * slabs
    depth, dout = out_weight.shape
    query, key, value = [a.reshape(rows, width) for a in (query_stream, key_stream, value_stream)]
    col = jnp.stack([pole_rate.reshape(-1), residue.reshape(-1)], axis=1)
    row = jnp.stack([pole_rate.reshape(-1), residue.reshape(-1)], axis=0)
    lane = jnp.repeat(pole_rate.T, members, axis=1)
    skip = skip_gain[None]

    if depth != LANES:
        driven, block_state, slab = states(key, value, col, lane, members, poles)
        incoming = incoming_state(slab, lane, rows, slabs)
        gated = convolve(driven, query, col, row, block_state, incoming, lane, skip, members, poles)
        weight = lax.all_gather(out_weight, AXES, axis=0, tiled=True)
        flat = gated.transpose(1, 0, 2).reshape(rows, width)
        out = jnp.dot(flat, weight, preferred_element_type=F32)
        return out.astype(BF16).reshape(seqs, rows, dout)

    place = lax.axis_index(AXES)
    core = place % 2
    half = dout // 2
    nb = half // COLS
    ring = devices // 8
    tiles = out_weight.reshape(depth, 2 * nb, COLS).transpose(1, 0, 2)
    mine = lax.dynamic_slice_in_dim(tiles, core * nb, nb, 0)
    give = lax.dynamic_slice_in_dim(tiles, (1 - core) * nb, nb, 0)
    got = swap(give, devices, 1)

    pieces = [(mine, 0, (0, 0, 0, 0)), (got, 0, (0, 0, 0, 1))]
    late = []
    cur = (mine, got)
    prev = None
    work = (key, value)
    for r in range(ring + 1):
        pay_x, pay_y = [], []
        if prev is not None:
            (a, ax), (b, by) = prev
            pay_x += [b, by]
            pay_y += [a, ax]
        if r < ring:
            pay_x.append(cur[0])
            pay_y.append(cur[1])
        pay_x = jnp.concatenate(pay_x, axis=0)
        pay_y = jnp.concatenate(pay_y, axis=0)
        pay_z = jnp.concatenate(cur, axis=0) if r + 1 < ring else None
        pay_x, pay_y, pay_z, work = fence((pay_x, pay_y, pay_z, work))
        new_z = ahead(pay_z, devices) if pay_z is not None else None
        new_x = swap(pay_x, devices, 2)
        new_y = swap(pay_y, devices, 4)
        if r == 0:
            work = states(*work, col, lane, members, poles)
        elif r == 1:
            driven, block_state, slab = work
            work = (driven, block_state, incoming_state(slab, lane, rows, slabs))
        elif r == 2:
            driven, block_state, incoming = work
            work = convolve(driven, query, col, row, block_state, incoming, lane, skip, members, poles)
        elif r == ring - 1:
            own = work
            work = (own, swap(own, devices, 1))
        elif r == ring:
            table = [p for p in pieces]
            idx = shard_table(place, ring, [p[2] for p in table])
            work = (work, project(idx, *work, [p[:2] for p in table], half))
        new_x, new_y, new_z, work = fence((new_x, new_y, new_z, work))
        at = 0
        if prev is not None:
            late = [
                (new_x, 0, (r - 1, 0, 1, 1)),
                (new_x, nb, (r - 1, 1, 1, 1)),
                (new_y, 0, (r - 1, 1, 0, 0)),
                (new_y, nb, (r - 1, 1, 1, 0)),
            ]
            if r < ring:
                pieces += late
            at = 2 * nb
        if r < ring:
            pieces += [(new_x, at, (r, 0, 1, 0)), (new_y, at, (r, 1, 0, 1))]
            prev = ((cur[0], new_x[at:]), (cur[1], new_y[at:]))
        if new_z is not None:
            pieces += [(new_z, 0, (r + 1, 0, 0, 0)), (new_z, nb, (r + 1, 0, 0, 1))]
            cur = (new_z[:nb], new_z[nb:])
    (own, peer), sums = work
    idx = shard_table(place, ring, [p[2] for p in late])
    out_own, out_peer = project(idx, own, peer, [p[:2] for p in late], half, sums, BF16)
    other = swap(out_peer, devices, 1)
    out = jnp.where(
        core == 0,
        jnp.concatenate([out_own, other], axis=1),
        jnp.concatenate([other, out_own], axis=1),
    )
    return out.reshape(seqs, rows, dout)


def shard_table(place, ring, steps):
    steps = np.asarray(steps, np.int32)
    z = (place // 8 + ring - steps[:, 0]) % ring
    low = (place % 8) ^ jnp.asarray(steps[:, 1] * 4 + steps[:, 2] * 2 + steps[:, 3])
    return (z * 8 + low).astype(jnp.int32)


def solution(mesh):
    shape = dict(mesh.shape)
    return jax.shard_map(
        lambda *args: local(shape, *args),
        mesh=mesh,
        in_specs=(
            P("dp", "ctx", None),
            P("dp", "ctx", None),
            P("dp", "ctx", None),
            P(),
            P(),
            P(),
            P(("dp", "ctx"), None),
        ),
        out_specs=P("dp", "ctx", None),
        check_vma=False,
    )
```

profile of v0, /device:TPU:1, one launch (start us, length us, event | category | flops | bytes accessed | tf_op | source)
XLA Modules:
  0.0 222.5 jit_solution(16530111122726928616)
XLA Ops:
  0.0 1.6 copy.25
  4.1 2.3 %pad_maximum_fusion.6 = bf16[16,128,256]{2,1,0:T(8,128)(2,1)} fusion(bf16[8,128,256]{2,1,0:T(8,128)(2,1)} %collective-permute-done.refs_4_, bf16[8,128,256]{2,1,0:T(8,128)(2,1)} %bitcast.1.refs_3_), kind=kLoop, calls=%fused_computation.7 | loop fusion | flops 524288 | bytes 2097152 | tf_op jit(solution)/shard_map/concatenate | solution.py:263
  6.3 2.4 %collective-permute-start.3 = (bf16[16,128,256]{2,1,0:T(8,128)(2,1)}, bf16[16,128,256]{2,1,0:T(8,128)(2,1)S(1)}, u32[]{:S(2)}, u32[]{:S(2)}) collective-permute-start(bf16[16,128,256]{2,1,0:T(8,128)(2,1)} %pad_maximum_fusion.6), channel_id=1, source_target_pairs={{0,8},{1,9},{2,10},{3,11},{4,12},{5,13},{6,14},{7,15},{8,16},{9,17... | collective-permute-start | bytes 3145736 | tf_op jit(solution)/shard_map/ppermute | solution.py:212
  12.4 2.0 broadcast_in_dim.7
  14.4 3.1 %reshape.74.refs_3_.refs_6_ = f32[16,4096]{1,0:T(8,128)S(1)} reshape(f32[16,256,16]{2,1,0:T(8,128)} %broadcast_in_dim.7) | data formatting | bytes 524288 | tf_op jit(solution)/shard_map/reshape | solution.py:225
  17.5 1.9 copy-done.5
  19.4 1.9 copy-done.6
  21.3 8.5 %states.1 = (bf16[384,4096]{1,0:T(8,128)(2,1)S(1)}, f32[48,4096]{1,0:T(8,128)S(1)}, f32[16,4096]{1,0:T(8,128)}) custom-call(bf16[384,4096]{1,0:T(8,128)(2,1)S(1)} %bitcast.10, bf16[384,4096]{1,0:T(8,128)(2,1)S(1)} %bitcast.11, f32[4096,2]{1,0:T(8,128)S(1)} %copy.30.refs_2_, f32[16,4096]{1,0:T(8,128)S(1)} %reshape.74.refs_3_.refs_6_), custom_call_target="tpu_custom_call" | custom-call | tf_op jit(solution)/shard_map/states/pallas_call | solution.py:103
  29.8 4.4 %collective-permute-done.3.refs_7_.refs_8_ = bf16[16,128,256]{2,1,0:T(8,128)(2,1)S(1)} collective-permute-done((bf16[16,128,256]{2,1,0:T(8,128)(2,1)}, bf16[16,128,256]{2,1,0:T(8,128)(2,1)S(1)}, u32[]{:S(2)}, u32[]{:S(2)}) %collective-permute-start.3) | collective-permute-done | bytes 1048608 | tf_op jit(solution)/shard_map/ppermute | solution.py:212
  34.3 3.6 %pad_maximum_fusion = (bf16[24,128,256]{2,1,0:T(8,128)(2,1)}, bf16[24,128,256]{2,1,0:T(8,128)(2,1)}) fusion(bf16[8,128,256]{2,1,0:T(8,128)(2,1)S(1)} %get-tuple-element.124, bf16[8,128,256]{2,1,0:T(8,128)(2,1)} %collective-permute-done.2.refs_6_, bf16[8,128,256]{2,1,0:T(8,128)(2,1)} %collective-permute-done.refs_4_, ...), kind=kLoop, calls=%fused_computation.1 | loop fusion | flops 3145728 | bytes 6291456 | tf_op jit(solution)/shard_map/concatenate | solution.py:261
  38.8 1.4 collective-permute-done.7
  40.2 1.8 add_select_fusion.3
  44.8 5.1 %collective-permute-done.8 = f32[16,4096]{1,0:T(8,128)} collective-permute-done((f32[16,4096]{1,0:T(8,128)}, f32[16,4096]{1,0:T(8,128)}, u32[]{:S(2)}, u32[]{:S(2)}) %collective-permute-start.8) | collective-permute-done | bytes 262176 | tf_op jit(solution)/shard_map/ppermute | solution.py:158
  49.9 1.8 add_select_fusion.2
  53.0 31.5 %collective-permute-done.9 = f32[16,4096]{1,0:T(8,128)} collective-permute-done((f32[16,4096]{1,0:T(8,128)}, f32[16,4096]{1,0:T(8,128)}, u32[]{:S(2)}, u32[]{:S(2)}) %collective-permute-start.9) | collective-permute-done | bytes 262176 | tf_op jit(solution)/shard_map/ppermute | solution.py:158
  84.4 2.0 add_select_fusion.refs_5_
  86.4 1.8 fusion.4
  88.3 1.5 slice.40
  95.3 1.6 copy-done.2
  96.9 1.9 copy-done.7
  98.8 1.9 copy-done.9
  102.7 15.2 %convolve.1.refs_1_ = bf16[32,384,128]{2,1,0:T(8,128)(2,1)S(1)} custom-call(bf16[384,4096]{1,0:T(8,128)(2,1)S(1)} %copy-done.9, bf16[384,4096]{1,0:T(8,128)(2,1)S(1)} %bitcast.12, f32[4096,2]{1,0:T(8,128)S(1)} %copy-done.2, f32[2,4096]{1,0:T(2,128)S(1)} %pad_maximum_fusion.10.refs_3_, f32[48,4096]{1,0:T(8,128)S(1)} %copy-done.13, f32[16,4096]{1,0:T(8,128)S(1)} %copy-done.11, ...), custom_call_target="tpu_custom_call" | custom-call | tf_op jit(solution)/shard_map/convolve/pallas_call | solution.py:133
  119.3 7.6 %collective-permute-done.10.refs_17_.refs_18_.refs_21_ = bf16[24,128,256]{2,1,0:T(8,128)(2,1)} collective-permute-done((bf16[24,128,256]{2,1,0:T(8,128)(2,1)}, bf16[24,128,256]{2,1,0:T(8,128)(2,1)}, u32[]{:S(2)}, u32[]{:S(2)}) %collective-permute-start.10) | collective-permute-done | bytes 1572896 | tf_op jit(solution)/shard_map/ppermute | solution.py:208
  132.5 3.1 %collective-permute-start.15 = (bf16[32,384,128]{2,1,0:T(8,128)(2,1)S(1)}, bf16[32,384,128]{2,1,0:T(8,128)(2,1)S(1)}, u32[]{:S(2)}, u32[]{:S(2)}) collective-permute-start(bf16[32,384,128]{2,1,0:T(8,128)(2,1)S(1)} %convolve.1.refs_1_), channel_id=1, source_target_pairs={{0,1},{1,0},{2,3},{3,2},{4,5},{5,4},{6,7},{7,6},{8,9},{9,8},{10,11... | collective-permute-start | bytes 9437192 | tf_op jit(solution)/shard_map/ppermute | solution.py:208
  137.2 34.4 %collective-permute-done.13.refs_25_.refs_26_.refs_29_ = bf16[24,128,256]{2,1,0:T(8,128)(2,1)S(1)} collective-permute-done((bf16[24,128,256]{2,1,0:T(8,128)(2,1)S(1)}, bf16[24,128,256]{2,1,0:T(8,128)(2,1)S(1)}, u32[]{:S(2)}, u32[]{:S(2)}) %collective-permute-start.13) | collective-permute-done | bytes 1572896 | tf_op jit(solution)/shard_map/ppermute | solution.py:208
  172.8 1.6 copy-done.18
  179.1 18.6 %project.2 = (f32[384,2048]{1,0:T(8,128)}, f32[384,2048]{1,0:T(8,128)}) custom-call(s32[28]{0:T(128)S(1)} %fusion.2.refs_0_, bf16[32,384,128]{2,1,0:T(8,128)(2,1)} %copy-done, bf16[32,384,128]{2,1,0:T(8,128)(2,1)} %copy-done.18, bf16[8,128,256]{2,1,0:T(8,128)(2,1)} %bitcast.1.refs_3_, bf16[8,128,256]{2,1,0:T(8,128)(2,1)} %collective-permute-done.refs_4_, ...), custom_call_target="tpu_custom_call" | custom-call | tf_op jit(solution)/shard_map/project/pallas_call | solution.py:193
  197.8 2.5 %collective-permute-done.16.refs_3_.refs_4_ = bf16[16,128,256]{2,1,0:T(8,128)(2,1)S(1)} collective-permute-done((bf16[16,128,256]{2,1,0:T(8,128)(2,1)}, bf16[16,128,256]{2,1,0:T(8,128)(2,1)S(1)}, u32[]{:S(2)}, u32[]{:S(2)}) %collective-permute-start.16) | collective-permute-done | bytes 1048608 | tf_op jit(solution)/shard_map/ppermute | solution.py:208
  201.3 10.3 %project.3 = (bf16[384,2048]{1,0:T(8,128)(2,1)S(1)}, bf16[384,2048]{1,0:T(8,128)(2,1)}) custom-call(s32[4]{0:T(128)S(1)} %xor_add_fusion.refs_0_, bf16[32,384,128]{2,1,0:T(8,128)(2,1)} %copy-done, bf16[32,384,128]{2,1,0:T(8,128)(2,1)} %copy-done.18, bf16[16,128,256]{2,1,0:T(8,128)(2,1)S(1)} %collective-permute-done.16.refs_3_.refs_4_, ...), custom_call_target="tpu_custom_call" | custom-call | tf_op jit(solution)/shard_map/project/pallas_call | solution.py:193
  212.8 2.4 %collective-permute-start.18 = (bf16[384,2048]{1,0:T(8,128)(2,1)}, bf16[384,2048]{1,0:T(8,128)(2,1)S(1)}, u32[]{:S(2)}, u32[]{:S(2)}) collective-permute-start(bf16[384,2048]{1,0:T(8,128)(2,1)} %get-tuple-element.118), channel_id=1, source_target_pairs={{0,1},{1,0},{2,3},{3,2},{4,5},{5,4},{6,7},{7,6},{8,9},{9,8},{10,11... | collective-permute-start | bytes 4718600 | tf_op jit(solution)/shard_map/ppermute | solution.py:208
  215.2 3.2 %collective-permute-done.18 = bf16[384,2048]{1,0:T(8,128)(2,1)S(1)} collective-permute-done((bf16[384,2048]{1,0:T(8,128)(2,1)}, bf16[384,2048]{1,0:T(8,128)(2,1)S(1)}, u32[]{:S(2)}, u32[]{:S(2)}) %collective-permute-start.18) | collective-permute-done | bytes 1572896 | tf_op jit(solution)/shard_map/ppermute | solution.py:208
  218.4 4.1 %maximum_select_fusion = bf16[1,384,4096]{2,1,0:T(8,128)(2,1)} fusion(bf16[1,384,2048]{2,1,0:T(8,128)(2,1)S(1)} %bitcast.16, bf16[1,384,2048]{2,1,0:T(8,128)(2,1)} %bitcast.13, pred[]{:T(512)S(6)} %eq.26), kind=kLoop, calls=%fused_computation | loop fusion | flops 14155776 | bytes 6291457 | tf_op jit(solution)/shard_map/jit(_where)/select_n | solution.py:305
  (115 shorter events, 34.9 us)
Async XLA Ops:
  2.0 2.1 collective-permute-start
  2.1 9.1 %copy-start.29 = (f32[256,16]{0,1:T(8,128)S(1)}, f32[256,16]{0,1:T(8,128)}, u32[]{:S(2)}) copy-start(f32[256,16]{0,1:T(8,128)} %param.15) | copy-start | bytes 49156
  2.1 9.4 %copy-start.28 = (f32[256,16]{0,1:T(8,128)S(1)}, f32[256,16]{0,1:T(8,128)}, u32[]{:S(2)}) copy-start(f32[256,16]{0,1:T(8,128)} %param.14) | copy-start | bytes 49156
  6.3 27.9 %collective-permute-start.3 = (bf16[16,128,256]{2,1,0:T(8,128)(2,1)}, bf16[16,128,256]{2,1,0:T(8,128)(2,1)S(1)}, u32[]{:S(2)}, u32[]{:S(2)}) collective-permute-start(bf16[16,128,256]{2,1,0:T(8,128)(2,1)} %pad_maximum_fusion.6), channel_id=1, source_target_pairs={{0,8},{1,9},{2,10},{3,11},{4,12},{5,13},{6,14},{7,15},{8,16},{9,17... | collective-permute-start | bytes 3145736 | tf_op jit(solution)/shard_map/ppermute | solution.py:212
  8.8 21.0 %collective-permute-start.1 = (bf16[8,128,256]{2,1,0:T(8,128)(2,1)}, bf16[8,128,256]{2,1,0:T(8,128)(2,1)}, u32[]{:S(2)}, u32[]{:S(2)}) collective-permute-start(bf16[8,128,256]{2,1,0:T(8,128)(2,1)} %bitcast.1.refs_3_), channel_id=1, source_target_pairs={{0,2},{1,3},{2,0},{3,1},{4,6},{5,7},{6,4},{7,5},{8,10},{9,11},{10,... | collective-permute-start | bytes 1572872 | tf_op jit(solution)/shard_map/ppermute | solution.py:208
  10.0 19.8 %collective-permute-start.2 = (bf16[8,128,256]{2,1,0:T(8,128)(2,1)}, bf16[8,128,256]{2,1,0:T(8,128)(2,1)}, u32[]{:S(2)}, u32[]{:S(2)}) collective-permute-start(bf16[8,128,256]{2,1,0:T(8,128)(2,1)} %collective-permute-done.refs_4_), channel_id=1, source_target_pairs={{0,4},{1,5},{2,6},{3,7},{4,0},{5,1},{6,2},{7,3},{8,12},{9,13},{10,... | collective-permute-start | bytes 1572872 | tf_op jit(solution)/shard_map/ppermute | solution.py:208
  12.4 5.2 %copy-start.1 = (f32[4096,2]{1,0:T(8,128)}, f32[4096,2]{1,0:T(8,128)S(1)}, u32[]{:S(2)}) copy-start(f32[4096,2]{1,0:T(8,128)S(1)} %copy.30.refs_2_) | copy-start | bytes 98308
  29.8 8.1 %copy-start.8 = (bf16[384,4096]{1,0:T(8,128)(2,1)}, bf16[384,4096]{1,0:T(8,128)(2,1)S(1)}, u32[]{:S(2)}) copy-start(bf16[384,4096]{1,0:T(8,128)(2,1)S(1)} %get-tuple-element.91.refs_0_) | copy-start | bytes 9437188
  29.8 8.1 %copy-start.12 = (f32[48,4096]{1,0:T(8,128)}, f32[48,4096]{1,0:T(8,128)S(1)}, u32[]{:S(2)}) copy-start(f32[48,4096]{1,0:T(8,128)S(1)} %get-tuple-element.92.refs_4_) | copy-start | bytes 2359300
  34.2 18.7 %copy-start.3 = (bf16[16,128,256]{2,1,0:T(8,128)(2,1)}, bf16[16,128,256]{2,1,0:T(8,128)(2,1)S(1)}, u32[]{:S(2)}) copy-start(bf16[16,128,256]{2,1,0:T(8,128)(2,1)S(1)} %collective-permute-done.3.refs_7_.refs_8_) | copy-start | bytes 3145732
  34.3 3.6 %copy-start.19 = (bf16[8,128,256]{2,1,0:T(8,128)(2,1)}, bf16[8,128,256]{2,1,0:T(8,128)(2,1)S(1)}, u32[]{:S(2)}) copy-start(bf16[8,128,256]{2,1,0:T(8,128)(2,1)S(1)} %get-tuple-element.123) | copy-start | bytes 1572868
  37.9 2.3 %collective-permute-start.7 = (f32[16,4096]{1,0:T(8,128)}, f32[16,4096]{1,0:T(8,128)S(1)}, u32[]{:S(2)}, u32[]{:S(2)}) collective-permute-start(f32[16,4096]{1,0:T(8,128)} %get-tuple-element.81), channel_id=1, source_target_pairs={{0,1},{1,0},{2,3},{3,2},{4,5},{5,4},{6,7},{7,6},{8,9},{9,8},{10,11... | collective-permute-start | bytes 786440 | tf_op jit(solution)/shard_map/ppermute | solution.py:158
  42.1 7.8 %collective-permute-start.8 = (f32[16,4096]{1,0:T(8,128)}, f32[16,4096]{1,0:T(8,128)}, u32[]{:S(2)}, u32[]{:S(2)}) collective-permute-start(f32[16,4096]{1,0:T(8,128)} %add_select_fusion.3), channel_id=1, source_target_pairs={{0,2},{1,3},{2,0},{3,1},{4,6},{5,7},{6,4},{7,5},{8,10},{9,11},{10,... | collective-permute-start | bytes 786440 | tf_op jit(solution)/shard_map/ppermute | solution.py:158
  43.3 43.1 %collective-permute-start.4 = (bf16[24,128,256]{2,1,0:T(8,128)(2,1)}, bf16[24,128,256]{2,1,0:T(8,128)(2,1)S(1)}, u32[]{:S(2)}, u32[]{:S(2)}) collective-permute-start(bf16[24,128,256]{2,1,0:T(8,128)(2,1)} %get-tuple-element.76), channel_id=1, source_target_pairs={{0,2},{1,3},{2,0},{3,1},{4,6},{5,7},{6,4},{7,5},{8,10},{9,11},{10,... | collective-permute-start | bytes 4718600 | tf_op jit(solution)/shard_map/ppermute | solution.py:208
  43.5 42.9 %collective-permute-start.5 = (bf16[24,128,256]{2,1,0:T(8,128)(2,1)}, bf16[24,128,256]{2,1,0:T(8,128)(2,1)}, u32[]{:S(2)}, u32[]{:S(2)}) collective-permute-start(bf16[24,128,256]{2,1,0:T(8,128)(2,1)} %get-tuple-element.77), channel_id=1, source_target_pairs={{0,4},{1,5},{2,6},{3,7},{4,0},{5,1},{6,2},{7,3},{8,12},{9,13},{10,... | collective-permute-start | bytes 4718600 | tf_op jit(solution)/shard_map/ppermute | solution.py:208
  51.7 32.7 %collective-permute-start.9 = (f32[16,4096]{1,0:T(8,128)}, f32[16,4096]{1,0:T(8,128)}, u32[]{:S(2)}, u32[]{:S(2)}) collective-permute-start(f32[16,4096]{1,0:T(8,128)} %add_select_fusion.2), channel_id=1, source_target_pairs={{0,4},{1,5},{2,6},{3,7},{4,0},{5,1},{6,2},{7,3},{8,12},{9,13},{10,... | collective-permute-start | bytes 786440 | tf_op jit(solution)/shard_map/ppermute | solution.py:158
  53.0 33.4 %collective-permute-start.6 = (bf16[16,128,256]{2,1,0:T(8,128)(2,1)S(1)}, bf16[16,128,256]{2,1,0:T(8,128)(2,1)}, u32[]{:S(2)}, u32[]{:S(2)}) collective-permute-start(bf16[16,128,256]{2,1,0:T(8,128)(2,1)S(1)} %collective-permute-done.3.refs_7_.refs_8_), channel_id=1, source_target_pairs={{0,8},{1,9},{2,10},{3,11},{4,12},{5,13},{6,14},{7,15},{8,16},{9,17... | collective-permute-start | bytes 3145736 | tf_op jit(solution)/shard_map/ppermute | solution.py:212
  91.2 3.9 %copy-start.26 = (f32[256,16]{1,0:T(8,128)S(1)}, f32[256,16]{1,0:T(8,128)}, u32[]{:S(2)}) copy-start(f32[256,16]{1,0:T(8,128)} %copy-done.25) | copy-start | bytes 49156
  91.2 4.1 %copy-start.14 = (f32[4096]{0:T(1024)S(1)}, f32[4096]{0:T(1024)}, u32[]{:S(2)}) copy-start(f32[4096]{0:T(1024)} %param.16) | copy-start | bytes 49156
  92.6 34.4 %collective-permute-start.10 = (bf16[24,128,256]{2,1,0:T(8,128)(2,1)}, bf16[24,128,256]{2,1,0:T(8,128)(2,1)}, u32[]{:S(2)}, u32[]{:S(2)}) collective-permute-start(bf16[24,128,256]{2,1,0:T(8,128)(2,1)} %pad_maximum_fusion.2), channel_id=1, source_target_pairs={{0,2},{1,3},{2,0},{3,1},{4,6},{5,7},{6,4},{7,5},{8,10},{9,11},{10,... | collective-permute-start | bytes 4718600 | tf_op jit(solution)/shard_map/ppermute | solution.py:208
  93.7 34.0 %collective-permute-start.11 = (bf16[24,128,256]{2,1,0:T(8,128)(2,1)}, bf16[24,128,256]{2,1,0:T(8,128)(2,1)}, u32[]{:S(2)}, u32[]{:S(2)}) collective-permute-start(bf16[24,128,256]{2,1,0:T(8,128)(2,1)} %pad_maximum_fusion.3), channel_id=1, source_target_pairs={{0,4},{1,5},{2,6},{3,7},{4,0},{5,1},{6,2},{7,3},{8,12},{9,13},{10,... | collective-permute-start | bytes 4718600 | tf_op jit(solution)/shard_map/ppermute | solution.py:208
  95.0 24.3 %collective-permute-start.12 = (bf16[16,128,256]{2,1,0:T(8,128)(2,1)}, bf16[16,128,256]{2,1,0:T(8,128)(2,1)}, u32[]{:S(2)}, u32[]{:S(2)}) collective-permute-start(bf16[16,128,256]{2,1,0:T(8,128)(2,1)} %collective-permute-done.6.refs_15_.refs_16_), channel_id=1, source_target_pairs={{0,8},{1,9},{2,10},{3,11},{4,12},{5,13},{6,14},{7,15},{8,16},{9,17... | collective-permute-start | bytes 3145736 | tf_op jit(solution)/shard_map/ppermute | solution.py:212
  118.0 14.5 %copy-start = (bf16[32,384,128]{2,1,0:T(8,128)(2,1)}, bf16[32,384,128]{2,1,0:T(8,128)(2,1)S(1)}, u32[]{:S(2)}) copy-start(bf16[32,384,128]{2,1,0:T(8,128)(2,1)S(1)} %convolve.1.refs_1_) | copy-start | bytes 9437188
  132.5 39.1 %collective-permute-start.15 = (bf16[32,384,128]{2,1,0:T(8,128)(2,1)S(1)}, bf16[32,384,128]{2,1,0:T(8,128)(2,1)S(1)}, u32[]{:S(2)}, u32[]{:S(2)}) collective-permute-start(bf16[32,384,128]{2,1,0:T(8,128)(2,1)S(1)} %convolve.1.refs_1_), channel_id=1, source_target_pairs={{0,1},{1,0},{2,3},{3,2},{4,5},{5,4},{6,7},{7,6},{8,9},{9,8},{10,11... | collective-permute-start | bytes 9437192 | tf_op jit(solution)/shard_map/ppermute | solution.py:208
  135.7 36.0 %collective-permute-start.13 = (bf16[24,128,256]{2,1,0:T(8,128)(2,1)S(1)}, bf16[24,128,256]{2,1,0:T(8,128)(2,1)S(1)}, u32[]{:S(2)}, u32[]{:S(2)}) collective-permute-start(bf16[24,128,256]{2,1,0:T(8,128)(2,1)S(1)} %pad_maximum_fusion.4), channel_id=1, source_target_pairs={{0,2},{1,3},{2,0},{3,1},{4,6},{5,7},{6,4},{7,5},{8,10},{9,11},{10,... | collective-permute-start | bytes 4718600 | tf_op jit(solution)/shard_map/ppermute | solution.py:208
  136.0 35.7 %collective-permute-start.14 = (bf16[24,128,256]{2,1,0:T(8,128)(2,1)S(1)}, bf16[24,128,256]{2,1,0:T(8,128)(2,1)S(1)}, u32[]{:S(2)}, u32[]{:S(2)}) collective-permute-start(bf16[24,128,256]{2,1,0:T(8,128)(2,1)S(1)} %pad_maximum_fusion.5), channel_id=1, source_target_pairs={{0,4},{1,5},{2,6},{3,7},{4,0},{5,1},{6,2},{7,3},{8,12},{9,13},{10,... | collective-permute-start | bytes 4718600 | tf_op jit(solution)/shard_map/ppermute | solution.py:208
  171.6 3.9 %copy-start.16 = (bf16[24,128,256]{2,1,0:T(8,128)(2,1)}, bf16[24,128,256]{2,1,0:T(8,128)(2,1)S(1)}, u32[]{:S(2)}) copy-start(bf16[24,128,256]{2,1,0:T(8,128)(2,1)S(1)} %collective-permute-done.13.refs_25_.refs_26_.refs_29_) | copy-start | bytes 4718596
  175.6 3.5 %copy-start.31 = (s32[28]{0:T(128)S(1)}, s32[28]{0:T(128)}, u32[]{:S(2)}) copy-start(s32[28]{0:T(128)} %constant.143.clone) | copy-start | bytes 340
  175.6 3.5 %copy-start.4 = (bf16[16,128,256]{2,1,0:T(8,128)(2,1)S(1)}, bf16[16,128,256]{2,1,0:T(8,128)(2,1)}, u32[]{:S(2)}) copy-start(bf16[16,128,256]{2,1,0:T(8,128)(2,1)} %copy-done.3) | copy-start | bytes 3145732
  176.7 23.6 %collective-permute-start.16 = (bf16[16,128,256]{2,1,0:T(8,128)(2,1)}, bf16[16,128,256]{2,1,0:T(8,128)(2,1)S(1)}, u32[]{:S(2)}, u32[]{:S(2)}) collective-permute-start(bf16[16,128,256]{2,1,0:T(8,128)(2,1)} %pad_maximum_fusion.7), channel_id=1, source_target_pairs={{0,2},{1,3},{2,0},{3,1},{4,6},{5,7},{6,4},{7,5},{8,10},{9,11},{10,... | collective-permute-start | bytes 3145736 | tf_op jit(solution)/shard_map/ppermute | solution.py:208
  177.9 23.4 %collective-permute-start.17 = (bf16[16,128,256]{2,1,0:T(8,128)(2,1)}, bf16[16,128,256]{2,1,0:T(8,128)(2,1)S(1)}, u32[]{:S(2)}, u32[]{:S(2)}) collective-permute-start(bf16[16,128,256]{2,1,0:T(8,128)(2,1)} %pad_maximum_fusion.8), channel_id=1, source_target_pairs={{0,4},{1,5},{2,6},{3,7},{4,0},{5,1},{6,2},{7,3},{8,12},{9,13},{10,... | collective-permute-start | bytes 3145736 | tf_op jit(solution)/shard_map/ppermute | solution.py:208
  212.8 5.6 %collective-permute-start.18 = (bf16[384,2048]{1,0:T(8,128)(2,1)}, bf16[384,2048]{1,0:T(8,128)(2,1)S(1)}, u32[]{:S(2)}, u32[]{:S(2)}) collective-permute-start(bf16[384,2048]{1,0:T(8,128)(2,1)} %get-tuple-element.118), channel_id=1, source_target_pairs={{0,1},{1,0},{2,3},{3,2},{4,5},{5,4},{6,7},{7,6},{8,9},{9,8},{10,11... | collective-permute-start | bytes 4718600 | tf_op jit(solution)/shard_map/ppermute | solution.py:208
  (21 other events, 41.5 us)
where the time goes:
time: 224 us; the launch traced here: 222 us
  waiting for transfers between devices  94.3 us (42%)
  Pallas kernels  52.7 us (24%)
  local copies, waits for them, and re-layouts  32.5 us (15%)
  starting transfers between devices  21.7 us (10%)
  other arithmetic  20.8 us (9%)
    ppermute x13, waiting for transfers between devices, swap(): return lax.ppermute(a, AXES, [(i, i ^ bit) for i in range(devices)])  50.6 us
    ppermute x3, waiting for transfers between devices, incoming_state(): other = lax.ppermute(total, 'ctx', [(i, i ^ width) for i in range(slabs)])  38 us
    pallas_call x2, Pallas kernels, project(): pl.pallas_call(lambda *refs: project_kernel(count, started, *refs), grid_...  29 us
    unnamed x71, local copies, waits for them, and re-layouts  19.3 us
    ppermute x13, starting transfers between devices, swap(): return lax.ppermute(a, AXES, [(i, i ^ bit) for i in range(devices)])  15.9 us
    pallas_call x1, Pallas kernels, convolve(): pl.pallas_call(lambda *refs: conv_kernel(members, poles, blocks, *refs),...  15.2 us
    pallas_call x1, Pallas kernels, states(): pl.pallas_call(lambda *refs: state_kernel(members, poles, blocks, *refs),...  8.49 us
    concatenate x4, other arithmetic, local(): pay_x = jnp.concatenate(pay_x, axis=0)  6.15 us
  transfers between devices with their start and end apart: 19, of which 12 were waited for; matrix products, arithmetic and copies ran while one was open for 5% of the time, Pallas kernels for 19%

commit v1 on v0

--- a/solution.py
+++ b/solution.py
@@ -8,7 +8,8 @@
 
 BLOCK = 128
 LANES = 128
-COLS = 256
+COLS = 512
+SCALE = 4
 F32 = jnp.float32
 BF16 = jnp.bfloat16
 AXES = ("dp", "ctx")
@@ -19,9 +20,17 @@
     return pltpu.CompilerParams(vmem_limit_bytes=mib << 20, dimension_semantics=("arbitrary",))
 
 
+def cost(flops, moved):
+    return pl.CostEstimate(flops=int(flops), transcendentals=0, bytes_accessed=int(moved))
+
+
 def split(a):
     high = a.astype(BF16)
     return high, (a - high.astype(F32)).astype(BF16)
+
+
+def in_hbm(a):
+    return pltpu.with_memory_space_constraint(a, pltpu.HBM)
 
 
 def iota(shape, axis):
@@ -120,8 +129,9 @@
             jax.ShapeDtypeStruct((poles, width), F32),
         ],
         compiler_params=params(32),
+        cost_estimate=cost(4 * poles * members * rows * width * SCALE, 6 * rows * width),
         name="states",
-    )(key, value, col, lane)
+    )(in_hbm(key), in_hbm(value), col, lane)
 
 
 def convolve(driven, query, col, row, block_state, incoming, lane, skip, members, poles):
@@ -146,70 +156,98 @@
         out_specs=pl.BlockSpec((step // LANES, rows, LANES), lambda i: (i, 0, 0)),
         out_shape=jax.ShapeDtypeStruct((width // LANES, rows, LANES), BF16),
         compiler_params=params(32),
+        cost_estimate=cost(2 * (BLOCK * LANES // members + 3 * LANES) * rows * width * SCALE, 6 * rows * width),
         name="convolve",
-    )(driven, query, col, row, block_state, incoming, lane, skip)
-
-
-def incoming_state(total, lane, rows, slabs):
+    )(in_hbm(driven), in_hbm(query), col, row, block_state, incoming, lane, skip)
+
+
+def scan_send(total, slabs, width):
+    return lax.ppermute(total, "ctx", [(i, i ^ width) for i in range(slabs)])
+
+
+def pair_total(slab, other, lane, rows, core):
+    decay = jnp.exp(-lane * float(rows))
+    total = jnp.where(core == 0, slab * decay + other, other * decay + slab)
+    half = slab.shape[1] // 2
+    return [lax.dynamic_slice_in_dim(a, core * half, half, 1) for a in (total, lane)]
+
+
+def scan_step(before, total, other, lane, rows, width):
     place = lax.axis_index("ctx")
-    before = jnp.zeros_like(total)
-    width = 1
-    while width < slabs:
-        other = lax.ppermute(total, "ctx", [(i, i ^ width) for i in range(slabs)])
-        upper = (place // width) % 2 == 1
-        offset = (place % width).astype(F32) * rows
-        before = jnp.where(upper, before + other * jnp.exp(-lane * offset), before)
-        decay = jnp.exp(-lane * float(rows * width))
-        total = jnp.where(upper, other * decay + total, total * decay + other)
-        width *= 2
-    return before
-
-
-def project_kernel(count, started, idx_ref, own_ref, peer_ref, *refs):
-    pieces, refs = refs[:count], refs[count:]
-    sums = None
-    if started:
-        sums = [refs[0][...], refs[1][...]]
-        refs = refs[2:]
-    for p in range(0, count, 2):
-        weight = jnp.concatenate([pieces[p][0], pieces[p + 1][0]], axis=0)
-        first, second = idx_ref[p], idx_ref[p + 1]
-        parts = []
-        for g_ref in (own_ref, peer_ref):
-            gated = jnp.concatenate([g_ref[first], g_ref[second]], axis=1)
-            parts.append(jnp.dot(gated, weight, preferred_element_type=F32))
-        sums = parts if sums is None else [a + b for a, b in zip(sums, parts)]
-    for o_ref, s in zip(refs, sums):
-        o_ref[...] = s.astype(o_ref.dtype)
-
-
-def project(idx, own, peer, pieces, wide, sums=None, dtype=F32):
-    shards, rows, depth = own.shape
-    count = len(pieces)
-    whole = pl.BlockSpec((shards, rows, depth), lambda b, i: (0, 0, 0), pipeline_mode=pl.Buffered(1))
+    upper = (place // width) % 2 == 1
+    offset = ((place % width) // 2 * 2).astype(F32) * rows
+    before = jnp.where(upper, before + other * jnp.exp(-lane * offset), before)
+    decay = jnp.exp(-lane * float(rows * width))
+    return before, jnp.where(upper, other * decay + total, total * decay + other)
+
+
+def incoming_state(before, other_half, other_slab, lane, rows, core):
+    ahead = jnp.where(
+        core == 0,
+        jnp.concatenate([before, other_half], axis=1),
+        jnp.concatenate([other_half, before], axis=1),
+    )
+    return jnp.where(core == 0, ahead, ahead * jnp.exp(-lane * float(rows)) + other_slab)
+
+
+def project_kernel(sizes, sides, started, idx_ref, *refs):
+    shards = sum(sizes) // LANES
+    gated = [refs[i * shards : (i + 1) * shards] for i in range(sides)]
+    refs = refs[sides * shards :]
+    weights, refs = refs[: len(sizes)], refs[len(sizes) :]
+    totals = [r[...] for r in refs[:sides]] if started else [None] * sides
+    outs = refs[-sides:]
+    weights, at = list(weights), 0
+    while weights:
+        depth, rhs = 0, []
+        while weights and depth + weights[0].shape[0] <= 2 * LANES:
+            rhs.append(weights.pop(0)[...])
+            depth += rhs[-1].shape[0]
+        rhs = jnp.concatenate(rhs, axis=0) if len(rhs) > 1 else rhs[0]
+        for i in range(sides):
+            lhs = [r[0] for r in gated[i][at : at + depth // LANES]]
+            lhs = jnp.concatenate(lhs, axis=1) if len(lhs) > 1 else lhs[0]
+            part = jnp.dot(lhs, rhs, preferred_element_type=F32)
+            totals[i] = part if totals[i] is None else totals[i] + part
+        at += depth // LANES
+    for o_ref, total in zip(outs, totals):
+        o_ref[...] = total.astype(o_ref.dtype)
+
+
+def project(place, ring, gated, pieces, wide, total=None, side=None, dout=None, dtype=F32):
+    shards, rows, depth = gated[0].shape
+    steps = [one for _, _, owners in pieces for one in owners]
+    sizes = [LANES * len(owners) for _, _, owners in pieces]
+    sides = len(gated)
+    nb = wide // COLS
+    idx = shard_table(place, ring, steps)
+    if side is not None:
+        idx = jnp.concatenate([idx, (side * nb).astype(jnp.int32)[None]])
     block = pl.BlockSpec((rows, COLS), lambda b, i: (0, b))
-    specs = [pl.BlockSpec((1, depth, COLS), lambda b, i, s=s: (s + b, 0, 0)) for _, s in pieces]
-    started = sums is not None
+    specs = [pl.BlockSpec((1, rows, depth), lambda b, i, p=p: (i[p], 0, 0)) for p in range(len(steps))] * sides
+    specs += [
+        pl.BlockSpec((size, COLS), lambda b, i, at=at: (at, b)) for size, (_, at, _) in zip(sizes, pieces)
+    ]
+    operands = [g for g in gated for _ in steps] + [a for a, _, _ in pieces]
+    if total is not None:
+        specs += [block] * sides
+        operands += list(total)
+    operands = [in_hbm(a) for a in operands]
+    last = len(steps)
+    shape = jax.ShapeDtypeStruct((rows, wide if side is None else dout), dtype)
     return pl.pallas_call(
-        lambda *refs: project_kernel(count, started, *refs),
+        lambda *refs: project_kernel(sizes, sides, total is not None, *refs),
         grid_spec=pltpu.PrefetchScalarGridSpec(
             num_scalar_prefetch=1,
-            grid=(wide // COLS,),
-            in_specs=[whole, whole] + specs + [block] * (2 * started),
-            out_specs=[block, block],
+            grid=(nb,),
+            in_specs=specs,
+            out_specs=[block if side is None else pl.BlockSpec((rows, COLS), lambda b, i: (0, i[last] + b))] * sides,
         ),
-        out_shape=[jax.ShapeDtypeStruct((rows, wide), dtype)] * 2,
+        out_shape=[shape] * sides,
         compiler_params=params(48),
+        cost_estimate=cost(2 * len(steps) * LANES * sides * rows * wide * SCALE, 4 * sides * rows * wide),
         name="project",
-    )(idx, own, peer, *[a for a, _ in pieces], *(sums or ()))
-
-
-def swap(a, devices, bit):
-    return lax.ppermute(a, AXES, [(i, i ^ bit) for i in range(devices)])
-
-
-def ahead(a, devices):
-    return lax.ppermute(a, AXES, [(i, (i + 8) % devices) for i in range(devices)])
+    )(idx, *operands)
 
 
 def local(mesh_shape, query_stream, key_stream, value_stream, pole_rate, residue, skip_gain, out_weight):
@@ -220,94 +258,135 @@
     devices = mesh_shape["dp"] * slabs
     depth, dout = out_weight.shape
     query, key, value = [a.reshape(rows, width) for a in (query_stream, key_stream, value_stream)]
-    col = jnp.stack([pole_rate.reshape(-1), residue.reshape(-1)], axis=1)
-    row = jnp.stack([pole_rate.reshape(-1), residue.reshape(-1)], axis=0)
-    lane = jnp.repeat(pole_rate.T, members, axis=1)
     skip = skip_gain[None]
 
     if depth != LANES:
+        core = lax.axis_index("ctx") % 2
+        col, row, lane = tables(pole_rate, residue, members)
         driven, block_state, slab = states(key, value, col, lane, members, poles)
-        incoming = incoming_state(slab, lane, rows, slabs)
+        other_slab = scan_send(slab, slabs, 1)
+        total, lane_half = pair_total(slab, other_slab, lane, rows, core)
+        before = jnp.zeros_like(total)
+        step = 2
+        while step < slabs:
+            other = scan_send(total, slabs, step)
+            before, total = scan_step(before, total, other, lane_half, rows, step)
+            step *= 2
+        incoming = incoming_state(before, scan_send(before, slabs, 1), other_slab, lane, rows, core)
         gated = convolve(driven, query, col, row, block_state, incoming, lane, skip, members, poles)
         weight = lax.all_gather(out_weight, AXES, axis=0, tiled=True)
         flat = gated.transpose(1, 0, 2).reshape(rows, width)
         out = jnp.dot(flat, weight, preferred_element_type=F32)
         return out.astype(BF16).reshape(seqs, rows, dout)
 
+    def swap(a, bit):
+        return lax.ppermute(a, AXES, [(i, i ^ bit) for i in range(devices)])
+
+    def ahead(a):
+        return lax.ppermute(a, AXES, [(i, (i + 8) % devices) for i in range(devices)])
+
     place = lax.axis_index(AXES)
     core = place % 2
     half = dout // 2
-    nb = half // COLS
     ring = devices // 8
-    tiles = out_weight.reshape(depth, 2 * nb, COLS).transpose(1, 0, 2)
-    mine = lax.dynamic_slice_in_dim(tiles, core * nb, nb, 0)
-    give = lax.dynamic_slice_in_dim(tiles, (1 - core) * nb, nb, 0)
-    got = swap(give, devices, 1)
-
-    pieces = [(mine, 0, (0, 0, 0, 0)), (got, 0, (0, 0, 0, 1))]
-    late = []
-    cur = (mine, got)
-    prev = None
-    work = (key, value)
-    for r in range(ring + 1):
-        pay_x, pay_y = [], []
-        if prev is not None:
-            (a, ax), (b, by) = prev
-            pay_x += [b, by]
-            pay_y += [a, ax]
-        if r < ring:
-            pay_x.append(cur[0])
-            pay_y.append(cur[1])
-        pay_x = jnp.concatenate(pay_x, axis=0)
-        pay_y = jnp.concatenate(pay_y, axis=0)
-        pay_z = jnp.concatenate(cur, axis=0) if r + 1 < ring else None
-        pay_x, pay_y, pay_z, work = fence((pay_x, pay_y, pay_z, work))
-        new_z = ahead(pay_z, devices) if pay_z is not None else None
-        new_x = swap(pay_x, devices, 2)
-        new_y = swap(pay_y, devices, 4)
-        if r == 0:
-            work = states(*work, col, lane, members, poles)
-        elif r == 1:
-            driven, block_state, slab = work
-            work = (driven, block_state, incoming_state(slab, lane, rows, slabs))
-        elif r == 2:
-            driven, block_state, incoming = work
-            work = convolve(driven, query, col, row, block_state, incoming, lane, skip, members, poles)
-        elif r == ring - 1:
-            own = work
-            work = (own, swap(own, devices, 1))
-        elif r == ring:
-            table = [p for p in pieces]
-            idx = shard_table(place, ring, [p[2] for p in table])
-            work = (work, project(idx, *work, [p[:2] for p in table], half))
-        new_x, new_y, new_z, work = fence((new_x, new_y, new_z, work))
-        at = 0
-        if prev is not None:
-            late = [
-                (new_x, 0, (r - 1, 0, 1, 1)),
-                (new_x, nb, (r - 1, 1, 1, 1)),
-                (new_y, 0, (r - 1, 1, 0, 0)),
-                (new_y, nb, (r - 1, 1, 1, 0)),
-            ]
-            if r < ring:
-                pieces += late
-            at = 2 * nb
-        if r < ring:
-            pieces += [(new_x, at, (r, 0, 1, 0)), (new_y, at, (r, 1, 0, 1))]
-            prev = ((cur[0], new_x[at:]), (cur[1], new_y[at:]))
-        if new_z is not None:
-            pieces += [(new_z, 0, (r + 1, 0, 0, 0)), (new_z, nb, (r + 1, 0, 0, 1))]
-            cur = (new_z[:nb], new_z[nb:])
-    (own, peer), sums = work
-    idx = shard_table(place, ring, [p[2] for p in late])
-    out_own, out_peer = project(idx, own, peer, [p[:2] for p in late], half, sums, BF16)
-    other = swap(out_peer, devices, 1)
-    out = jnp.where(
-        core == 0,
-        jnp.concatenate([out_own, other], axis=1),
-        jnp.concatenate([other, out_own], axis=1),
-    )
-    return out.reshape(seqs, rows, dout)
+    mine = lax.dynamic_slice_in_dim(out_weight, core * half, half, 1)
+    give = lax.dynamic_slice_in_dim(out_weight, (1 - core) * half, half, 1)
+
+    got = swap(give, 1)
+    cur = jnp.concatenate([mine, got], axis=0)
+    both = [(0, 0, 0, 0), (0, 0, 0, 1)]
+    pieces = [(cur, 0, both)]
+
+    def straight(cur, back, last):
+        new = [swap(cur, 2), swap(cur, 4)] + ([] if last else [ahead(cur)])
+        owners = [[(back + dz, dy, dx, k) for k in (0, 1)] for dz, dy, dx in ((0, 0, 1), (0, 1, 0), (1, 0, 0))]
+        return [(a, 0, o) for a, o in zip(new, owners)]
+
+    def diagonal(over_x, over_y, back):
+        return [(swap(over_y, 4), 0, [(back, 1, 1, 0)]), (swap(over_x, 2), 0, [(back, 1, 1, 1)])]
+
+    def over(new):
+        return new[1][0][depth:], new[0][0][:depth]
+
+    def settle(new, work):
+        arrays, work = fence(([a for a, _, _ in new], work))
+        return [(a, at, o) for a, (_, at, o) in zip(arrays, new)], work
+
+    cur, pole_rate, residue, key, value = fence((cur, pole_rate, residue, key, value))
+    col, row, lane = tables(pole_rate, residue, members)
+    new = straight(cur, 0, False)
+    driven, block_state, slab = states(key, value, col, lane, members, poles)
+    new, (driven, block_state, slab, lane) = settle(new, (driven, block_state, slab, lane))
+    pieces += new
+    cur = new[2][0]
+    new = diagonal(*over(new), 0)
+    other_slab = scan_send(slab, slabs, 1)
+    total, lane_half = pair_total(slab, other_slab, lane, rows, core)
+    other = scan_send(total, slabs, 2)
+    before, total = scan_step(jnp.zeros_like(total), total, other, lane_half, rows, 2)
+    new, (before, total, other_slab, lane_half, cur) = settle(new, (before, total, other_slab, lane_half, cur))
+    pieces += new
+    other = scan_send(total, slabs, 4)
+    before, _ = scan_step(before, total, other, lane_half, rows, 4)
+    new = straight(cur, 1, False)
+    other_half = scan_send(before, slabs, 1)
+    new, (before, other_half) = settle(new, (before, other_half))
+    pieces += new
+    back = 2
+    gated = None
+    while back < ring - 1:
+        done = diagonal(*over(new), back - 1)
+        new = done + straight(new[2][0], back, False)
+        if gated is None:
+            incoming = incoming_state(before, other_half, other_slab, lane, rows, core)
+            gated = convolve(driven, query, col, row, block_state, incoming, lane, skip, members, poles)
+        new, gated = settle(new, gated)
+        pieces += new
+        new = new[2:]
+        back += 1
+    cur = new[2][0]
+    new = diagonal(*over(new), back - 1)
+    peer = swap(gated, 1)
+    new, (gated, peer, cur) = settle(new, (gated, peer, cur))
+    pieces += new
+    new = straight(cur, back, True)
+    sums = project(place, ring, (gated, peer), pieces, half)
+    new, (gated, peer, sums) = settle(new, (gated, peer, sums))
+    late = diagonal(*over(new), back)
+    sums = project(place, ring, (gated, peer), new, half, sums)
+    late, (gated, peer, (sum_own, sum_peer)) = settle(late, (gated, peer, sums))
+    (out_peer,) = project(place, ring, [peer], late, half, [sum_peer], dtype=BF16)
+    other = swap(out_peer, 1)
+    (out,) = project(place, ring, [gated], late, half, [sum_own], core, dout, dtype=BF16)
+    return put(other, 1 - core, out).reshape(seqs, rows, dout)
+
+
+def put_kernel(side_ref, half_ref, whole_ref, o_ref):
+    o_ref[...] = half_ref[...]
+
+
+def put(half, side, whole):
+    rows, wide = half.shape
+    nb = wide // COLS
+    return pl.pallas_call(
+        put_kernel,
+        grid_spec=pltpu.PrefetchScalarGridSpec(
+            num_scalar_prefetch=1,
+            grid=(nb,),
+            in_specs=[pl.BlockSpec((rows, COLS), lambda b, i: (0, b)), pl.BlockSpec(memory_space=pl.ANY)],
+            out_specs=pl.BlockSpec((rows, COLS), lambda b, i: (0, i[0] * nb + b)),
+        ),
+        out_shape=jax.ShapeDtypeStruct(whole.shape, whole.dtype),
+        input_output_aliases={2: 0},
+        compiler_params=params(32),
+        name="put",
+    )(side.astype(jnp.int32)[None], half, whole)
+
+
+def tables(pole_rate, residue, members):
+    col = jnp.stack([pole_rate.reshape(-1), residue.reshape(-1)], axis=1)
+    row = jnp.stack([pole_rate.reshape(-1), residue.reshape(-1)], axis=0)
+    return col, row, jnp.repeat(pole_rate.T, members, axis=1)
 
 
 def shard_table(place, ring, steps):

time: 224 us -> 195 us (0.87)
  waiting for transfers between devices: 94.3 us -> 67 us
  other arithmetic: 20.8 us -> 5.39 us
  Pallas kernels: 52.7 us -> 64.9 us
  starting transfers between devices: 21.7 us -> 29.8 us
  local copies, waits for them, and re-layouts: 32.5 us -> 26.3 us
    ppermute x3 -> x4, waiting for transfers between devices: 38 us -> 23.3 us  [scan_send(): return lax.ppermute(total, 'ctx', [(i, i ^ width) for i in range(slabs)])]
    concatenate x8 -> x2, other arithmetic: 11 us -> 1.12 us  [the longest x1 1.04 us: local(): cur = jnp.concatenate([mine, got], axis=0)]
    ppermute x13 -> x19, waiting for transfers between devices: 50.6 us -> 40.8 us  [swap(): return lax.ppermute(a, AXES, [(i, i ^ bit) for i in range(devices)])]
    unnamed x71 -> x54, local copies, waits for them, and re-layouts: 19.3 us -> 11 us
    pallas_call x2 -> x5, Pallas kernels: 29 us -> 36.9 us  [the longest x4 35.1 us: project(): pl.pallas_call(lambda *refs: project_kernel(sizes, sides, total is not No...]
    select_n x4 -> x5, other arithmetic: 9.7 us -> 3.41 us  [the longest x2 1.68 us: scan_step(): before = jnp.where(upper, before + other * jnp.exp(-lane * offset), before)]
    ppermute x3 -> x4, starting transfers between devices: 3.4 us -> 7 us  [scan_send(): return lax.ppermute(total, 'ctx', [(i, i ^ width) for i in range(slabs)])]
    pallas_call x1, Pallas kernels: 8.49 us -> 11.7 us  [states(): pl.pallas_call(lambda *refs: state_kernel(members, poles, blocks, *refs),...]
  transfers between devices with their start and end apart: 19 -> 26, of which waited for: 12 -> 15; matrix products, arithmetic and copies ran while one was open for 5% -> 9% of each run, Pallas kernels for 19% -> 30%
where the time goes in v1:
time: 195 us; the launch traced here: 194 us
  waiting for transfers between devices  67 us (34%)
  Pallas kernels  64.9 us (33%)
  starting transfers between devices  29.8 us (15%)
  local copies, waits for them, and re-layouts  26.3 us (13%)
  other arithmetic  5.39 us (3%)
    ppermute x19, waiting for transfers between devices, swap(): return lax.ppermute(a, AXES, [(i, i ^ bit) for i in range(devices)])  40.8 us
    pallas_call x4, Pallas kernels, project(): pl.pallas_call(lambda *refs: project_kernel(sizes, sides, total is not No...  35.1 us
    ppermute x4, waiting for transfers between devices, scan_send(): return lax.ppermute(total, 'ctx', [(i, i ^ width) for i in range(slabs)])  23.3 us
    ppermute x19, starting transfers between devices, swap(): return lax.ppermute(a, AXES, [(i, i ^ bit) for i in range(devices)])  17.7 us
    pallas_call x1, Pallas kernels, convolve(): pl.pallas_call(lambda *refs: conv_kernel(members, poles, blocks, *refs),...  16.4 us
    pallas_call x1, Pallas kernels, states(): pl.pallas_call(lambda *refs: state_kernel(members, poles, blocks, *refs),...  11.7 us
    unnamed x54, local copies, waits for them, and re-layouts  11 us
    ppermute x4, starting transfers between devices, scan_send(): return lax.ppermute(total, 'ctx', [(i, i ^ width) for i in range(slabs)])  7 us
  transfers between devices with their start and end apart: 26, of which 15 were waited for; matrix products, arithmetic and copies ran while one was open for 9% of the time, Pallas kernels for 30%

profile of v1, /device:TPU:1, one launch (start us, length us, event | category | flops | bytes accessed | tf_op | source)
XLA Modules:
  0.0 193.7 jit_solution(2524215048769933284)
XLA Ops:
  0.0 1.3 constant_dynamic-slice_fusion.2
  1.4 1.9 collective-permute-done
  4.3 2.4 %collective-permute-start.3 = (bf16[256,2048]{1,0:T(8,128)(2,1)}, bf16[256,2048]{1,0:T(8,128)(2,1)}, u32[]{:S(2)}, u32[]{:S(2)}) collective-permute-start(bf16[256,2048]{1,0:T(8,128)(2,1)} %pad_maximum_fusion.refs_53_), channel_id=1, source_target_pairs={{0,8},{1,9},{2,10},{3,11},{4,12},{5,13},{6,14},{7,15},{8,16},{9,17... | collective-permute-start | bytes 3145736 | tf_op jit(solution)/shard_map/ppermute | solution.py:286
  10.9 2.0 %broadcast_in_dim.16 = f32[16,256,16]{2,1,0:T(8,128)} broadcast(f32[16,256]{1,0:T(8,128)S(1)} %bitcast.9), dimensions={0,1} | broadcast | bytes 278528 | tf_op jit(solution)/shard_map/broadcast_in_dim | solution.py:389
  12.9 3.1 %reshape.17.refs_3_.refs_6_ = f32[16,4096]{1,0:T(8,128)S(1)} reshape(f32[16,256,16]{2,1,0:T(8,128)} %broadcast_in_dim.16) | data formatting | bytes 524288 | tf_op jit(solution)/shard_map/reshape | solution.py:389
  16.0 11.7 %states.1 = (bf16[384,4096]{1,0:T(8,128)(2,1)S(1)}, f32[48,4096]{1,0:T(8,128)S(1)}, f32[16,4096]{1,0:T(8,128)S(1)}) custom-call(bf16[384,4096]{1,0:T(8,128)(2,1)} %bitcast.10, bf16[384,4096]{1,0:T(8,128)(2,1)} %bitcast.11, f32[4096,2]{1,0:T(8,128)S(1)} %copy.29.refs_2_, f32[16,4096]{1,0:T(8,128)S(1)} %reshape.17.refs_3_.refs_6_), custom_call_target="tpu_custom_call" | custom-call | flops 6442450944 | bytes 9437184 | tf_op jit(solution)/shard_map/states/pallas_call | solution.py:112
  27.7 1.7 copy-done.6
  29.4 2.9 %collective-permute-done.3.refs_56_ = bf16[256,2048]{1,0:T(8,128)(2,1)} collective-permute-done((bf16[256,2048]{1,0:T(8,128)(2,1)}, bf16[256,2048]{1,0:T(8,128)(2,1)}, u32[]{:S(2)}, u32[]{:S(2)}) %collective-permute-start.3) | collective-permute-done | bytes 1048608 | tf_op jit(solution)/shard_map/ppermute | solution.py:286
  32.3 1.6 collective-permute-start.6
  41.8 10.2 %collective-permute-done.5.refs_58_ = bf16[128,2048]{1,0:T(8,128)(2,1)S(1)} collective-permute-done((bf16[128,2048]{1,0:T(8,128)(2,1)S(1)}, bf16[128,2048]{1,0:T(8,128)(2,1)S(1)}, u32[]{:S(2)}, u32[]{:S(2)}) %collective-permute-start.5) | collective-permute-done | bytes 524320 | tf_op jit(solution)/shard_map/ppermute | solution.py:283
  52.0 1.3 collective-permute-start.10
  54.7 1.2 collective-permute-start.11
  57.6 21.5 %collective-permute-done.11 = f32[16,2048]{1,0:T(8,128)} collective-permute-done((f32[16,2048]{1,0:T(8,128)}, f32[16,2048]{1,0:T(8,128)}, u32[]{:S(2)}, u32[]{:S(2)}) %collective-permute-start.11) | collective-permute-done | bytes 131104 | tf_op jit(solution)/shard_map/ppermute | solution.py:165
  80.1 3.0 %collective-permute-start.12 = (f32[16,2048]{1,0:T(8,128)S(1)}, f32[16,2048]{1,0:T(8,128)S(1)}, u32[]{:S(2)}, u32[]{:S(2)}) collective-permute-start(f32[16,2048]{1,0:T(8,128)S(1)} %add_select_fusion.1), channel_id=1, source_target_pairs={{0,1},{1,0},{2,3},{3,2},{4,5},{5,4},{6,7},{7,6},{8,9},{9,8},{10,11... | collective-permute-start | bytes 393224 | tf_op jit(solution)/shard_map/ppermute | solution.py:165
  84.1 1.3 collective-permute-start.17
  89.6 1.6 copy-done.4
  92.4 16.4 %convolve.1.refs_1_.refs_2_.refs_3_.refs_4_.refs_5_.refs_6_.refs_7_.refs_8_.refs_9_.refs_10_.refs_11_.refs_12_.refs_13_.refs_14_.refs_15_.refs_16_.refs_17_.refs_18_.refs_19_.refs_20_.refs_21_.refs_22_.refs_23_.refs_24_.refs_25_.refs_26_ = bf16[32,384,128]{2,1,0:T(8,128)(2,1)S(1)} custom-call(bf16[384,4096]{1,0:T(8,128)(2,1)} %copy-done.6, ...), custom_call_target="tpu_custom_call" | custom-call | flops 17716740096 | bytes 9437184 | tf_op jit(solution)/shard_map/convolve/pallas_call | solution.py:143
  108.7 12.2 %collective-permute-done.14.refs_63_ = bf16[128,2048]{1,0:T(8,128)(2,1)S(1)} collective-permute-done((bf16[128,2048]{1,0:T(8,128)(2,1)S(1)}, bf16[128,2048]{1,0:T(8,128)(2,1)S(1)}, u32[]{:S(2)}, u32[]{:S(2)}) %collective-permute-start.14) | collective-permute-done | bytes 524320 | tf_op jit(solution)/shard_map/ppermute | solution.py:283
  121.9 1.8 collective-permute-start.20
  123.7 1.9 slice.28
  125.6 1.9 slice.29
  129.9 11.5 %collective-permute-done.19.refs_68_ = bf16[128,2048]{1,0:T(8,128)(2,1)} collective-permute-done((bf16[128,2048]{1,0:T(8,128)(2,1)}, bf16[128,2048]{1,0:T(8,128)(2,1)}, u32[]{:S(2)}, u32[]{:S(2)}) %collective-permute-start.19) | collective-permute-done | bytes 524320 | tf_op jit(solution)/shard_map/ppermute | solution.py:283
  142.1 1.2 collective-permute-start.22
  143.7 18.3 %project.4 = (f32[384,2048]{1,0:T(8,128)S(1)}, f32[384,2048]{1,0:T(8,128)}) custom-call(s32[26]{0:T(128)S(1)} %fusion.2.refs_0_, bf16[32,384,128]{2,1,0:T(8,128)(2,1)} %copy-done, bf16[32,384,128]{2,1,0:T(8,128)(2,1)} %copy-done, bf16[32,384,128]{2,1,0:T(8,128)(2,1)} %copy-done, bf16[32,384,128]{2,1,0:T(8,128)(2,1)} %copy-done, ...), custom_call_target="tpu_custom_call" | custom-call | flops 41875931136 | bytes 6291456 | tf_op jit(solution)/shard_map/project/pallas_call | solution.py:238
  162.1 1.7 copy-done.1
  163.8 2.1 %collective-permute-done.22.refs_10_ = bf16[256,2048]{1,0:T(8,128)(2,1)S(1)} collective-permute-done((bf16[256,2048]{1,0:T(8,128)(2,1)}, bf16[256,2048]{1,0:T(8,128)(2,1)S(1)}, u32[]{:S(2)}, u32[]{:S(2)}) %collective-permute-start.22) | collective-permute-done | bytes 1048608 | tf_op jit(solution)/shard_map/ppermute | solution.py:283
  167.8 7.4 %project.5 = (f32[384,2048]{1,0:T(8,128)S(1)}, f32[384,2048]{1,0:T(8,128)}) custom-call(s32[4]{0:T(128)S(1)} %xor_add_fusion.refs_0_, bf16[32,384,128]{2,1,0:T(8,128)(2,1)} %copy-done, bf16[32,384,128]{2,1,0:T(8,128)(2,1)} %copy-done, bf16[32,384,128]{2,1,0:T(8,128)(2,1)} %copy-done, bf16[32,384,128]{2,1,0:T(8,128)(2,1)} %copy-done, ...), custom_call_target="tpu_custom_call" | custom-call | flops 6442450944 | bytes 6291456 | tf_op jit(solution)/shard_map/project/pallas_call | solution.py:238
  175.2 1.7 copy-done.2
  179.1 4.1 %project.6 = bf16[384,2048]{1,0:T(8,128)(2,1)S(1)} custom-call(s32[2]{0:T(128)S(1)} %xor_add_fusion.1.refs_0_, ...), custom_call_target="tpu_custom_call" | custom-call | flops 1610612736 | bytes 3145728 | tf_op jit(solution)/shard_map/project/pallas_call | solution.py:238
  183.2 3.4 %collective-permute-start.25 = (bf16[384,2048]{1,0:T(8,128)(2,1)S(1)}, bf16[384,2048]{1,0:T(8,128)(2,1)S(1)}, u32[]{:S(2)}, u32[]{:S(2)}) collective-permute-start(bf16[384,2048]{1,0:T(8,128)(2,1)S(1)} %project.6), channel_id=1, source_target_pairs={{0,1},{1,0},{2,3},{3,2},{4,5},{5,4},{6,7},{7,6},{8,9},{9,8},{10,11... | collective-permute-start | bytes 4718600 | tf_op jit(solution)/shard_map/ppermute | solution.py:283
  186.7 5.2 %project.7.whole_ref = bf16[384,4096]{1,0:T(8,128)(2,1)} custom-call(s32[3]{0:T(128)S(1)} %pad_add_fusion.refs_0_, bf16[32,384,128]{2,1,0:T(8,128)(2,1)} %copy-done, bf16[32,384,128]{2,1,0:T(8,128)(2,1)} %copy-done, bf16[128,2048]{1,0:T(8,128)(2,1)} %copy-done.13, bf16[128,2048]{1,0:T(8,128)(2,1)} %copy-done.14, f32[384,2048]{1,0:T(8,128)} %copy-done.2), custom_call_target="tpu_custom_call" | custom-call | flops 1610612736 | bytes 3145728 | tf_op jit(solution)/shard_map/project/pallas_call | solution.py:238
  191.9 1.8 put.1
  (112 shorter events, 32.0 us)
Async XLA Ops:
  1.3 2.0 %collective-permute-start = (bf16[128,2048]{1,0:T(8,128)(2,1)S(1)}, bf16[128,2048]{1,0:T(8,128)(2,1)S(1)}, u32[]{:S(2)}, u32[]{:S(2)}) collective-permute-start(bf16[128,2048]{1,0:T(8,128)(2,1)S(1)} %get-tuple-element.116), channel_id=1, source_target_pairs={{0,1},{1,0},{2,3},{3,2},{4,5},{5,4},{6,7},{7,6},{8,9},{9,8},{10,11... | collective-permute-start | bytes 1572872 | tf_op jit(solution)/shard_map/ppermute | solution.py:283
  4.3 28.0 %collective-permute-start.3 = (bf16[256,2048]{1,0:T(8,128)(2,1)}, bf16[256,2048]{1,0:T(8,128)(2,1)}, u32[]{:S(2)}, u32[]{:S(2)}) collective-permute-start(bf16[256,2048]{1,0:T(8,128)(2,1)} %pad_maximum_fusion.refs_53_), channel_id=1, source_target_pairs={{0,8},{1,9},{2,10},{3,11},{4,12},{5,13},{6,14},{7,15},{8,16},{9,17... | collective-permute-start | bytes 3145736 | tf_op jit(solution)/shard_map/ppermute | solution.py:286
  6.7 25.6 %collective-permute-start.2 = (bf16[256,2048]{1,0:T(8,128)(2,1)}, bf16[256,2048]{1,0:T(8,128)(2,1)}, u32[]{:S(2)}, u32[]{:S(2)}) collective-permute-start(bf16[256,2048]{1,0:T(8,128)(2,1)} %pad_maximum_fusion.refs_53_), channel_id=1, source_target_pairs={{0,4},{1,5},{2,6},{3,7},{4,0},{5,1},{6,2},{7,3},{8,12},{9,13},{10,... | collective-permute-start | bytes 3145736 | tf_op jit(solution)/shard_map/ppermute | solution.py:283
  8.0 24.3 %collective-permute-start.1 = (bf16[256,2048]{1,0:T(8,128)(2,1)}, bf16[256,2048]{1,0:T(8,128)(2,1)}, u32[]{:S(2)}, u32[]{:S(2)}) collective-permute-start(bf16[256,2048]{1,0:T(8,128)(2,1)} %pad_maximum_fusion.refs_53_), channel_id=1, source_target_pairs={{0,2},{1,3},{2,0},{3,1},{4,6},{5,7},{6,4},{7,5},{8,10},{9,11},{10,... | collective-permute-start | bytes 3145736 | tf_op jit(solution)/shard_map/ppermute | solution.py:283
  29.4 57.5 %copy-start.7 = (f32[48,4096]{1,0:T(8,128)}, f32[48,4096]{1,0:T(8,128)S(1)}, u32[]{:S(2)}) copy-start(f32[48,4096]{1,0:T(8,128)S(1)} %get-tuple-element.80.refs_4_) | copy-start | bytes 2359300
  32.3 2.7 %collective-permute-start.6 = (f32[16,4096]{1,0:T(8,128)S(1)}, f32[16,4096]{1,0:T(8,128)S(1)}, u32[]{:S(2)}, u32[]{:S(2)}) collective-permute-start(f32[16,4096]{1,0:T(8,128)S(1)} %get-tuple-element.69), channel_id=1, source_target_pairs={{0,1},{1,0},{2,3},{3,2},{4,5},{5,4},{6,7},{7,6},{8,9},{9,8},{10,11... | collective-permute-start | bytes 786440 | tf_op jit(solution)/shard_map/ppermute | solution.py:165
  35.7 4.7 %collective-permute-start.7 = (f32[16,2048]{1,0:T(8,128)S(1)}, f32[16,2048]{1,0:T(8,128)S(1)}, u32[]{:S(2)}, u32[]{:S(2)}) collective-permute-start(f32[16,2048]{1,0:T(8,128)S(1)} %add_select_fusion.3), channel_id=1, source_target_pairs={{0,2},{1,3},{2,0},{3,1},{4,6},{5,7},{6,4},{7,5},{8,10},{9,11},{10,... | collective-permute-start | bytes 393224 | tf_op jit(solution)/shard_map/ppermute | solution.py:165
  38.0 51.6 %copy-start.5 = (f32[4096]{0:T(1024)S(1)}, f32[4096]{0:T(1024)}, u32[]{:S(2)}) copy-start(f32[4096]{0:T(1024)} %param.20) | copy-start | bytes 49156
  39.1 12.9 %collective-permute-start.5 = (bf16[128,2048]{1,0:T(8,128)(2,1)S(1)}, bf16[128,2048]{1,0:T(8,128)(2,1)S(1)}, u32[]{:S(2)}, u32[]{:S(2)}) collective-permute-start(bf16[128,2048]{1,0:T(8,128)(2,1)S(1)} %slice.25), channel_id=1, source_target_pairs={{0,2},{1,3},{2,0},{3,1},{4,6},{5,7},{6,4},{7,5},{8,10},{9,11},{10,... | collective-permute-start | bytes 1572872 | tf_op jit(solution)/shard_map/ppermute | solution.py:283
  39.4 12.6 %collective-permute-start.4 = (bf16[128,2048]{1,0:T(8,128)(2,1)S(1)}, bf16[128,2048]{1,0:T(8,128)(2,1)S(1)}, u32[]{:S(2)}, u32[]{:S(2)}) collective-permute-start(bf16[128,2048]{1,0:T(8,128)(2,1)S(1)} %slice.24), channel_id=1, source_target_pairs={{0,4},{1,5},{2,6},{3,7},{4,0},{5,1},{6,2},{7,3},{8,12},{9,13},{10,... | collective-permute-start | bytes 1572872 | tf_op jit(solution)/shard_map/ppermute | solution.py:283
  52.0 32.1 %collective-permute-start.10 = (bf16[256,2048]{1,0:T(8,128)(2,1)}, bf16[256,2048]{1,0:T(8,128)(2,1)}, u32[]{:S(2)}, u32[]{:S(2)}) collective-permute-start(bf16[256,2048]{1,0:T(8,128)(2,1)} %collective-permute-done.3.refs_56_), channel_id=1, source_target_pairs={{0,8},{1,9},{2,10},{3,11},{4,12},{5,13},{6,14},{7,15},{8,16},{9,17... | collective-permute-start | bytes 3145736 | tf_op jit(solution)/shard_map/ppermute | solution.py:286
  53.4 30.8 %collective-permute-start.9 = (bf16[256,2048]{1,0:T(8,128)(2,1)}, bf16[256,2048]{1,0:T(8,128)(2,1)S(1)}, u32[]{:S(2)}, u32[]{:S(2)}) collective-permute-start(bf16[256,2048]{1,0:T(8,128)(2,1)} %collective-permute-done.3.refs_56_), channel_id=1, source_target_pairs={{0,4},{1,5},{2,6},{3,7},{4,0},{5,1},{6,2},{7,3},{8,12},{9,13},{10,... | collective-permute-start | bytes 3145736 | tf_op jit(solution)/shard_map/ppermute | solution.py:283
  53.6 30.5 %collective-permute-start.8 = (bf16[256,2048]{1,0:T(8,128)(2,1)}, bf16[256,2048]{1,0:T(8,128)(2,1)S(1)}, u32[]{:S(2)}, u32[]{:S(2)}) collective-permute-start(bf16[256,2048]{1,0:T(8,128)(2,1)} %collective-permute-done.3.refs_56_), channel_id=1, source_target_pairs={{0,2},{1,3},{2,0},{3,1},{4,6},{5,7},{6,4},{7,5},{8,10},{9,11},{10,... | collective-permute-start | bytes 3145736 | tf_op jit(solution)/shard_map/ppermute | solution.py:283
  54.7 24.4 %collective-permute-start.11 = (f32[16,2048]{1,0:T(8,128)}, f32[16,2048]{1,0:T(8,128)}, u32[]{:S(2)}, u32[]{:S(2)}) collective-permute-start(f32[16,2048]{1,0:T(8,128)} %get-tuple-element.74), channel_id=1, source_target_pairs={{0,4},{1,5},{2,6},{3,7},{4,0},{5,1},{6,2},{7,3},{8,12},{9,13},{10,... | collective-permute-start | bytes 393224 | tf_op jit(solution)/shard_map/ppermute | solution.py:165
  80.1 4.0 %collective-permute-start.12 = (f32[16,2048]{1,0:T(8,128)S(1)}, f32[16,2048]{1,0:T(8,128)S(1)}, u32[]{:S(2)}, u32[]{:S(2)}) collective-permute-start(f32[16,2048]{1,0:T(8,128)S(1)} %add_select_fusion.1), channel_id=1, source_target_pairs={{0,1},{1,0},{2,3},{3,2},{4,5},{5,4},{6,7},{7,6},{8,9},{9,8},{10,11... | collective-permute-start | bytes 393224 | tf_op jit(solution)/shard_map/ppermute | solution.py:165
  84.1 36.9 %collective-permute-start.17 = (bf16[256,2048]{1,0:T(8,128)(2,1)}, bf16[256,2048]{1,0:T(8,128)(2,1)}, u32[]{:S(2)}, u32[]{:S(2)}) collective-permute-start(bf16[256,2048]{1,0:T(8,128)(2,1)} %collective-permute-done.10.refs_61_), channel_id=1, source_target_pairs={{0,8},{1,9},{2,10},{3,11},{4,12},{5,13},{6,14},{7,15},{8,16},{9,17... | collective-permute-start | bytes 3145736 | tf_op jit(solution)/shard_map/ppermute | solution.py:286
  85.5 35.5 %collective-permute-start.16 = (bf16[256,2048]{1,0:T(8,128)(2,1)}, bf16[256,2048]{1,0:T(8,128)(2,1)}, u32[]{:S(2)}, u32[]{:S(2)}) collective-permute-start(bf16[256,2048]{1,0:T(8,128)(2,1)} %collective-permute-done.10.refs_61_), channel_id=1, source_target_pairs={{0,4},{1,5},{2,6},{3,7},{4,0},{5,1},{6,2},{7,3},{8,12},{9,13},{10,... | collective-permute-start | bytes 3145736 | tf_op jit(solution)/shard_map/ppermute | solution.py:283
  85.7 36.0 %collective-permute-start.15 = (bf16[256,2048]{1,0:T(8,128)(2,1)}, bf16[256,2048]{1,0:T(8,128)(2,1)}, u32[]{:S(2)}, u32[]{:S(2)}) collective-permute-start(bf16[256,2048]{1,0:T(8,128)(2,1)} %collective-permute-done.10.refs_61_), channel_id=1, source_target_pairs={{0,2},{1,3},{2,0},{3,1},{4,6},{5,7},{6,4},{7,5},{8,10},{9,11},{10,... | collective-permute-start | bytes 3145736 | tf_op jit(solution)/shard_map/ppermute | solution.py:283
  86.9 34.0 %collective-permute-start.14 = (bf16[128,2048]{1,0:T(8,128)(2,1)S(1)}, bf16[128,2048]{1,0:T(8,128)(2,1)S(1)}, u32[]{:S(2)}, u32[]{:S(2)}) collective-permute-start(bf16[128,2048]{1,0:T(8,128)(2,1)S(1)} %slice.27), channel_id=1, source_target_pairs={{0,2},{1,3},{2,0},{3,1},{4,6},{5,7},{6,4},{7,5},{8,10},{9,11},{10,... | collective-permute-start | bytes 1572872 | tf_op jit(solution)/shard_map/ppermute | solution.py:283
  87.3 33.6 %collective-permute-start.13 = (bf16[128,2048]{1,0:T(8,128)(2,1)S(1)}, bf16[128,2048]{1,0:T(8,128)(2,1)S(1)}, u32[]{:S(2)}, u32[]{:S(2)}) collective-permute-start(bf16[128,2048]{1,0:T(8,128)(2,1)S(1)} %slice.26), channel_id=1, source_target_pairs={{0,4},{1,5},{2,6},{3,7},{4,0},{5,1},{6,2},{7,3},{8,12},{9,13},{10,... | collective-permute-start | bytes 1572872 | tf_op jit(solution)/shard_map/ppermute | solution.py:283
  92.4 37.4 %copy-start.26 = (s32[2]{0:T(128)S(1)}, s32[2]{0:T(128)}, u32[]{:S(2)}) copy-start(s32[2]{0:T(128)} %constant.167.clone) | copy-start | bytes 28
  92.4 37.4 %copy-start.25 = (s32[4]{0:T(128)S(1)}, s32[4]{0:T(128)}, u32[]{:S(2)}) copy-start(s32[4]{0:T(128)} %constant.166.clone) | copy-start | bytes 52
  92.4 37.5 %copy-start.23 = (s32[26]{0:T(128)S(1)}, s32[26]{0:T(128)}, u32[]{:S(2)}) copy-start(s32[26]{0:T(128)} %constant.172) | copy-start | bytes 316
  92.4 37.5 %copy-start.24 = (s32[26]{0:T(128)S(1)}, s32[26]{0:T(128)}, u32[]{:S(2)}) copy-start(s32[26]{0:T(128)} %constant.164.clone) | copy-start | bytes 316
  121.9 20.2 %collective-permute-start.20 = (bf16[32,384,128]{2,1,0:T(8,128)(2,1)S(1)}, bf16[32,384,128]{2,1,0:T(8,128)(2,1)}, u32[]{:S(2)}, u32[]{:S(2)}) collective-permute-start(bf16[32,384,128]{2,1,0:T(8,128)(2,1)S(1)} %convolve.1.refs_1_.refs_2_.refs_3_.refs_4_.refs_5_.refs_6_.refs_7_.refs_8_.refs_9_.refs_10_.refs_11, ...), channel_id=1, source_target_pairs={{0,1},{1,0},{2,3},{3,2},{4,5},{5,4},{6,7},{7,6},{8,9},{9,8},{10,11... | collective-permute-start | bytes 9437192 | tf_op jit(solution)/shard_map/ppermute | solution.py:283
  127.5 13.9 %collective-permute-start.19 = (bf16[128,2048]{1,0:T(8,128)(2,1)}, bf16[128,2048]{1,0:T(8,128)(2,1)}, u32[]{:S(2)}, u32[]{:S(2)}) collective-permute-start(bf16[128,2048]{1,0:T(8,128)(2,1)} %slice.29), channel_id=1, source_target_pairs={{0,2},{1,3},{2,0},{3,1},{4,6},{5,7},{6,4},{7,5},{8,10},{9,11},{10,... | collective-permute-start | bytes 1572872 | tf_op jit(solution)/shard_map/ppermute | solution.py:283
  128.5 13.6 %collective-permute-start.18 = (bf16[128,2048]{1,0:T(8,128)(2,1)}, bf16[128,2048]{1,0:T(8,128)(2,1)}, u32[]{:S(2)}, u32[]{:S(2)}) collective-permute-start(bf16[128,2048]{1,0:T(8,128)(2,1)} %slice.28), channel_id=1, source_target_pairs={{0,4},{1,5},{2,6},{3,7},{4,0},{5,1},{6,2},{7,3},{8,12},{9,13},{10,... | collective-permute-start | bytes 1572872 | tf_op jit(solution)/shard_map/ppermute | solution.py:283
  142.1 23.8 %collective-permute-start.22 = (bf16[256,2048]{1,0:T(8,128)(2,1)}, bf16[256,2048]{1,0:T(8,128)(2,1)S(1)}, u32[]{:S(2)}, u32[]{:S(2)}) collective-permute-start(bf16[256,2048]{1,0:T(8,128)(2,1)} %collective-permute-done.17.refs_66_), channel_id=1, source_target_pairs={{0,4},{1,5},{2,6},{3,7},{4,0},{5,1},{6,2},{7,3},{8,12},{9,13},{10,... | collective-permute-start | bytes 3145736 | tf_op jit(solution)/shard_map/ppermute | solution.py:283
  143.3 23.5 %collective-permute-start.21 = (bf16[256,2048]{1,0:T(8,128)(2,1)}, bf16[256,2048]{1,0:T(8,128)(2,1)S(1)}, u32[]{:S(2)}, u32[]{:S(2)}) collective-permute-start(bf16[256,2048]{1,0:T(8,128)(2,1)} %collective-permute-done.17.refs_66_), channel_id=1, source_target_pairs={{0,2},{1,3},{2,0},{3,1},{4,6},{5,7},{6,4},{7,5},{8,10},{9,11},{10,... | collective-permute-start | bytes 3145736 | tf_op jit(solution)/shard_map/ppermute | solution.py:283
  166.9 11.2 %collective-permute-start.23 = (bf16[128,2048]{1,0:T(8,128)(2,1)S(1)}, bf16[128,2048]{1,0:T(8,128)(2,1)S(1)}, u32[]{:S(2)}, u32[]{:S(2)}) collective-permute-start(bf16[128,2048]{1,0:T(8,128)(2,1)S(1)} %slice.30), channel_id=1, source_target_pairs={{0,4},{1,5},{2,6},{3,7},{4,0},{5,1},{6,2},{7,3},{8,12},{9,13},{10,... | collective-permute-start | bytes 1572872 | tf_op jit(solution)/shard_map/ppermute | solution.py:283
  167.3 10.9 %collective-permute-start.24 = (bf16[128,2048]{1,0:T(8,128)(2,1)S(1)}, bf16[128,2048]{1,0:T(8,128)(2,1)S(1)}, u32[]{:S(2)}, u32[]{:S(2)}) collective-permute-start(bf16[128,2048]{1,0:T(8,128)(2,1)S(1)} %slice.31), channel_id=1, source_target_pairs={{0,2},{1,3},{2,0},{3,1},{4,6},{5,7},{6,4},{7,5},{8,10},{9,11},{10,... | collective-permute-start | bytes 1572872 | tf_op jit(solution)/shard_map/ppermute | solution.py:283
  183.2 8.7 %collective-permute-start.25 = (bf16[384,2048]{1,0:T(8,128)(2,1)S(1)}, bf16[384,2048]{1,0:T(8,128)(2,1)S(1)}, u32[]{:S(2)}, u32[]{:S(2)}) collective-permute-start(bf16[384,2048]{1,0:T(8,128)(2,1)S(1)} %project.6), channel_id=1, source_target_pairs={{0,1},{1,0},{2,3},{3,2},{4,5},{5,4},{6,7},{7,6},{8,9},{9,8},{10,11... | collective-permute-start | bytes 4718600 | tf_op jit(solution)/shard_map/ppermute | solution.py:283
  (21 other events, 99.7 us)

commit v2 on v1

--- a/solution.py
+++ b/solution.py
@@ -10,6 +10,7 @@
 LANES = 128
 COLS = 512
 SCALE = 4
+STEP = 1024
 F32 = jnp.float32
 BF16 = jnp.bfloat16
 AXES = ("dp", "ctx")
@@ -37,31 +38,36 @@
     return lax.broadcasted_iota(jnp.int32, shape, axis)
 
 
-def state_kernel(members, poles, blocks, k_ref, v_ref, col_ref, lane_ref, d_ref, bs_ref, slab_ref):
+def lane_rate(rate, same, per, poles):
+    return jnp.where(same, rate, 0.0).reshape(per, poles, same.shape[1]).sum(axis=0)
+
+
+def state_kernel(members, poles, blocks, k_ref, v_ref, col_ref, d_ref, bs_ref, slab_ref):
     per = LANES // members
+    wide = per * poles
+    back = (BLOCK - 1 - iota((wide, BLOCK), 1)).astype(F32)
+    same = iota((wide, LANES), 0) // poles == iota((wide, LANES), 1) // members
     for sub in range(k_ref.shape[1] // LANES):
         at = slice(sub * LANES, (sub + 1) * LANES)
         d = (k_ref[:, at].astype(F32) * v_ref[:, at].astype(F32)).astype(BF16)
         d_ref[:, at] = d
-        rate = col_ref[sub * per * poles : (sub + 1) * per * poles, 0:1]
-        back = (BLOCK - 1 - iota((per * poles, BLOCK), 1)).astype(F32)
-        ending = jnp.concatenate(split(jnp.exp(-rate * back)), axis=0)
+        rate = col_ref[sub * wide : (sub + 1) * wide, 0:1]
+        ending = jnp.concatenate(split(jnp.exp(-rate * back)), axis=1)
         tiles = jnp.concatenate([d[b * BLOCK : (b + 1) * BLOCK] for b in range(blocks)], axis=1)
+        tiles = jnp.concatenate([tiles, tiles], axis=0)
         part = jnp.dot(ending, tiles, preferred_element_type=F32)
-        part = part[: per * poles] + part[per * poles :]
-        same = iota(part.shape, 0) // poles == (iota(part.shape, 1) % LANES) // members
-        state = jnp.where(same, part, 0.0).reshape(per, poles, blocks * LANES).sum(axis=0)
-        decay = jnp.exp(-lane_ref[:, at] * BLOCK)
+        decay = jnp.exp(-lane_rate(rate, same, per, poles) * BLOCK)
         slab = None
         for b in range(blocks):
-            one = state[:, b * LANES : (b + 1) * LANES]
+            one = jnp.where(same, part[:, b * LANES : (b + 1) * LANES], 0.0)
+            one = one.reshape(per, poles, LANES).sum(axis=0)
             bs_ref[b * poles : (b + 1) * poles, at] = one
             slab = one if slab is None else slab * decay + one
         slab_ref[:, at] = slab
 
 
 def conv_kernel(
-    members, poles, blocks, d_ref, q_ref, col_ref, row_ref, bs_ref, inc_ref, lane_ref, skip_ref, g_ref
+    members, poles, blocks, d_ref, q_ref, col_ref, row_ref, bs_ref, inc_ref, skip_ref, g_ref
 ):
     per = LANES // members
     wide = per * poles
@@ -83,8 +89,8 @@
         reach = row_ref[1:2, at_row] * jnp.exp(-row_ref[0:1, at_row] * ahead)
         high, low = split(reach)
         left = jnp.concatenate(left + [high, low, high], axis=1)
-        decay = jnp.exp(-lane_ref[:, at] * BLOCK)
         same = iota((wide, LANES), 0) // poles == iota((wide, LANES), 1) // members
+        decay = jnp.exp(-lane_rate(rate, same, per, poles) * BLOCK)
         owner = iota((1, LANES), 1) // members
         state = inc_ref[:, at]
         right = []
@@ -103,10 +109,10 @@
             g_ref[sub, rows, :] = (q_ref[rows, at].astype(F32) * whole).astype(BF16)
 
 
-def states(key, value, col, lane, members, poles):
+def states(key, value, col, members, poles):
     rows, width = key.shape
     blocks = rows // BLOCK
-    step = 2 * LANES
+    step = STEP
     seq = pl.BlockSpec((rows, step), lambda i: (0, i))
     wide = step // members * poles
     return pl.pallas_call(
@@ -116,7 +122,6 @@
             seq,
             seq,
             pl.BlockSpec((wide, 2), lambda i: (i, 0)),
-            pl.BlockSpec((poles, step), lambda i: (0, i)),
         ],
         out_specs=[
             seq,
@@ -131,13 +136,13 @@
         compiler_params=params(32),
         cost_estimate=cost(4 * poles * members * rows * width * SCALE, 6 * rows * width),
         name="states",
-    )(in_hbm(key), in_hbm(value), col, lane)
-
-
-def convolve(driven, query, col, row, block_state, incoming, lane, skip, members, poles):
+    )(in_hbm(key), in_hbm(value), col)
+
+
+def convolve(driven, query, col, row, block_state, incoming, skip, members, poles):
     rows, width = driven.shape
     blocks = rows // BLOCK
-    step = 2 * LANES
+    step = STEP
     seq = pl.BlockSpec((rows, step), lambda i: (0, i))
     wide = step // members * poles
     return pl.pallas_call(
@@ -150,7 +155,6 @@
             pl.BlockSpec((2, wide), lambda i: (0, i)),
             pl.BlockSpec((blocks * poles, step), lambda i: (0, i)),
             pl.BlockSpec((poles, step), lambda i: (0, i)),
-            pl.BlockSpec((poles, step), lambda i: (0, i)),
             pl.BlockSpec((1, step), lambda i: (0, i)),
         ],
         out_specs=pl.BlockSpec((step // LANES, rows, LANES), lambda i: (i, 0, 0)),
@@ -158,7 +162,7 @@
         compiler_params=params(32),
         cost_estimate=cost(2 * (BLOCK * LANES // members + 3 * LANES) * rows * width * SCALE, 6 * rows * width),
         name="convolve",
-    )(in_hbm(driven), in_hbm(query), col, row, block_state, incoming, lane, skip)
+    )(in_hbm(driven), in_hbm(query), col, row, block_state, incoming, skip)
 
 
 def scan_send(total, slabs, width):
@@ -172,13 +176,15 @@
     return [lax.dynamic_slice_in_dim(a, core * half, half, 1) for a in (total, lane)]
 
 
-def scan_step(before, total, other, lane, rows, width):
-    place = lax.axis_index("ctx")
-    upper = (place // width) % 2 == 1
-    offset = ((place % width) // 2 * 2).astype(F32) * rows
-    before = jnp.where(upper, before + other * jnp.exp(-lane * offset), before)
-    decay = jnp.exp(-lane * float(rows * width))
-    return before, jnp.where(upper, other * decay + total, total * decay + other)
+def pairs_ahead(total, lane, rows, slabs):
+    pair = lax.axis_index("ctx") // 2
+    before = jnp.zeros_like(total)
+    for step in range(1, slabs // 2):
+        other = scan_send(total, slabs, 2 * step)
+        gap = pair - 1 - (pair ^ step)
+        decay = jnp.exp(-lane * (jnp.maximum(gap, 0).astype(F32) * float(2 * rows)))
+        before = before + jnp.where(gap >= 0, other * decay, 0.0)
+    return before
 
 
 def incoming_state(before, other_half, other_slab, lane, rows, core):
@@ -214,19 +220,19 @@
         o_ref[...] = total.astype(o_ref.dtype)
 
 
-def project(place, ring, gated, pieces, wide, total=None, side=None, dout=None, dtype=F32):
+def project(place, ring, gated, pieces, wide, total=None, side=None, dout=None, dtype=F32, cols=COLS):
     shards, rows, depth = gated[0].shape
     steps = [one for _, _, owners in pieces for one in owners]
     sizes = [LANES * len(owners) for _, _, owners in pieces]
     sides = len(gated)
-    nb = wide // COLS
+    nb = wide // cols
     idx = shard_table(place, ring, steps)
     if side is not None:
         idx = jnp.concatenate([idx, (side * nb).astype(jnp.int32)[None]])
-    block = pl.BlockSpec((rows, COLS), lambda b, i: (0, b))
+    block = pl.BlockSpec((rows, cols), lambda b, i: (0, b))
     specs = [pl.BlockSpec((1, rows, depth), lambda b, i, p=p: (i[p], 0, 0)) for p in range(len(steps))] * sides
     specs += [
-        pl.BlockSpec((size, COLS), lambda b, i, at=at: (at, b)) for size, (_, at, _) in zip(sizes, pieces)
+        pl.BlockSpec((size, cols), lambda b, i, at=at: (at, b)) for size, (_, at, _) in zip(sizes, pieces)
     ]
     operands = [g for g in gated for _ in steps] + [a for a, _, _ in pieces]
     if total is not None:
@@ -241,7 +247,7 @@
             num_scalar_prefetch=1,
             grid=(nb,),
             in_specs=specs,
-            out_specs=[block if side is None else pl.BlockSpec((rows, COLS), lambda b, i: (0, i[last] + b))] * sides,
+            out_specs=[block if side is None else pl.BlockSpec((rows, cols), lambda b, i: (0, i[last] + b))] * sides,
         ),
         out_shape=[shape] * sides,
         compiler_params=params(48),
@@ -260,20 +266,15 @@
     query, key, value = [a.reshape(rows, width) for a in (query_stream, key_stream, value_stream)]
     skip = skip_gain[None]
 
-    if depth != LANES:
+    if depth != LANES or devices != 32:
         core = lax.axis_index("ctx") % 2
-        col, row, lane = tables(pole_rate, residue, members)
-        driven, block_state, slab = states(key, value, col, lane, members, poles)
+        col, lane = columns(pole_rate, residue), lanes(pole_rate, members)
+        driven, block_state, slab = states(key, value, col, members, poles)
         other_slab = scan_send(slab, slabs, 1)
         total, lane_half = pair_total(slab, other_slab, lane, rows, core)
-        before = jnp.zeros_like(total)
-        step = 2
-        while step < slabs:
-            other = scan_send(total, slabs, step)
-            before, total = scan_step(before, total, other, lane_half, rows, step)
-            step *= 2
+        before = pairs_ahead(total, lane_half, rows, slabs)
         incoming = incoming_state(before, scan_send(before, slabs, 1), other_slab, lane, rows, core)
-        gated = convolve(driven, query, col, row, block_state, incoming, lane, skip, members, poles)
+        gated = convolve(driven, query, col, col.T, block_state, incoming, skip, members, poles)
         weight = lax.all_gather(out_weight, AXES, axis=0, tiled=True)
         flat = gated.transpose(1, 0, 2).reshape(rows, width)
         out = jnp.dot(flat, weight, preferred_element_type=F32)
@@ -292,72 +293,80 @@
     mine = lax.dynamic_slice_in_dim(out_weight, core * half, half, 1)
     give = lax.dynamic_slice_in_dim(out_weight, (1 - core) * half, half, 1)
 
-    got = swap(give, 1)
-    cur = jnp.concatenate([mine, got], axis=0)
-    both = [(0, 0, 0, 0), (0, 0, 0, 1)]
-    pieces = [(cur, 0, both)]
-
-    def straight(cur, back, last):
-        new = [swap(cur, 2), swap(cur, 4)] + ([] if last else [ahead(cur)])
-        owners = [[(back + dz, dy, dx, k) for k in (0, 1)] for dz, dy, dx in ((0, 0, 1), (0, 1, 0), (1, 0, 0))]
-        return [(a, 0, o) for a, o in zip(new, owners)]
-
-    def diagonal(over_x, over_y, back):
-        return [(swap(over_y, 4), 0, [(back, 1, 1, 0)]), (swap(over_x, 2), 0, [(back, 1, 1, 1)])]
-
-    def over(new):
-        return new[1][0][depth:], new[0][0][:depth]
-
     def settle(new, work):
         arrays, work = fence(([a for a, _, _ in new], work))
-        return [(a, at, o) for a, (_, at, o) in zip(arrays, new)], work
-
-    cur, pole_rate, residue, key, value = fence((cur, pole_rate, residue, key, value))
-    col, row, lane = tables(pole_rate, residue, members)
-    new = straight(cur, 0, False)
-    driven, block_state, slab = states(key, value, col, lane, members, poles)
-    new, (driven, block_state, slab, lane) = settle(new, (driven, block_state, slab, lane))
+        return [(a, 0, o) for a, (_, _, o) in zip(arrays, new)], work
+
+    def along_x(a, back, y, k):
+        return swap(a, 2), 0, [(back, y, 1, i) for i in k]
+
+    def along_y(a, back, x, k):
+        return swap(a, 4), 0, [(back, 1, x, i) for i in k]
+
+    both = (0, 1)
+    got = swap(give, 1)
+    new = [along_x(mine, 0, 0, (0,)), along_y(mine, 0, 0, (0,)), (ahead(mine), 0, [(1, 0, 0, 0)])]
+    driven, block_state, slab = states(key, value, columns(pole_rate, residue), members, poles)
+    work = (got, driven, block_state, slab, pole_rate, residue)
+    new, (got, driven, block_state, slab, pole_rate, residue) = settle(new, work)
+    pieces = [(mine, 0, [(0, 0, 0, 0)]), (got, 0, [(0, 0, 0, 1)])]
+    more = [along_x(got, 0, 0, (1,)), along_y(got, 0, 0, (1,)), (ahead(got), 0, [(1, 0, 0, 1)])]
+    other_slab = scan_send(slab, slabs, 1)
+    lane = lanes(pole_rate, members)
+    total, lane_half = pair_total(slab, other_slab, lane, rows, core)
+    work = (total, lane_half, other_slab, [a for a, _, _ in new])
+    more, (total, lane_half, other_slab, (x_mine, y_mine, z_mine)) = settle(more, work)
+    for one, two in zip(new, more):
+        pieces += [one, two]
+    (x_got, _, _), (y_got, _, _), (z_got, _, _) = more
+    new = [
+        along_x(y_got, 0, 1, (1,)),
+        along_y(x_mine, 0, 1, (0,)),
+        along_x(z_mine, 1, 0, (0,)),
+        along_y(z_got, 1, 0, (1,)),
+        (ahead(jnp.concatenate([z_mine, z_got], axis=0)), 0, [(2, 0, 0, 0), (2, 0, 0, 1)]),
+    ]
+    before = pairs_ahead(total, lane_half, rows, slabs)
+    other_half = scan_send(before, slabs, 1)
+    aside = jnp.concatenate([x_got, y_mine], axis=0)
+    new, (before, other_half, other_slab, aside) = settle(new, (before, other_half, other_slab, aside))
     pieces += new
-    cur = new[2][0]
-    new = diagonal(*over(new), 0)
-    other_slab = scan_send(slab, slabs, 1)
-    total, lane_half = pair_total(slab, other_slab, lane, rows, core)
-    other = scan_send(total, slabs, 2)
-    before, total = scan_step(jnp.zeros_like(total), total, other, lane_half, rows, 2)
-    new, (before, total, other_slab, lane_half, cur) = settle(new, (before, total, other_slab, lane_half, cur))
+    (x_half, _, _), (y_half, _, _), (cur, _, _) = new[2:]
+    new = [
+        along_x(y_half, 1, 1, (1,)),
+        along_y(x_half, 1, 1, (0,)),
+        along_x(cur[:depth], 2, 0, (0,)),
+        along_y(cur[depth:], 2, 0, (1,)),
+        (ahead(cur), 0, [(3, 0, 0, 0), (3, 0, 0, 1)]),
+    ]
+    incoming = incoming_state(before, other_half, other_slab, lane, rows, core)
+    col = columns(pole_rate, residue)
+    gated = convolve(driven, query, col, col.T, block_state, incoming, skip, members, poles)
+    new, gated = settle(new, gated)
     pieces += new
-    other = scan_send(total, slabs, 4)
-    before, _ = scan_step(before, total, other, lane_half, rows, 4)
-    new = straight(cur, 1, False)
-    other_half = scan_send(before, slabs, 1)
-    new, (before, other_half) = settle(new, (before, other_half))
-    pieces += new
-    back = 2
-    gated = None
-    while back < ring - 1:
-        done = diagonal(*over(new), back - 1)
-        new = done + straight(new[2][0], back, False)
-        if gated is None:
-            incoming = incoming_state(before, other_half, other_slab, lane, rows, core)
-            gated = convolve(driven, query, col, row, block_state, incoming, lane, skip, members, poles)
-        new, gated = settle(new, gated)
-        pieces += new
-        new = new[2:]
-        back += 1
-    cur = new[2][0]
-    new = diagonal(*over(new), back - 1)
+    (x_half, _, _), (y_half, _, _), (cur, _, _) = new[2:]
+    new = [
+        along_x(cur, 3, 0, both),
+        along_y(cur, 3, 0, both),
+        (ahead(aside), 0, [(1, 0, 1, 1), (1, 1, 0, 0)]),
+    ]
     peer = swap(gated, 1)
-    new, (gated, peer, cur) = settle(new, (gated, peer, cur))
-    pieces += new
-    new = straight(cur, back, True)
-    sums = project(place, ring, (gated, peer), pieces, half)
-    new, (gated, peer, sums) = settle(new, (gated, peer, sums))
-    late = diagonal(*over(new), back)
-    sums = project(place, ring, (gated, peer), new, half, sums)
-    late, (gated, peer, (sum_own, sum_peer)) = settle(late, (gated, peer, sums))
-    (out_peer,) = project(place, ring, [peer], late, half, [sum_peer], dtype=BF16)
+    (sum_own,) = project(place, ring, [gated], pieces, half)
+    new, (gated, peer, sum_own, x_half, y_half) = settle(new, (gated, peer, sum_own, x_half, y_half))
+    (x_whole, _, _), (y_whole, _, _), (aside, _, _) = new
+    late = [
+        along_x(y_half, 2, 1, (1,)),
+        along_y(x_half, 2, 1, (0,)),
+        along_x(y_whole[depth:], 3, 1, (1,)),
+        along_y(x_whole[:depth], 3, 1, (0,)),
+        (ahead(aside), 0, [(2, 0, 1, 1), (2, 1, 0, 0)]),
+    ]
+    (sum_own,) = project(place, ring, [gated], new, half, [sum_own], cols=2 * COLS)
+    (sum_peer,) = project(place, ring, [peer], pieces + new, half)
+    late, (gated, peer, sum_own, sum_peer) = settle(late, (gated, peer, sum_own, sum_peer))
+    (out_peer,) = project(place, ring, [peer], late, half, [sum_peer], dtype=BF16, cols=2 * COLS)
     other = swap(out_peer, 1)
-    (out,) = project(place, ring, [gated], late, half, [sum_own], core, dout, dtype=BF16)
+    (out,) = project(place, ring, [gated], late, half, [sum_own], core, dout, dtype=BF16, cols=2 * COLS)
     return put(other, 1 - core, out).reshape(seqs, rows, dout)
 
 
@@ -383,10 +392,12 @@
     )(side.astype(jnp.int32)[None], half, whole)
 
 
-def tables(pole_rate, residue, members):
-    col = jnp.stack([pole_rate.reshape(-1), residue.reshape(-1)], axis=1)
-    row = jnp.stack([pole_rate.reshape(-1), residue.reshape(-1)], axis=0)
-    return col, row, jnp.repeat(pole_rate.T, members, axis=1)
+def columns(pole_rate, residue):
+    return jnp.stack([pole_rate.reshape(-1), residue.reshape(-1)], axis=1)
+
+
+def lanes(pole_rate, members):
+    return jnp.repeat(pole_rate.T, members, axis=1)
 
 
 def shard_table(place, ring, steps):

time: 195 us -> 170 us (0.87)
  waiting for transfers between devices: 67 us -> 50.5 us
  Pallas kernels: 64.9 us -> 52.6 us
  starting transfers between devices: 29.8 us -> 35.2 us
  local copies, waits for them, and re-layouts: 26.3 us -> 22.9 us
  other arithmetic: 5.39 us -> 7.68 us
    ppermute x4 -> x5, waiting for transfers between devices: 23.3 us -> 1.21 us  [scan_send(): return lax.ppermute(total, 'ctx', [(i, i ^ width) for i in range(slabs)])]
    ppermute x3 -> x6, waiting for transfers between devices: 2.93 us -> 20.4 us  [ahead(): lax.ppermute(a, AXES, [(i, (i + 8) % devices) for i in range(devices)])]
    ppermute x19 -> x21, waiting for transfers between devices: 40.8 us -> 28.9 us  [swap(): return lax.ppermute(a, AXES, [(i, i ^ bit) for i in range(devices)])]
    pallas_call x1, Pallas kernels: 11.7 us -> 5.16 us  [states(): pl.pallas_call(lambda *refs: state_kernel(members, poles, blocks, *refs),...]
    pallas_call x1, Pallas kernels: 16.4 us -> 11.6 us  [convolve(): pl.pallas_call(lambda *refs: conv_kernel(members, poles, blocks, *refs),...]
    slice x8 -> x3, local copies, waits for them, and re-layouts: 6.05 us -> 1.7 us  [the longest x1 1.62 us: local(): cur[depth:]]
    concatenate x1 -> x2, other arithmetic: 1.04 us -> 4.44 us  [the longest x1 2.32 us: local(): aside = jnp.concatenate([x_got, y_mine], axis=0)]
    ppermute x19 -> x21, starting transfers between devices: 17.7 us -> 20.9 us  [swap(): return lax.ppermute(a, AXES, [(i, i ^ bit) for i in range(devices)])]
  transfers between devices with their start and end apart: 26 -> 32, of which waited for: 15 -> 7; matrix products, arithmetic and copies ran while one was open for 9% -> 10% of each run, Pallas kernels for 30% -> 27%
where the time goes in v2:
time: 170 us; the launch traced here: 169 us
  Pallas kernels  52.6 us (31%)
  waiting for transfers between devices  50.5 us (30%)
  starting transfers between devices  35.2 us (21%)
  local copies, waits for them, and re-layouts  22.9 us (13%)
  other arithmetic  7.68 us (5%)
    pallas_call x5, Pallas kernels, project(): pl.pallas_call(lambda *refs: project_kernel(sizes, sides, total is not No...  34.1 us
    ppermute x21, waiting for transfers between devices, swap(): return lax.ppermute(a, AXES, [(i, i ^ bit) for i in range(devices)])  28.9 us
    ppermute x21, starting transfers between devices, swap(): return lax.ppermute(a, AXES, [(i, i ^ bit) for i in range(devices)])  20.9 us
    ppermute x6, waiting for transfers between devices, ahead(): lax.ppermute(a, AXES, [(i, (i + 8) % devices) for i in range(devices)])  20.4 us
    unnamed x82, local copies, waits for them, and re-layouts  12 us
    pallas_call x1, Pallas kernels, convolve(): pl.pallas_call(lambda *refs: conv_kernel(members, poles, blocks, *refs),...  11.6 us
    ppermute x5, starting transfers between devices, scan_send(): return lax.ppermute(total, 'ctx', [(i, i ^ width) for i in range(slabs)])  8.94 us
    ppermute x6, starting transfers between devices, ahead(): lax.ppermute(a, AXES, [(i, (i + 8) % devices) for i in range(devices)])  5.31 us
  transfers between devices with their start and end apart: 32, of which 7 were waited for; matrix products, arithmetic and copies ran while one was open for 10% of the time, Pallas kernels for 27%

profile of v2, /device:TPU:1, one launch (start us, length us, event | category | flops | bytes accessed | tf_op | source)
XLA Modules:
  0.0 169.4 jit_solution(2772474652563891165)
XLA Ops:
  0.0 2.1 %constant_dynamic-slice_fusion.1 = (bf16[128,2048]{1,0:T(8,128)(2,1)}, bf16[128,2048]{1,0:T(8,128)(2,1)S(1)}) fusion(bf16[128,4096]{1,0:T(8,128)(2,1)} %param.23, s32[]{:T(128)S(6)} %select_n.105, s32[]{:T(128)S(6)} %select_n.104), kind=kLoop, calls=%fused_computation.22 | loop fusion | bytes 2097160 | tf_op jit(solution)/shard_map/dynamic_slice | solution.py:294
  2.1 2.1 %collective-permute-start.2 = (bf16[128,2048]{1,0:T(8,128)(2,1)S(1)}, bf16[128,2048]{1,0:T(8,128)(2,1)}, u32[]{:S(2)}, u32[]{:S(2)}) collective-permute-start(bf16[128,2048]{1,0:T(8,128)(2,1)S(1)} %get-tuple-element.114.refs_21_.refs_27_), channel_id=1, source_target_pairs={{0,8},{1,9},{2,10},{3,11},{4,12},{5,13},{6,14},{7,15},{8,16},{9,17... | collective-permute-start | bytes 1572872 | tf_op jit(solution)/shard_map/ppermute | solution.py:287
  6.7 1.5 collective-permute-start.3
  10.8 5.2 %states.1 = (bf16[384,4096]{1,0:T(8,128)(2,1)S(1)}, f32[48,4096]{1,0:T(8,128)S(1)}, f32[16,4096]{1,0:T(8,128)S(1)}) custom-call(bf16[384,4096]{1,0:T(8,128)(2,1)} %bitcast.12, bf16[384,4096]{1,0:T(8,128)(2,1)} %bitcast.13, f32[4096,2]{1,0:T(8,128)S(1)} %copy.33.refs_2_), custom_call_target="tpu_custom_call" | custom-call | flops 6442450944 | bytes 9437184 | tf_op jit(solution)/shard_map/states/pallas_call | solution.py:118
  16.0 1.7 copy-done.6
  18.6 1.4 collective-permute-start.6
  20.6 2.9 %collective-permute-start.7 = (f32[16,4096]{1,0:T(8,128)S(1)}, f32[16,4096]{1,0:T(8,128)}, u32[]{:S(2)}, u32[]{:S(2)}) collective-permute-start(f32[16,4096]{1,0:T(8,128)S(1)} %get-tuple-element.62), channel_id=1, source_target_pairs={{0,1},{1,0},{2,3},{3,2},{4,5},{5,4},{6,7},{7,6},{8,9},{9,8},{10,11... | collective-permute-start | bytes 786440 | tf_op jit(solution)/shard_map/ppermute | solution.py:169
  24.1 2.3 %reshape.17 = f32[16,4096]{1,0:T(8,128)} reshape(f32[16,256,16]{2,1,0:T(8,128)S(1)} %broadcast_in_dim.19) | data formatting | bytes 524288 | tf_op jit(solution)/shard_map/reshape | solution.py:400
  29.3 3.5 %collective-permute-done.6.refs_28_.refs_34_ = bf16[128,2048]{1,0:T(8,128)(2,1)S(1)} collective-permute-done((bf16[128,2048]{1,0:T(8,128)(2,1)}, bf16[128,2048]{1,0:T(8,128)(2,1)S(1)}, u32[]{:S(2)}, u32[]{:S(2)}) %collective-permute-start.6) | collective-permute-done | bytes 524320 | tf_op jit(solution)/shard_map/ppermute | solution.py:287
  34.0 1.4 collective-permute-start.13
  35.4 2.1 %pad_maximum_fusion = bf16[256,2048]{1,0:T(8,128)(2,1)} fusion(bf16[128,2048]{1,0:T(8,128)(2,1)S(1)} %collective-permute-done.6.refs_28_.refs_34_, bf16[128,2048]{1,0:T(8,128)(2,1)} %collective-permute-done.2.refs_27_.refs_33_), kind=kLoop, calls=%fused_computation | loop fusion | flops 2097152 | bytes 2097152 | tf_op jit(solution)/shard_map/concatenate | solution.py:327
  39.4 3.3 %collective-permute-start.16 = (f32[16,2048]{1,0:T(8,128)S(1)}, f32[16,2048]{1,0:T(8,128)S(1)}, u32[]{:S(2)}, u32[]{:S(2)}) collective-permute-start(f32[16,2048]{1,0:T(8,128)S(1)} %select_add_fusion), channel_id=1, source_target_pairs={{0,1},{1,0},{2,3},{3,2},{4,5},{5,4},{6,7},{7,6},{8,9},{9,8},{10,11... | collective-permute-start | bytes 393224 | tf_op jit(solution)/shard_map/ppermute | solution.py:169
  46.2 2.0 %copy.36.refs_2_ = f32[4096,2]{1,0:T(8,128)} copy(f32[4096,2]{0,1:T(2,128)S(1)} %get-tuple-element.116) | data formatting | bytes 65536 | tf_op jit(solution)/shard_map/stack | solution.py:396
  48.2 2.3 %pad_maximum_fusion.1 = bf16[256,2048]{1,0:T(8,128)(2,1)} fusion(bf16[128,2048]{1,0:T(8,128)(2,1)S(1)} %copy-done.13, bf16[128,2048]{1,0:T(8,128)(2,1)} %collective-permute-done.4.refs_24_.refs_30_), kind=kLoop, calls=%fused_computation.1 | loop fusion | flops 2097152 | bytes 2097152 | tf_op jit(solution)/shard_map/concatenate | solution.py:331
  50.5 17.8 %collective-permute-done.9.refs_30_.refs_36_ = bf16[128,2048]{1,0:T(8,128)(2,1)S(1)} collective-permute-done((bf16[128,2048]{1,0:T(8,128)(2,1)}, bf16[128,2048]{1,0:T(8,128)(2,1)S(1)}, u32[]{:S(2)}, u32[]{:S(2)}) %collective-permute-start.9) | collective-permute-done | bytes 524320 | tf_op jit(solution)/shard_map/ppermute | solution.py:284
  68.4 1.6 fusion.13
  75.2 11.6 %convolve.1.refs_1_.refs_2_.refs_3_.refs_4_.refs_5_.refs_6_.refs_7_.refs_8_.refs_9_.refs_10_.refs_11_.refs_12_.refs_13_.refs_14_.refs_15_.refs_16_.refs_17_.refs_18_.refs_19_.refs_20_ = bf16[32,384,128]{2,1,0:T(8,128)(2,1)S(1)} custom-call(bf16[384,4096]{1,0:T(8,128)(2,1)} %copy-done.6, bf16[384,4096]{1,0:T(8,128)(2,1)} %bitcast.14, ...), custom_call_target="tpu_custom_call" | custom-call | flops 17716740096 | bytes 9437184 | tf_op jit(solution)/shard_map/convolve/pallas_call | solution.py:148
  86.8 8.2 %collective-permute-done.20.refs_37_.refs_43_ = bf16[128,2048]{1,0:T(8,128)(2,1)S(1)} collective-permute-done((bf16[128,2048]{1,0:T(8,128)(2,1)S(1)}, bf16[128,2048]{1,0:T(8,128)(2,1)S(1)}, u32[]{:S(2)}, u32[]{:S(2)}) %collective-permute-start.20) | collective-permute-done | bytes 524320 | tf_op jit(solution)/shard_map/ppermute | solution.py:284
  96.7 2.5 %collective-permute-start.25 = (bf16[32,384,128]{2,1,0:T(8,128)(2,1)S(1)}, bf16[32,384,128]{2,1,0:T(8,128)(2,1)}, u32[]{:S(2)}, u32[]{:S(2)}) collective-permute-start(bf16[32,384,128]{2,1,0:T(8,128)(2,1)S(1)} %convolve.1.refs_1_.refs_2_.refs_3_.refs_4_.refs_5_.refs_6_.refs_7_.refs_8_.refs_9_.refs_10_.refs_11, ...), channel_id=1, source_target_pairs={{0,1},{1,0},{2,3},{3,2},{4,5},{5,4},{6,7},{7,6},{8,9},{9,8},{10,11... | collective-permute-start | bytes 9437192 | tf_op jit(solution)/shard_map/ppermute | solution.py:284
  101.5 9.0 %project.5.refs_10_ = f32[384,2048]{1,0:T(8,128)S(1)} custom-call(s32[20]{0:T(128)S(1)} %fusion.5.refs_0_, bf16[32,384,128]{2,1,0:T(8,128)(2,1)} %copy-done, bf16[32,384,128]{2,1,0:T(8,128)(2,1)} %copy-done, bf16[32,384,128]{2,1,0:T(8,128)(2,1)} %copy-done, bf16[32,384,128]{2,1,0:T(8,128)(2,1)} %copy-done, bf16[32,384,128]{2,1,0:T(8,128)(2,1)} %copy-done, ...), custom_call_target="tpu_custom_call" | custom-call | flops 16106127360 | bytes 3145728 | tf_op jit(solution)/shard_map/project/pallas_call | solution.py:244
  110.5 1.7 %copy-done.1 = f32[384,2048]{1,0:T(8,128)} copy-done((f32[384,2048]{1,0:T(8,128)}, f32[384,2048]{1,0:T(8,128)S(1)}, u32[]{:S(2)}) %copy-start.1) | copy-done | bytes 3145752
  112.2 14.0 %collective-permute-done.24.refs_9_.refs_47_ = bf16[256,2048]{1,0:T(8,128)(2,1)S(1)} collective-permute-done((bf16[256,2048]{1,0:T(8,128)(2,1)}, bf16[256,2048]{1,0:T(8,128)(2,1)S(1)}, u32[]{:S(2)}, u32[]{:S(2)}) %collective-permute-start.24) | collective-permute-done | bytes 1048608 | tf_op jit(solution)/shard_map/ppermute | solution.py:287
  129.3 10.7 %project.7.refs_12_ = f32[384,2048]{1,0:T(8,128)S(1)} custom-call(s32[26]{0:T(128)S(1)} %fusion.11.refs_0_, ...), custom_call_target="tpu_custom_call" | custom-call | flops 20937965568 | bytes 3145728 | tf_op jit(solution)/shard_map/project/pallas_call | solution.py:244
  140.1 1.7 copy-done.2
  141.7 4.6 %project.6.refs_12_ = f32[384,2048]{1,0:T(8,128)S(1)} custom-call(s32[6]{0:T(128)S(1)} %fusion.8.refs_0_, bf16[32,384,128]{2,1,0:T(8,128)(2,1)} %copy-done, bf16[32,384,128]{2,1,0:T(8,128)(2,1)} %copy-done, bf16[32,384,128]{2,1,0:T(8,128)(2,1)} %copy-done, bf16[32,384,128]{2,1,0:T(8,128)(2,1)} %copy-done, bf16[32,384,128]{2,1,0:T(8,128)(2,1)} %copy-done, ...), custom_call_target="tpu_custom_call" | custom-call | flops 4831838208 | bytes 3145728 | tf_op jit(solution)/shard_map/project/pallas_call | solution.py:244
  146.3 1.7 %copy-done.3 = f32[384,2048]{1,0:T(8,128)} copy-done((f32[384,2048]{1,0:T(8,128)}, f32[384,2048]{1,0:T(8,128)S(1)}, u32[]{:S(2)}) %copy-start.3) | copy-done | bytes 3145752
  148.1 2.8 %collective-permute-done.26.refs_7_ = bf16[128,2048]{1,0:T(8,128)(2,1)S(1)} collective-permute-done((bf16[128,2048]{1,0:T(8,128)(2,1)S(1)}, bf16[128,2048]{1,0:T(8,128)(2,1)S(1)}, u32[]{:S(2)}, u32[]{:S(2)}) %collective-permute-start.26) | collective-permute-done | bytes 524320 | tf_op jit(solution)/shard_map/ppermute | solution.py:284
  150.9 2.9 %collective-permute-done.30.refs_11_ = bf16[256,2048]{1,0:T(8,128)(2,1)S(1)} collective-permute-done((bf16[256,2048]{1,0:T(8,128)(2,1)S(1)}, bf16[256,2048]{1,0:T(8,128)(2,1)S(1)}, u32[]{:S(2)}, u32[]{:S(2)}) %collective-permute-start.30) | collective-permute-done | bytes 1048608 | tf_op jit(solution)/shard_map/ppermute | solution.py:287
  154.8 4.5 %project.8 = bf16[384,2048]{1,0:T(8,128)(2,1)S(1)} custom-call(s32[6]{0:T(128)S(1)} %fusion.2.refs_0_, ...), custom_call_target="tpu_custom_call" | custom-call | flops 4831838208 | bytes 3145728 | tf_op jit(solution)/shard_map/project/pallas_call | solution.py:244
  159.3 2.9 %collective-permute-start.31 = (bf16[384,2048]{1,0:T(8,128)(2,1)S(1)}, bf16[384,2048]{1,0:T(8,128)(2,1)S(1)}, u32[]{:S(2)}, u32[]{:S(2)}) collective-permute-start(bf16[384,2048]{1,0:T(8,128)(2,1)S(1)} %project.8), channel_id=1, source_target_pairs={{0,1},{1,0},{2,3},{3,2},{4,5},{5,4},{6,7},{7,6},{8,9},{9,8},{10,11... | collective-permute-start | bytes 4718600 | tf_op jit(solution)/shard_map/ppermute | solution.py:284
  162.3 5.3 %project.9.whole_ref = bf16[384,4096]{1,0:T(8,128)(2,1)} custom-call(s32[7]{0:T(128)S(1)} %pad_add_fusion.refs_0_, bf16[32,384,128]{2,1,0:T(8,128)(2,1)} %copy-done, bf16[32,384,128]{2,1,0:T(8,128)(2,1)} %copy-done, bf16[32,384,128]{2,1,0:T(8,128)(2,1)} %copy-done, bf16[32,384,128]{2,1,0:T(8,128)(2,1)} %copy-done, bf16[32,384,128]{2,1,0:T(8,128)(2,1)} %copy-done, ...), custom_call_target="tpu_custom_call" | custom-call | flops 4831838208 | bytes 3145728 | tf_op jit(solution)/shard_map/project/pallas_call | solution.py:244
  167.6 1.8 %put.1 = bf16[384,4096]{1,0:T(8,128)(2,1)} custom-call(s32[1]{0:T(128)} %bitcast.side_ref, bf16[384,2048]{1,0:T(8,128)(2,1)S(1)} %collective-permute-done.31.half_ref, bf16[384,4096]{1,0:T(8,128)(2,1)} %project.9.whole_ref), custom_call_target="tpu_custom_call", output_to_operand_aliasing={{}: (2, {})} | custom-call | tf_op jit(solution)/shard_map/put/pallas_call | solution.py:380
  (150 shorter events, 29.8 us)
Async XLA Ops:
  2.1 16.4 %collective-permute-start.2 = (bf16[128,2048]{1,0:T(8,128)(2,1)S(1)}, bf16[128,2048]{1,0:T(8,128)(2,1)}, u32[]{:S(2)}, u32[]{:S(2)}) collective-permute-start(bf16[128,2048]{1,0:T(8,128)(2,1)S(1)} %get-tuple-element.114.refs_21_.refs_27_), channel_id=1, source_target_pairs={{0,8},{1,9},{2,10},{3,11},{4,12},{5,13},{6,14},{7,15},{8,16},{9,17... | collective-permute-start | bytes 1572872 | tf_op jit(solution)/shard_map/ppermute | solution.py:287
  4.2 14.3 %collective-permute-start.1 = (bf16[128,2048]{1,0:T(8,128)(2,1)S(1)}, bf16[128,2048]{1,0:T(8,128)(2,1)S(1)}, u32[]{:S(2)}, u32[]{:S(2)}) collective-permute-start(bf16[128,2048]{1,0:T(8,128)(2,1)S(1)} %get-tuple-element.114.refs_21_.refs_27_), channel_id=1, source_target_pairs={{0,4},{1,5},{2,6},{3,7},{4,0},{5,1},{6,2},{7,3},{8,12},{9,13},{10,... | collective-permute-start | bytes 1572872 | tf_op jit(solution)/shard_map/ppermute | solution.py:284
  5.5 13.1 %collective-permute-start = (bf16[128,2048]{1,0:T(8,128)(2,1)S(1)}, bf16[128,2048]{1,0:T(8,128)(2,1)}, u32[]{:S(2)}, u32[]{:S(2)}) collective-permute-start(bf16[128,2048]{1,0:T(8,128)(2,1)S(1)} %get-tuple-element.114.refs_21_.refs_27_), channel_id=1, source_target_pairs={{0,2},{1,3},{2,0},{3,1},{4,6},{5,7},{6,4},{7,5},{8,10},{9,11},{10,... | collective-permute-start | bytes 1572872 | tf_op jit(solution)/shard_map/ppermute | solution.py:284
  6.7 11.8 %collective-permute-start.3 = (bf16[128,2048]{1,0:T(8,128)(2,1)}, bf16[128,2048]{1,0:T(8,128)(2,1)}, u32[]{:S(2)}, u32[]{:S(2)}) collective-permute-start(bf16[128,2048]{1,0:T(8,128)(2,1)} %get-tuple-element.113), channel_id=1, source_target_pairs={{0,1},{1,0},{2,3},{3,2},{4,5},{5,4},{6,7},{7,6},{8,9},{9,8},{10,11... | collective-permute-start | bytes 1572872 | tf_op jit(solution)/shard_map/ppermute | solution.py:284
  18.6 14.2 %collective-permute-start.6 = (bf16[128,2048]{1,0:T(8,128)(2,1)}, bf16[128,2048]{1,0:T(8,128)(2,1)S(1)}, u32[]{:S(2)}, u32[]{:S(2)}) collective-permute-start(bf16[128,2048]{1,0:T(8,128)(2,1)} %collective-permute-done.3.refs_22_.refs_28_), channel_id=1, source_target_pairs={{0,8},{1,9},{2,10},{3,11},{4,12},{5,13},{6,14},{7,15},{8,16},{9,17... | collective-permute-start | bytes 1572872 | tf_op jit(solution)/shard_map/ppermute | solution.py:287
  19.9 12.8 %collective-permute-start.5 = (bf16[128,2048]{1,0:T(8,128)(2,1)}, bf16[128,2048]{1,0:T(8,128)(2,1)}, u32[]{:S(2)}, u32[]{:S(2)}) collective-permute-start(bf16[128,2048]{1,0:T(8,128)(2,1)} %collective-permute-done.3.refs_22_.refs_28_), channel_id=1, source_target_pairs={{0,4},{1,5},{2,6},{3,7},{4,0},{5,1},{6,2},{7,3},{8,12},{9,13},{10,... | collective-permute-start | bytes 1572872 | tf_op jit(solution)/shard_map/ppermute | solution.py:284
  20.1 12.6 %collective-permute-start.4 = (bf16[128,2048]{1,0:T(8,128)(2,1)}, bf16[128,2048]{1,0:T(8,128)(2,1)}, u32[]{:S(2)}, u32[]{:S(2)}) collective-permute-start(bf16[128,2048]{1,0:T(8,128)(2,1)} %collective-permute-done.3.refs_22_.refs_28_), channel_id=1, source_target_pairs={{0,2},{1,3},{2,0},{3,1},{4,6},{5,7},{6,4},{7,5},{8,10},{9,11},{10,... | collective-permute-start | bytes 1572872 | tf_op jit(solution)/shard_map/ppermute | solution.py:284
  20.6 7.7 %collective-permute-start.7 = (f32[16,4096]{1,0:T(8,128)S(1)}, f32[16,4096]{1,0:T(8,128)}, u32[]{:S(2)}, u32[]{:S(2)}) collective-permute-start(f32[16,4096]{1,0:T(8,128)S(1)} %get-tuple-element.62), channel_id=1, source_target_pairs={{0,1},{1,0},{2,3},{3,2},{4,5},{5,4},{6,7},{7,6},{8,9},{9,8},{10,11... | collective-permute-start | bytes 786440 | tf_op jit(solution)/shard_map/ppermute | solution.py:169
  32.7 5.4 %collective-permute-start.15 = (f32[16,2048]{1,0:T(8,128)S(1)}, f32[16,2048]{1,0:T(8,128)S(1)}, u32[]{:S(2)}, u32[]{:S(2)}) collective-permute-start(f32[16,2048]{1,0:T(8,128)S(1)} %add_select_fusion.1), channel_id=1, source_target_pairs={{0,6},{1,7},{2,4},{3,5},{4,2},{5,3},{6,0},{7,1},{8,14},{9,15},{10,... | collective-permute-start | bytes 393224 | tf_op jit(solution)/shard_map/ppermute | solution.py:169
  34.0 5.3 %collective-permute-start.14 = (f32[16,2048]{1,0:T(8,128)S(1)}, f32[16,2048]{1,0:T(8,128)S(1)}, u32[]{:S(2)}, u32[]{:S(2)}) collective-permute-start(f32[16,2048]{1,0:T(8,128)S(1)} %add_select_fusion.1), channel_id=1, source_target_pairs={{0,4},{1,5},{2,6},{3,7},{4,0},{5,1},{6,2},{7,3},{8,12},{9,13},{10,... | collective-permute-start | bytes 393224 | tf_op jit(solution)/shard_map/ppermute | solution.py:169
  34.0 5.3 %collective-permute-start.13 = (f32[16,2048]{1,0:T(8,128)S(1)}, f32[16,2048]{1,0:T(8,128)S(1)}, u32[]{:S(2)}, u32[]{:S(2)}) collective-permute-start(f32[16,2048]{1,0:T(8,128)S(1)} %add_select_fusion.1), channel_id=1, source_target_pairs={{0,2},{1,3},{2,0},{3,1},{4,6},{5,7},{6,4},{7,5},{8,10},{9,11},{10,... | collective-permute-start | bytes 393224 | tf_op jit(solution)/shard_map/ppermute | solution.py:169
  37.6 30.8 %collective-permute-start.12 = (bf16[256,2048]{1,0:T(8,128)(2,1)}, bf16[256,2048]{1,0:T(8,128)(2,1)}, u32[]{:S(2)}, u32[]{:S(2)}) collective-permute-start(bf16[256,2048]{1,0:T(8,128)(2,1)} %pad_maximum_fusion), channel_id=1, source_target_pairs={{0,8},{1,9},{2,10},{3,11},{4,12},{5,13},{6,14},{7,15},{8,16},{9,17... | collective-permute-start | bytes 3145736 | tf_op jit(solution)/shard_map/ppermute | solution.py:287
  39.4 6.0 %collective-permute-start.16 = (f32[16,2048]{1,0:T(8,128)S(1)}, f32[16,2048]{1,0:T(8,128)S(1)}, u32[]{:S(2)}, u32[]{:S(2)}) collective-permute-start(f32[16,2048]{1,0:T(8,128)S(1)} %select_add_fusion), channel_id=1, source_target_pairs={{0,1},{1,0},{2,3},{3,2},{4,5},{5,4},{6,7},{7,6},{8,9},{9,8},{10,11... | collective-permute-start | bytes 393224 | tf_op jit(solution)/shard_map/ppermute | solution.py:169
  43.1 25.2 %collective-permute-start.10 = (bf16[128,2048]{1,0:T(8,128)(2,1)}, bf16[128,2048]{1,0:T(8,128)(2,1)}, u32[]{:S(2)}, u32[]{:S(2)}) collective-permute-start(bf16[128,2048]{1,0:T(8,128)(2,1)} %collective-permute-done.2.refs_27_.refs_33_), channel_id=1, source_target_pairs={{0,2},{1,3},{2,0},{3,1},{4,6},{5,7},{6,4},{7,5},{8,10},{9,11},{10,... | collective-permute-start | bytes 1572872 | tf_op jit(solution)/shard_map/ppermute | solution.py:284
  43.9 24.5 %collective-permute-start.11 = (bf16[128,2048]{1,0:T(8,128)(2,1)S(1)}, bf16[128,2048]{1,0:T(8,128)(2,1)}, u32[]{:S(2)}, u32[]{:S(2)}) collective-permute-start(bf16[128,2048]{1,0:T(8,128)(2,1)S(1)} %collective-permute-done.6.refs_28_.refs_34_), channel_id=1, source_target_pairs={{0,4},{1,5},{2,6},{3,7},{4,0},{5,1},{6,2},{7,3},{8,12},{9,13},{10,... | collective-permute-start | bytes 1572872 | tf_op jit(solution)/shard_map/ppermute | solution.py:284
  44.9 23.5 %collective-permute-start.9 = (bf16[128,2048]{1,0:T(8,128)(2,1)}, bf16[128,2048]{1,0:T(8,128)(2,1)S(1)}, u32[]{:S(2)}, u32[]{:S(2)}) collective-permute-start(bf16[128,2048]{1,0:T(8,128)(2,1)} %collective-permute-done.refs_23_.refs_29_), channel_id=1, source_target_pairs={{0,4},{1,5},{2,6},{3,7},{4,0},{5,1},{6,2},{7,3},{8,12},{9,13},{10,... | collective-permute-start | bytes 1572872 | tf_op jit(solution)/shard_map/ppermute | solution.py:284
  45.3 23.0 %collective-permute-start.8 = (bf16[128,2048]{1,0:T(8,128)(2,1)}, bf16[128,2048]{1,0:T(8,128)(2,1)S(1)}, u32[]{:S(2)}, u32[]{:S(2)}) collective-permute-start(bf16[128,2048]{1,0:T(8,128)(2,1)} %collective-permute-done.5.refs_26_.refs_32_), channel_id=1, source_target_pairs={{0,2},{1,3},{2,0},{3,1},{4,6},{5,7},{6,4},{7,5},{8,10},{9,11},{10,... | collective-permute-start | bytes 1572872 | tf_op jit(solution)/shard_map/ppermute | solution.py:284
  70.0 25.9 %collective-permute-start.21 = (bf16[256,2048]{1,0:T(8,128)(2,1)}, bf16[256,2048]{1,0:T(8,128)(2,1)}, u32[]{:S(2)}, u32[]{:S(2)}) collective-permute-start(bf16[256,2048]{1,0:T(8,128)(2,1)} %collective-permute-done.12.refs_33_.refs_39_), channel_id=1, source_target_pairs={{0,8},{1,9},{2,10},{3,11},{4,12},{5,13},{6,14},{7,15},{8,16},{9,17... | collective-permute-start | bytes 3145736 | tf_op jit(solution)/shard_map/ppermute | solution.py:287
  71.1 15.7 %collective-permute-start.17 = (bf16[128,2048]{1,0:T(8,128)(2,1)}, bf16[128,2048]{1,0:T(8,128)(2,1)S(1)}, u32[]{:S(2)}, u32[]{:S(2)}) collective-permute-start(bf16[128,2048]{1,0:T(8,128)(2,1)} %collective-permute-done.11.refs_32_.refs_38_), channel_id=1, source_target_pairs={{0,2},{1,3},{2,0},{3,1},{4,6},{5,7},{6,4},{7,5},{8,10},{9,11},{10,... | collective-permute-start | bytes 1572872 | tf_op jit(solution)/shard_map/ppermute | solution.py:284
  71.8 15.1 %collective-permute-start.18 = (bf16[128,2048]{1,0:T(8,128)(2,1)}, bf16[128,2048]{1,0:T(8,128)(2,1)S(1)}, u32[]{:S(2)}, u32[]{:S(2)}) collective-permute-start(bf16[128,2048]{1,0:T(8,128)(2,1)} %collective-permute-done.10.refs_31_.refs_37_), channel_id=1, source_target_pairs={{0,4},{1,5},{2,6},{3,7},{4,0},{5,1},{6,2},{7,3},{8,12},{9,13},{10,... | collective-permute-start | bytes 1572872 | tf_op jit(solution)/shard_map/ppermute | solution.py:284
  72.7 22.4 %collective-permute-start.20 = (bf16[128,2048]{1,0:T(8,128)(2,1)S(1)}, bf16[128,2048]{1,0:T(8,128)(2,1)S(1)}, u32[]{:S(2)}, u32[]{:S(2)}) collective-permute-start(bf16[128,2048]{1,0:T(8,128)(2,1)S(1)} %get-tuple-element.111), channel_id=1, source_target_pairs={{0,4},{1,5},{2,6},{3,7},{4,0},{5,1},{6,2},{7,3},{8,12},{9,13},{10,... | collective-permute-start | bytes 1572872 | tf_op jit(solution)/shard_map/ppermute | solution.py:284
  73.2 21.8 %collective-permute-start.19 = (bf16[128,2048]{1,0:T(8,128)(2,1)S(1)}, bf16[128,2048]{1,0:T(8,128)(2,1)S(1)}, u32[]{:S(2)}, u32[]{:S(2)}) collective-permute-start(bf16[128,2048]{1,0:T(8,128)(2,1)S(1)} %get-tuple-element.112), channel_id=1, source_target_pairs={{0,2},{1,3},{2,0},{3,1},{4,6},{5,7},{6,4},{7,5},{8,10},{9,11},{10,... | collective-permute-start | bytes 1572872 | tf_op jit(solution)/shard_map/ppermute | solution.py:284
  96.7 29.5 %collective-permute-start.25 = (bf16[32,384,128]{2,1,0:T(8,128)(2,1)S(1)}, bf16[32,384,128]{2,1,0:T(8,128)(2,1)}, u32[]{:S(2)}, u32[]{:S(2)}) collective-permute-start(bf16[32,384,128]{2,1,0:T(8,128)(2,1)S(1)} %convolve.1.refs_1_.refs_2_.refs_3_.refs_4_.refs_5_.refs_6_.refs_7_.refs_8_.refs_9_.refs_10_.refs_11, ...), channel_id=1, source_target_pairs={{0,1},{1,0},{2,3},{3,2},{4,5},{5,4},{6,7},{7,6},{8,9},{9,8},{10,11... | collective-permute-start | bytes 9437192 | tf_op jit(solution)/shard_map/ppermute | solution.py:284
  99.3 26.8 %collective-permute-start.24 = (bf16[256,2048]{1,0:T(8,128)(2,1)}, bf16[256,2048]{1,0:T(8,128)(2,1)S(1)}, u32[]{:S(2)}, u32[]{:S(2)}) collective-permute-start(bf16[256,2048]{1,0:T(8,128)(2,1)} %pad_maximum_fusion.1), channel_id=1, source_target_pairs={{0,8},{1,9},{2,10},{3,11},{4,12},{5,13},{6,14},{7,15},{8,16},{9,17... | collective-permute-start | bytes 3145736 | tf_op jit(solution)/shard_map/ppermute | solution.py:287
  99.5 26.6 %collective-permute-start.23 = (bf16[256,2048]{1,0:T(8,128)(2,1)}, bf16[256,2048]{1,0:T(8,128)(2,1)S(1)}, u32[]{:S(2)}, u32[]{:S(2)}) collective-permute-start(bf16[256,2048]{1,0:T(8,128)(2,1)} %collective-permute-done.21.refs_38_.refs_44_), channel_id=1, source_target_pairs={{0,4},{1,5},{2,6},{3,7},{4,0},{5,1},{6,2},{7,3},{8,12},{9,13},{10,... | collective-permute-start | bytes 3145736 | tf_op jit(solution)/shard_map/ppermute | solution.py:284
  100.6 25.6 %collective-permute-start.22 = (bf16[256,2048]{1,0:T(8,128)(2,1)}, bf16[256,2048]{1,0:T(8,128)(2,1)S(1)}, u32[]{:S(2)}, u32[]{:S(2)}) collective-permute-start(bf16[256,2048]{1,0:T(8,128)(2,1)} %collective-permute-done.21.refs_38_.refs_44_), channel_id=1, source_target_pairs={{0,2},{1,3},{2,0},{3,1},{4,6},{5,7},{6,4},{7,5},{8,10},{9,11},{10,... | collective-permute-start | bytes 3145736 | tf_op jit(solution)/shard_map/ppermute | solution.py:284
  126.3 21.8 %collective-permute-start.29 = (bf16[128,2048]{1,0:T(8,128)(2,1)S(1)}, bf16[128,2048]{1,0:T(8,128)(2,1)S(1)}, u32[]{:S(2)}, u32[]{:S(2)}) collective-permute-start(bf16[128,2048]{1,0:T(8,128)(2,1)S(1)} %slice.15), channel_id=1, source_target_pairs={{0,4},{1,5},{2,6},{3,7},{4,0},{5,1},{6,2},{7,3},{8,12},{9,13},{10,... | collective-permute-start | bytes 1572872 | tf_op jit(solution)/shard_map/ppermute | solution.py:284
  127.3 20.8 %collective-permute-start.28 = (bf16[128,2048]{1,0:T(8,128)(2,1)S(1)}, bf16[128,2048]{1,0:T(8,128)(2,1)S(1)}, u32[]{:S(2)}, u32[]{:S(2)}) collective-permute-start(bf16[128,2048]{1,0:T(8,128)(2,1)S(1)} %slice.14), channel_id=1, source_target_pairs={{0,2},{1,3},{2,0},{3,1},{4,6},{5,7},{6,4},{7,5},{8,10},{9,11},{10,... | collective-permute-start | bytes 1572872 | tf_op jit(solution)/shard_map/ppermute | solution.py:284
  128.4 22.5 %collective-permute-start.26 = (bf16[128,2048]{1,0:T(8,128)(2,1)S(1)}, bf16[128,2048]{1,0:T(8,128)(2,1)S(1)}, u32[]{:S(2)}, u32[]{:S(2)}) collective-permute-start(bf16[128,2048]{1,0:T(8,128)(2,1)S(1)} %copy-done.21), channel_id=1, source_target_pairs={{0,2},{1,3},{2,0},{3,1},{4,6},{5,7},{6,4},{7,5},{8,10},{9,11},{10,... | collective-permute-start | bytes 1572872 | tf_op jit(solution)/shard_map/ppermute | solution.py:284
  128.8 22.1 %collective-permute-start.27 = (bf16[128,2048]{1,0:T(8,128)(2,1)S(1)}, bf16[128,2048]{1,0:T(8,128)(2,1)S(1)}, u32[]{:S(2)}, u32[]{:S(2)}) collective-permute-start(bf16[128,2048]{1,0:T(8,128)(2,1)S(1)} %copy-done.23), channel_id=1, source_target_pairs={{0,4},{1,5},{2,6},{3,7},{4,0},{5,1},{6,2},{7,3},{8,12},{9,13},{10,... | collective-permute-start | bytes 1572872 | tf_op jit(solution)/shard_map/ppermute | solution.py:284
  129.3 24.5 %collective-permute-start.30 = (bf16[256,2048]{1,0:T(8,128)(2,1)S(1)}, bf16[256,2048]{1,0:T(8,128)(2,1)S(1)}, u32[]{:S(2)}, u32[]{:S(2)}) collective-permute-start(bf16[256,2048]{1,0:T(8,128)(2,1)S(1)} %collective-permute-done.24.refs_9_.refs_47_), channel_id=1, source_target_pairs={{0,8},{1,9},{2,10},{3,11},{4,12},{5,13},{6,14},{7,15},{8,16},{9,17... | collective-permute-start | bytes 3145736 | tf_op jit(solution)/shard_map/ppermute | solution.py:287
  159.3 8.3 %collective-permute-start.31 = (bf16[384,2048]{1,0:T(8,128)(2,1)S(1)}, bf16[384,2048]{1,0:T(8,128)(2,1)S(1)}, u32[]{:S(2)}, u32[]{:S(2)}) collective-permute-start(bf16[384,2048]{1,0:T(8,128)(2,1)S(1)} %project.8), channel_id=1, source_target_pairs={{0,1},{1,0},{2,3},{3,2},{4,5},{5,4},{6,7},{7,6},{8,9},{9,8},{10,11... | collective-permute-start | bytes 4718600 | tf_op jit(solution)/shard_map/ppermute | solution.py:284
  (40 other events, 535.3 us)

commit v3 on v2

--- a/solution.py
+++ b/solution.py
@@ -129,7 +129,7 @@
             pl.BlockSpec((poles, step), lambda i: (0, i)),
         ],
         out_shape=[
-            jax.ShapeDtypeStruct((rows, width), BF16),
+            pltpu.HBM((rows, width), BF16),
             jax.ShapeDtypeStruct((blocks * poles, width), F32),
             jax.ShapeDtypeStruct((poles, width), F32),
         ],
@@ -220,7 +220,7 @@
         o_ref[...] = total.astype(o_ref.dtype)
 
 
-def project(place, ring, gated, pieces, wide, total=None, side=None, dout=None, dtype=F32, cols=COLS):
+def project(place, ring, gated, pieces, wide, total=None, side=None, dout=None, dtype=F32, cols=COLS, free=0):
     shards, rows, depth = gated[0].shape
     steps = [one for _, _, owners in pieces for one in owners]
     sizes = [LANES * len(owners) for _, _, owners in pieces]
@@ -235,12 +235,12 @@
         pl.BlockSpec((size, cols), lambda b, i, at=at: (at, b)) for size, (_, at, _) in zip(sizes, pieces)
     ]
     operands = [g for g in gated for _ in steps] + [a for a, _, _ in pieces]
+    operands = [in_hbm(a) for a in operands[: len(operands) - free]] + operands[len(operands) - free :]
     if total is not None:
         specs += [block] * sides
         operands += list(total)
-    operands = [in_hbm(a) for a in operands]
     last = len(steps)
-    shape = jax.ShapeDtypeStruct((rows, wide if side is None else dout), dtype)
+    shape = jax.ShapeDtypeStruct((rows, wide), dtype) if side is None else pltpu.HBM((rows, dout), dtype)
     return pl.pallas_call(
         lambda *refs: project_kernel(sizes, sides, total is not None, *refs),
         grid_spec=pltpu.PrefetchScalarGridSpec(
@@ -351,43 +351,48 @@
         (ahead(aside), 0, [(1, 0, 1, 1), (1, 1, 0, 0)]),
     ]
     peer = swap(gated, 1)
-    (sum_own,) = project(place, ring, [gated], pieces, half)
+    (sum_own,) = project(place, ring, [gated], pieces, half, free=5)
     new, (gated, peer, sum_own, x_half, y_half) = settle(new, (gated, peer, sum_own, x_half, y_half))
     (x_whole, _, _), (y_whole, _, _), (aside, _, _) = new
+    (sum_own,) = project(place, ring, [gated], new, half, [sum_own], cols=2 * COLS, free=3)
+    over_x, over_y, sum_own = fence((y_whole, x_whole, sum_own))
+    over_x, over_y = over_x[depth:], over_y[:depth]
     late = [
         along_x(y_half, 2, 1, (1,)),
         along_y(x_half, 2, 1, (0,)),
-        along_x(y_whole[depth:], 3, 1, (1,)),
-        along_y(x_whole[:depth], 3, 1, (0,)),
+        along_x(over_x, 3, 1, (1,)),
+        along_y(over_y, 3, 1, (0,)),
         (ahead(aside), 0, [(2, 0, 1, 1), (2, 1, 0, 0)]),
     ]
-    (sum_own,) = project(place, ring, [gated], new, half, [sum_own], cols=2 * COLS)
-    (sum_peer,) = project(place, ring, [peer], pieces + new, half)
+    (sum_peer,) = project(place, ring, [peer], pieces + new, half, free=8)
     late, (gated, peer, sum_own, sum_peer) = settle(late, (gated, peer, sum_own, sum_peer))
-    (out_peer,) = project(place, ring, [peer], late, half, [sum_peer], dtype=BF16, cols=2 * COLS)
+    (out_peer,) = project(place, ring, [peer], late, half, [sum_peer], dtype=BF16, cols=2 * COLS, free=5)
     other = swap(out_peer, 1)
-    (out,) = project(place, ring, [gated], late, half, [sum_own], core, dout, dtype=BF16, cols=2 * COLS)
+    (out,) = project(place, ring, [gated], late, half, [sum_own], core, dout, dtype=BF16, cols=2 * COLS, free=5)
     return put(other, 1 - core, out).reshape(seqs, rows, dout)
 
 
-def put_kernel(side_ref, half_ref, whole_ref, o_ref):
-    o_ref[...] = half_ref[...]
+def put_kernel(side_ref, half_ref, whole_ref, o_ref, sem):
+    wide = half_ref.shape[1]
+    at = pl.multiple_of(side_ref[0] * wide, wide)
+    copy = pltpu.make_async_copy(half_ref, o_ref.at[:, pl.ds(at, wide)], sem)
+    copy.start()
+    copy.wait()
 
 
 def put(half, side, whole):
-    rows, wide = half.shape
-    nb = wide // COLS
     return pl.pallas_call(
         put_kernel,
-        grid_spec=pltpu.PrefetchScalarGridSpec(
-            num_scalar_prefetch=1,
-            grid=(nb,),
-            in_specs=[pl.BlockSpec((rows, COLS), lambda b, i: (0, b)), pl.BlockSpec(memory_space=pl.ANY)],
-            out_specs=pl.BlockSpec((rows, COLS), lambda b, i: (0, i[0] * nb + b)),
-        ),
-        out_shape=jax.ShapeDtypeStruct(whole.shape, whole.dtype),
+        in_specs=[
+            pl.BlockSpec(memory_space=pltpu.SMEM),
+            pl.BlockSpec(memory_space=pltpu.VMEM),
+            pl.BlockSpec(memory_space=pl.ANY),
+        ],
+        out_specs=pl.BlockSpec(memory_space=pl.ANY),
+        out_shape=pltpu.HBM(whole.shape, whole.dtype),
+        scratch_shapes=[pltpu.SemaphoreType.DMA(())],
         input_output_aliases={2: 0},
-        compiler_params=params(32),
+        compiler_params=pltpu.CompilerParams(vmem_limit_bytes=32 << 20),
         name="put",
     )(side.astype(jnp.int32)[None], half, whole)
 

time: 170 us -> 167 us (0.982)
  local copies, waits for them, and re-layouts: 22.9 us -> 19.3 us
  Pallas kernels: 52.6 us -> 55.2 us
  waiting for transfers between devices: 50.5 us -> 48.1 us
    unnamed x82 -> x66, local copies, waits for them, and re-layouts: 12 us -> 8.52 us
    ppermute x6, waiting for transfers between devices: 20.4 us -> 17.5 us  [ahead(): lax.ppermute(a, AXES, [(i, (i + 8) % devices) for i in range(devices)])]
  transfers between devices with their start and end apart: 32 -> 32, of which waited for: 7 -> 10; matrix products, arithmetic and copies ran while one was open for 10% -> 10% of each run, Pallas kernels for 27% -> 29%
where the time goes in v3:
time: 167 us
  Pallas kernels  55.2 us (33%)
  waiting for transfers between devices  48.1 us (29%)
  starting transfers between devices  35.8 us (21%)
  local copies, waits for them, and re-layouts  19.3 us (12%)
  other arithmetic  7.68 us (5%)
    pallas_call x5, Pallas kernels, project(): pl.pallas_call(lambda *refs: project_kernel(sizes, sides, total is not No...  35.1 us
    ppermute x21, waiting for transfers between devices, swap(): return lax.ppermute(a, AXES, [(i, i ^ bit) for i in range(devices)])  29.1 us
    ppermute x21, starting transfers between devices, swap(): return lax.ppermute(a, AXES, [(i, i ^ bit) for i in range(devices)])  20.9 us
    ppermute x6, waiting for transfers between devices, ahead(): lax.ppermute(a, AXES, [(i, (i + 8) % devices) for i in range(devices)])  17.5 us
    pallas_call x1, Pallas kernels, convolve(): pl.pallas_call(lambda *refs: conv_kernel(members, poles, blocks, *refs),...  11.6 us
    ppermute x5, starting transfers between devices, scan_send(): return lax.ppermute(total, 'ctx', [(i, i ^ width) for i in range(slabs)])  10.1 us
    unnamed x66, local copies, waits for them, and re-layouts  8.52 us
    pallas_call x1, Pallas kernels, states(): pl.pallas_call(lambda *refs: state_kernel(members, poles, blocks, *refs),...  5.88 us
  transfers between devices with their start and end apart: 32, of which 10 were waited for; matrix products, arithmetic and copies ran while one was open for 10% of the time, Pallas kernels for 29%

profile of v3, /device:TPU:1, one launch (start us, length us, event | category | flops | bytes accessed | tf_op | source)
XLA Modules:
  0.0 166.7 jit_solution(15746038995987143618)
XLA Ops:
  0.0 2.1 %constant_dynamic-slice_fusion.1 = (bf16[128,2048]{1,0:T(8,128)(2,1)}, bf16[128,2048]{1,0:T(8,128)(2,1)S(1)}) fusion(bf16[128,4096]{1,0:T(8,128)(2,1)} %param.23, s32[]{:T(128)S(6)} %select_n.105, s32[]{:T(128)S(6)} %select_n.104), kind=kLoop, calls=%fused_computation.22 | loop fusion | bytes 2097160 | tf_op jit(solution)/shard_map/dynamic_slice | solution.py:294
  2.1 2.1 %collective-permute-start.2 = (bf16[128,2048]{1,0:T(8,128)(2,1)S(1)}, bf16[128,2048]{1,0:T(8,128)(2,1)}, u32[]{:S(2)}, u32[]{:S(2)}) collective-permute-start(bf16[128,2048]{1,0:T(8,128)(2,1)S(1)} %get-tuple-element.120.refs_21_.refs_27_), channel_id=1, source_target_pairs={{0,8},{1,9},{2,10},{3,11},{4,12},{5,13},{6,14},{7,15},{8,16},{9,17... | collective-permute-start | bytes 1572872 | tf_op jit(solution)/shard_map/ppermute | solution.py:287
  4.2 1.2 collective-permute-start.1
  6.7 1.5 collective-permute-start.3
  10.8 5.9 %states.1 = (bf16[384,4096]{1,0:T(8,128)(2,1)}, f32[48,4096]{1,0:T(8,128)S(1)}, f32[16,4096]{1,0:T(8,128)S(1)}) custom-call(bf16[384,4096]{1,0:T(8,128)(2,1)} %bitcast.12, bf16[384,4096]{1,0:T(8,128)(2,1)} %bitcast.13, f32[4096,2]{1,0:T(8,128)S(1)} %copy.33.refs_2_), custom_call_target="tpu_custom_call" | custom-call | flops 6442450944 | bytes 9437184 | tf_op jit(solution)/shard_map/states/pallas_call | solution.py:118
  19.4 1.2 collective-permute-start.4
  20.6 2.9 %collective-permute-start.7 = (f32[16,4096]{1,0:T(8,128)S(1)}, f32[16,4096]{1,0:T(8,128)}, u32[]{:S(2)}, u32[]{:S(2)}) collective-permute-start(f32[16,4096]{1,0:T(8,128)S(1)} %get-tuple-element.65), channel_id=1, source_target_pairs={{0,1},{1,0},{2,3},{3,2},{4,5},{5,4},{6,7},{7,6},{8,9},{9,8},{10,11... | collective-permute-start | bytes 786440 | tf_op jit(solution)/shard_map/ppermute | solution.py:169
  24.1 2.3 %reshape.17 = f32[16,4096]{1,0:T(8,128)} reshape(f32[16,256,16]{2,1,0:T(8,128)S(1)} %broadcast_in_dim.19) | data formatting | bytes 524288 | tf_op jit(solution)/shard_map/reshape | solution.py:405
  29.2 2.4 %collective-permute-done.6.refs_28_.refs_34_ = bf16[128,2048]{1,0:T(8,128)(2,1)S(1)} collective-permute-done((bf16[128,2048]{1,0:T(8,128)(2,1)}, bf16[128,2048]{1,0:T(8,128)(2,1)S(1)}, u32[]{:S(2)}, u32[]{:S(2)}) %collective-permute-start.6) | collective-permute-done | bytes 524320 | tf_op jit(solution)/shard_map/ppermute | solution.py:287
  31.7 2.4 %collective-permute-start.15 = (f32[16,2048]{1,0:T(8,128)S(1)}, f32[16,2048]{1,0:T(8,128)S(1)}, u32[]{:S(2)}, u32[]{:S(2)}) collective-permute-start(f32[16,2048]{1,0:T(8,128)S(1)} %add_select_fusion.1), channel_id=1, source_target_pairs={{0,6},{1,7},{2,4},{3,5},{4,2},{5,3},{6,0},{7,1},{8,14},{9,15},{10,... | collective-permute-start | bytes 393224 | tf_op jit(solution)/shard_map/ppermute | solution.py:169
  34.4 2.2 %pad_maximum_fusion = bf16[256,2048]{1,0:T(8,128)(2,1)} fusion(bf16[128,2048]{1,0:T(8,128)(2,1)S(1)} %collective-permute-done.6.refs_28_.refs_34_, bf16[128,2048]{1,0:T(8,128)(2,1)} %collective-permute-done.2.refs_27_.refs_33_), kind=kLoop, calls=%fused_computation | loop fusion | flops 2097152 | bytes 2097152 | tf_op jit(solution)/shard_map/concatenate | solution.py:327
  36.6 1.3 collective-permute-done.14
  38.1 4.4 %collective-permute-start.16 = (f32[16,2048]{1,0:T(8,128)S(1)}, f32[16,2048]{1,0:T(8,128)S(1)}, u32[]{:S(2)}, u32[]{:S(2)}) collective-permute-start(f32[16,2048]{1,0:T(8,128)S(1)} %select_add_fusion), channel_id=1, source_target_pairs={{0,1},{1,0},{2,3},{3,2},{4,5},{5,4},{6,7},{7,6},{8,9},{9,8},{10,11... | collective-permute-start | bytes 393224 | tf_op jit(solution)/shard_map/ppermute | solution.py:169
  46.0 2.0 %copy.36.refs_2_ = f32[4096,2]{1,0:T(8,128)} copy(f32[4096,2]{0,1:T(2,128)S(1)} %get-tuple-element.122) | data formatting | bytes 65536 | tf_op jit(solution)/shard_map/stack | solution.py:401
  48.0 2.3 %pad_maximum_fusion.1 = bf16[256,2048]{1,0:T(8,128)(2,1)} fusion(bf16[128,2048]{1,0:T(8,128)(2,1)S(1)} %copy-done.17, bf16[128,2048]{1,0:T(8,128)(2,1)} %collective-permute-done.4.refs_24_.refs_30_), kind=kLoop, calls=%fused_computation.1 | loop fusion | flops 2097152 | bytes 2097152 | tf_op jit(solution)/shard_map/concatenate | solution.py:331
  50.3 17.6 %collective-permute-done.9.refs_30_.refs_36_ = bf16[128,2048]{1,0:T(8,128)(2,1)S(1)} collective-permute-done((bf16[128,2048]{1,0:T(8,128)(2,1)}, bf16[128,2048]{1,0:T(8,128)(2,1)S(1)}, u32[]{:S(2)}, u32[]{:S(2)}) %collective-permute-start.9) | collective-permute-done | bytes 524320 | tf_op jit(solution)/shard_map/ppermute | solution.py:284
  68.1 1.6 fusion.13
  69.6 1.3 collective-permute-start.21
  71.5 1.4 collective-permute-start.18
  75.0 11.6 %convolve.1.refs_1_.refs_2_.refs_3_.refs_4_.refs_5_.refs_6_.refs_7_.refs_8_.refs_9_.refs_10_.refs_11_.refs_12_.refs_13_.refs_14_.refs_15_.refs_16_.refs_17_.refs_18_.refs_19_.refs_20_ = bf16[32,384,128]{2,1,0:T(8,128)(2,1)S(1)} custom-call(bf16[384,4096]{1,0:T(8,128)(2,1)} %get-tuple-element.82.refs_0_, bf16[384,4096]{1,0:T(8,128)(2,1)} %bitcast.14, ...), custom_call_target="tpu_custom_call" | custom-call | flops 17716740096 | bytes 9437184 | tf_op jit(solution)/shard_map/convolve/pallas_call | solution.py:148
  88.6 6.2 %collective-permute-done.20.refs_37_.refs_43_ = bf16[128,2048]{1,0:T(8,128)(2,1)} collective-permute-done((bf16[128,2048]{1,0:T(8,128)(2,1)S(1)}, bf16[128,2048]{1,0:T(8,128)(2,1)}, u32[]{:S(2)}, u32[]{:S(2)}) %collective-permute-start.20) | collective-permute-done | bytes 524320 | tf_op jit(solution)/shard_map/ppermute | solution.py:284
  95.7 2.6 %collective-permute-start.25 = (bf16[32,384,128]{2,1,0:T(8,128)(2,1)S(1)}, bf16[32,384,128]{2,1,0:T(8,128)(2,1)}, u32[]{:S(2)}, u32[]{:S(2)}) collective-permute-start(bf16[32,384,128]{2,1,0:T(8,128)(2,1)S(1)} %convolve.1.refs_1_.refs_2_.refs_3_.refs_4_.refs_5_.refs_6_.refs_7_.refs_8_.refs_9_.refs_10_.refs_11, ...), channel_id=1, source_target_pairs={{0,1},{1,0},{2,3},{3,2},{4,5},{5,4},{6,7},{7,6},{8,9},{9,8},{10,11... | collective-permute-start | bytes 9437192 | tf_op jit(solution)/shard_map/ppermute | solution.py:284
  103.4 9.6 %project.5.refs_10_ = f32[384,2048]{1,0:T(8,128)} custom-call(s32[20]{0:T(128)S(1)} %fusion.5.refs_0_, bf16[32,384,128]{2,1,0:T(8,128)(2,1)} %copy-done, bf16[32,384,128]{2,1,0:T(8,128)(2,1)} %copy-done, bf16[32,384,128]{2,1,0:T(8,128)(2,1)} %copy-done, bf16[32,384,128]{2,1,0:T(8,128)(2,1)} %copy-done, bf16[32,384,128]{2,1,0:T(8,128)(2,1)} %copy-done, ...), custom_call_target="tpu_custom_call" | custom-call | flops 16106127360 | bytes 3145728 | tf_op jit(solution)/shard_map/project/pallas_call | solution.py:244
  113.0 12.2 %collective-permute-done.24.refs_9_.refs_47_ = bf16[256,2048]{1,0:T(8,128)(2,1)S(1)} collective-permute-done((bf16[256,2048]{1,0:T(8,128)(2,1)}, bf16[256,2048]{1,0:T(8,128)(2,1)S(1)}, u32[]{:S(2)}, u32[]{:S(2)}) %collective-permute-start.24) | collective-permute-done | bytes 1048608 | tf_op jit(solution)/shard_map/ppermute | solution.py:287
  127.1 5.0 %project.6.refs_12_ = f32[384,2048]{1,0:T(8,128)} custom-call(s32[6]{0:T(128)S(1)} %fusion.8.refs_0_, bf16[32,384,128]{2,1,0:T(8,128)(2,1)} %copy-done, bf16[32,384,128]{2,1,0:T(8,128)(2,1)} %copy-done, bf16[32,384,128]{2,1,0:T(8,128)(2,1)} %copy-done, bf16[32,384,128]{2,1,0:T(8,128)(2,1)} %copy-done, bf16[32,384,128]{2,1,0:T(8,128)(2,1)} %copy-done, ...), custom_call_target="tpu_custom_call" | custom-call | flops 4831838208 | bytes 3145728 | tf_op jit(solution)/shard_map/project/pallas_call | solution.py:244
  133.5 11.1 %project.7.refs_12_ = f32[384,2048]{1,0:T(8,128)} custom-call(s32[26]{0:T(128)S(1)} %fusion.11.refs_0_, ...), custom_call_target="tpu_custom_call" | custom-call | flops 20937965568 | bytes 3145728 | tf_op jit(solution)/shard_map/project/pallas_call | solution.py:244
  144.6 5.1 %collective-permute-done.29.refs_10_ = bf16[128,2048]{1,0:T(8,128)(2,1)S(1)} collective-permute-done((bf16[128,2048]{1,0:T(8,128)(2,1)S(1)}, bf16[128,2048]{1,0:T(8,128)(2,1)S(1)}, u32[]{:S(2)}, u32[]{:S(2)}) %collective-permute-start.29) | collective-permute-done | bytes 524320 | tf_op jit(solution)/shard_map/ppermute | solution.py:284
  149.8 2.4 %collective-permute-done.30.refs_11_ = bf16[256,2048]{1,0:T(8,128)(2,1)S(1)} collective-permute-done((bf16[256,2048]{1,0:T(8,128)(2,1)S(1)}, bf16[256,2048]{1,0:T(8,128)(2,1)S(1)}, u32[]{:S(2)}, u32[]{:S(2)}) %collective-permute-start.30) | collective-permute-done | bytes 1048608 | tf_op jit(solution)/shard_map/ppermute | solution.py:287
  152.2 4.7 %project.8 = bf16[384,2048]{1,0:T(8,128)(2,1)} custom-call(s32[6]{0:T(128)S(1)} %fusion.2.refs_0_, ...), custom_call_target="tpu_custom_call" | custom-call | flops 4831838208 | bytes 3145728 | tf_op jit(solution)/shard_map/project/pallas_call | solution.py:244
  156.9 2.3 %collective-permute-start.31 = (bf16[384,2048]{1,0:T(8,128)(2,1)}, bf16[384,2048]{1,0:T(8,128)(2,1)}, u32[]{:S(2)}, u32[]{:S(2)}) collective-permute-start(bf16[384,2048]{1,0:T(8,128)(2,1)} %project.8), channel_id=1, source_target_pairs={{0,1},{1,0},{2,3},{3,2},{4,5},{5,4},{6,7},{7,6},{8,9},{9,8},{10,11... | collective-permute-start | bytes 4718600 | tf_op jit(solution)/shard_map/ppermute | solution.py:284
  159.3 4.7 %project.9.whole_ref = bf16[384,4096]{1,0:T(8,128)(2,1)} custom-call(s32[7]{0:T(128)S(1)} %pad_add_fusion.refs_0_, bf16[32,384,128]{2,1,0:T(8,128)(2,1)} %copy-done, bf16[32,384,128]{2,1,0:T(8,128)(2,1)} %copy-done, bf16[32,384,128]{2,1,0:T(8,128)(2,1)} %copy-done, bf16[32,384,128]{2,1,0:T(8,128)(2,1)} %copy-done, bf16[32,384,128]{2,1,0:T(8,128)(2,1)} %copy-done, ...), custom_call_target="tpu_custom_call" | custom-call | flops 4831838208 | bytes 3145728 | tf_op jit(solution)/shard_map/project/pallas_call | solution.py:244
  164.0 2.6 %put.1 = bf16[384,4096]{1,0:T(8,128)(2,1)} custom-call(s32[1]{0:T(128)} %bitcast.side_ref, bf16[384,2048]{1,0:T(8,128)(2,1)} %collective-permute-done.31.half_ref, bf16[384,4096]{1,0:T(8,128)(2,1)} %project.9.whole_ref), custom_call_target="tpu_custom_call", output_to_operand_aliasing={{}: (2, {})} | custom-call | tf_op jit(solution)/shard_map/put/pallas_call | solution.py:384
  (134 shorter events, 27.9 us)
Async XLA Ops:
  2.1 15.9 %collective-permute-start.2 = (bf16[128,2048]{1,0:T(8,128)(2,1)S(1)}, bf16[128,2048]{1,0:T(8,128)(2,1)}, u32[]{:S(2)}, u32[]{:S(2)}) collective-permute-start(bf16[128,2048]{1,0:T(8,128)(2,1)S(1)} %get-tuple-element.120.refs_21_.refs_27_), channel_id=1, source_target_pairs={{0,8},{1,9},{2,10},{3,11},{4,12},{5,13},{6,14},{7,15},{8,16},{9,17... | collective-permute-start | bytes 1572872 | tf_op jit(solution)/shard_map/ppermute | solution.py:287
  4.2 13.8 %collective-permute-start.1 = (bf16[128,2048]{1,0:T(8,128)(2,1)S(1)}, bf16[128,2048]{1,0:T(8,128)(2,1)S(1)}, u32[]{:S(2)}, u32[]{:S(2)}) collective-permute-start(bf16[128,2048]{1,0:T(8,128)(2,1)S(1)} %get-tuple-element.120.refs_21_.refs_27_), channel_id=1, source_target_pairs={{0,4},{1,5},{2,6},{3,7},{4,0},{5,1},{6,2},{7,3},{8,12},{9,13},{10,... | collective-permute-start | bytes 1572872 | tf_op jit(solution)/shard_map/ppermute | solution.py:284
  5.5 12.5 %collective-permute-start = (bf16[128,2048]{1,0:T(8,128)(2,1)S(1)}, bf16[128,2048]{1,0:T(8,128)(2,1)}, u32[]{:S(2)}, u32[]{:S(2)}) collective-permute-start(bf16[128,2048]{1,0:T(8,128)(2,1)S(1)} %get-tuple-element.120.refs_21_.refs_27_), channel_id=1, source_target_pairs={{0,2},{1,3},{2,0},{3,1},{4,6},{5,7},{6,4},{7,5},{8,10},{9,11},{10,... | collective-permute-start | bytes 1572872 | tf_op jit(solution)/shard_map/ppermute | solution.py:284
  6.7 10.9 %collective-permute-start.3 = (bf16[128,2048]{1,0:T(8,128)(2,1)}, bf16[128,2048]{1,0:T(8,128)(2,1)}, u32[]{:S(2)}, u32[]{:S(2)}) collective-permute-start(bf16[128,2048]{1,0:T(8,128)(2,1)} %get-tuple-element.119), channel_id=1, source_target_pairs={{0,1},{1,0},{2,3},{3,2},{4,5},{5,4},{6,7},{7,6},{8,9},{9,8},{10,11... | collective-permute-start | bytes 1572872 | tf_op jit(solution)/shard_map/ppermute | solution.py:284
  18.0 13.6 %collective-permute-start.6 = (bf16[128,2048]{1,0:T(8,128)(2,1)}, bf16[128,2048]{1,0:T(8,128)(2,1)S(1)}, u32[]{:S(2)}, u32[]{:S(2)}) collective-permute-start(bf16[128,2048]{1,0:T(8,128)(2,1)} %collective-permute-done.3.refs_22_.refs_28_), channel_id=1, source_target_pairs={{0,8},{1,9},{2,10},{3,11},{4,12},{5,13},{6,14},{7,15},{8,16},{9,17... | collective-permute-start | bytes 1572872 | tf_op jit(solution)/shard_map/ppermute | solution.py:287
  19.0 12.6 %collective-permute-start.5 = (bf16[128,2048]{1,0:T(8,128)(2,1)}, bf16[128,2048]{1,0:T(8,128)(2,1)}, u32[]{:S(2)}, u32[]{:S(2)}) collective-permute-start(bf16[128,2048]{1,0:T(8,128)(2,1)} %collective-permute-done.3.refs_22_.refs_28_), channel_id=1, source_target_pairs={{0,4},{1,5},{2,6},{3,7},{4,0},{5,1},{6,2},{7,3},{8,12},{9,13},{10,... | collective-permute-start | bytes 1572872 | tf_op jit(solution)/shard_map/ppermute | solution.py:284
  19.4 12.3 %collective-permute-start.4 = (bf16[128,2048]{1,0:T(8,128)(2,1)}, bf16[128,2048]{1,0:T(8,128)(2,1)}, u32[]{:S(2)}, u32[]{:S(2)}) collective-permute-start(bf16[128,2048]{1,0:T(8,128)(2,1)} %collective-permute-done.3.refs_22_.refs_28_), channel_id=1, source_target_pairs={{0,2},{1,3},{2,0},{3,1},{4,6},{5,7},{6,4},{7,5},{8,10},{9,11},{10,... | collective-permute-start | bytes 1572872 | tf_op jit(solution)/shard_map/ppermute | solution.py:284
  20.6 7.7 %collective-permute-start.7 = (f32[16,4096]{1,0:T(8,128)S(1)}, f32[16,4096]{1,0:T(8,128)}, u32[]{:S(2)}, u32[]{:S(2)}) collective-permute-start(f32[16,4096]{1,0:T(8,128)S(1)} %get-tuple-element.65), channel_id=1, source_target_pairs={{0,1},{1,0},{2,3},{3,2},{4,5},{5,4},{6,7},{7,6},{8,9},{9,8},{10,11... | collective-permute-start | bytes 786440 | tf_op jit(solution)/shard_map/ppermute | solution.py:169
  31.7 4.9 %collective-permute-start.15 = (f32[16,2048]{1,0:T(8,128)S(1)}, f32[16,2048]{1,0:T(8,128)S(1)}, u32[]{:S(2)}, u32[]{:S(2)}) collective-permute-start(f32[16,2048]{1,0:T(8,128)S(1)} %add_select_fusion.1), channel_id=1, source_target_pairs={{0,6},{1,7},{2,4},{3,5},{4,2},{5,3},{6,0},{7,1},{8,14},{9,15},{10,... | collective-permute-start | bytes 393224 | tf_op jit(solution)/shard_map/ppermute | solution.py:169
  34.0 3.8 %collective-permute-start.14 = (f32[16,2048]{1,0:T(8,128)S(1)}, f32[16,2048]{1,0:T(8,128)S(1)}, u32[]{:S(2)}, u32[]{:S(2)}) collective-permute-start(f32[16,2048]{1,0:T(8,128)S(1)} %add_select_fusion.1), channel_id=1, source_target_pairs={{0,4},{1,5},{2,6},{3,7},{4,0},{5,1},{6,2},{7,3},{8,12},{9,13},{10,... | collective-permute-start | bytes 393224 | tf_op jit(solution)/shard_map/ppermute | solution.py:169
  34.0 4.0 %collective-permute-start.13 = (f32[16,2048]{1,0:T(8,128)S(1)}, f32[16,2048]{1,0:T(8,128)S(1)}, u32[]{:S(2)}, u32[]{:S(2)}) collective-permute-start(f32[16,2048]{1,0:T(8,128)S(1)} %add_select_fusion.1), channel_id=1, source_target_pairs={{0,2},{1,3},{2,0},{3,1},{4,6},{5,7},{6,4},{7,5},{8,10},{9,11},{10,... | collective-permute-start | bytes 393224 | tf_op jit(solution)/shard_map/ppermute | solution.py:169
  36.6 31.5 %collective-permute-start.12 = (bf16[256,2048]{1,0:T(8,128)(2,1)}, bf16[256,2048]{1,0:T(8,128)(2,1)}, u32[]{:S(2)}, u32[]{:S(2)}) collective-permute-start(bf16[256,2048]{1,0:T(8,128)(2,1)} %pad_maximum_fusion), channel_id=1, source_target_pairs={{0,8},{1,9},{2,10},{3,11},{4,12},{5,13},{6,14},{7,15},{8,16},{9,17... | collective-permute-start | bytes 3145736 | tf_op jit(solution)/shard_map/ppermute | solution.py:287
  38.1 6.8 %collective-permute-start.16 = (f32[16,2048]{1,0:T(8,128)S(1)}, f32[16,2048]{1,0:T(8,128)S(1)}, u32[]{:S(2)}, u32[]{:S(2)}) collective-permute-start(f32[16,2048]{1,0:T(8,128)S(1)} %select_add_fusion), channel_id=1, source_target_pairs={{0,1},{1,0},{2,3},{3,2},{4,5},{5,4},{6,7},{7,6},{8,9},{9,8},{10,11... | collective-permute-start | bytes 393224 | tf_op jit(solution)/shard_map/ppermute | solution.py:169
  43.0 25.0 %collective-permute-start.10 = (bf16[128,2048]{1,0:T(8,128)(2,1)}, bf16[128,2048]{1,0:T(8,128)(2,1)}, u32[]{:S(2)}, u32[]{:S(2)}) collective-permute-start(bf16[128,2048]{1,0:T(8,128)(2,1)} %collective-permute-done.2.refs_27_.refs_33_), channel_id=1, source_target_pairs={{0,2},{1,3},{2,0},{3,1},{4,6},{5,7},{6,4},{7,5},{8,10},{9,11},{10,... | collective-permute-start | bytes 1572872 | tf_op jit(solution)/shard_map/ppermute | solution.py:284
  43.5 24.6 %collective-permute-start.11 = (bf16[128,2048]{1,0:T(8,128)(2,1)S(1)}, bf16[128,2048]{1,0:T(8,128)(2,1)}, u32[]{:S(2)}, u32[]{:S(2)}) collective-permute-start(bf16[128,2048]{1,0:T(8,128)(2,1)S(1)} %collective-permute-done.6.refs_28_.refs_34_), channel_id=1, source_target_pairs={{0,4},{1,5},{2,6},{3,7},{4,0},{5,1},{6,2},{7,3},{8,12},{9,13},{10,... | collective-permute-start | bytes 1572872 | tf_op jit(solution)/shard_map/ppermute | solution.py:284
  44.6 23.4 %collective-permute-start.9 = (bf16[128,2048]{1,0:T(8,128)(2,1)}, bf16[128,2048]{1,0:T(8,128)(2,1)S(1)}, u32[]{:S(2)}, u32[]{:S(2)}) collective-permute-start(bf16[128,2048]{1,0:T(8,128)(2,1)} %collective-permute-done.refs_23_.refs_29_), channel_id=1, source_target_pairs={{0,4},{1,5},{2,6},{3,7},{4,0},{5,1},{6,2},{7,3},{8,12},{9,13},{10,... | collective-permute-start | bytes 1572872 | tf_op jit(solution)/shard_map/ppermute | solution.py:284
  45.0 23.1 %collective-permute-start.8 = (bf16[128,2048]{1,0:T(8,128)(2,1)}, bf16[128,2048]{1,0:T(8,128)(2,1)S(1)}, u32[]{:S(2)}, u32[]{:S(2)}) collective-permute-start(bf16[128,2048]{1,0:T(8,128)(2,1)} %collective-permute-done.5.refs_26_.refs_32_), channel_id=1, source_target_pairs={{0,2},{1,3},{2,0},{3,1},{4,6},{5,7},{6,4},{7,5},{8,10},{9,11},{10,... | collective-permute-start | bytes 1572872 | tf_op jit(solution)/shard_map/ppermute | solution.py:284
  69.6 26.1 %collective-permute-start.21 = (bf16[256,2048]{1,0:T(8,128)(2,1)}, bf16[256,2048]{1,0:T(8,128)(2,1)}, u32[]{:S(2)}, u32[]{:S(2)}) collective-permute-start(bf16[256,2048]{1,0:T(8,128)(2,1)} %collective-permute-done.12.refs_33_.refs_39_), channel_id=1, source_target_pairs={{0,8},{1,9},{2,10},{3,11},{4,12},{5,13},{6,14},{7,15},{8,16},{9,17... | collective-permute-start | bytes 3145736 | tf_op jit(solution)/shard_map/ppermute | solution.py:287
  70.9 15.7 %collective-permute-start.17 = (bf16[128,2048]{1,0:T(8,128)(2,1)}, bf16[128,2048]{1,0:T(8,128)(2,1)S(1)}, u32[]{:S(2)}, u32[]{:S(2)}) collective-permute-start(bf16[128,2048]{1,0:T(8,128)(2,1)} %collective-permute-done.11.refs_32_.refs_38_), channel_id=1, source_target_pairs={{0,2},{1,3},{2,0},{3,1},{4,6},{5,7},{6,4},{7,5},{8,10},{9,11},{10,... | collective-permute-start | bytes 1572872 | tf_op jit(solution)/shard_map/ppermute | solution.py:284
  71.5 15.9 %collective-permute-start.18 = (bf16[128,2048]{1,0:T(8,128)(2,1)}, bf16[128,2048]{1,0:T(8,128)(2,1)S(1)}, u32[]{:S(2)}, u32[]{:S(2)}) collective-permute-start(bf16[128,2048]{1,0:T(8,128)(2,1)} %collective-permute-done.10.refs_31_.refs_37_), channel_id=1, source_target_pairs={{0,4},{1,5},{2,6},{3,7},{4,0},{5,1},{6,2},{7,3},{8,12},{9,13},{10,... | collective-permute-start | bytes 1572872 | tf_op jit(solution)/shard_map/ppermute | solution.py:284
  73.0 21.9 %collective-permute-start.20 = (bf16[128,2048]{1,0:T(8,128)(2,1)S(1)}, bf16[128,2048]{1,0:T(8,128)(2,1)}, u32[]{:S(2)}, u32[]{:S(2)}) collective-permute-start(bf16[128,2048]{1,0:T(8,128)(2,1)S(1)} %get-tuple-element.117), channel_id=1, source_target_pairs={{0,4},{1,5},{2,6},{3,7},{4,0},{5,1},{6,2},{7,3},{8,12},{9,13},{10,... | collective-permute-start | bytes 1572872 | tf_op jit(solution)/shard_map/ppermute | solution.py:284
  73.0 21.8 %collective-permute-start.19 = (bf16[128,2048]{1,0:T(8,128)(2,1)S(1)}, bf16[128,2048]{1,0:T(8,128)(2,1)S(1)}, u32[]{:S(2)}, u32[]{:S(2)}) collective-permute-start(bf16[128,2048]{1,0:T(8,128)(2,1)S(1)} %get-tuple-element.118), channel_id=1, source_target_pairs={{0,2},{1,3},{2,0},{3,1},{4,6},{5,7},{6,4},{7,5},{8,10},{9,11},{10,... | collective-permute-start | bytes 1572872 | tf_op jit(solution)/shard_map/ppermute | solution.py:284
  95.7 29.6 %collective-permute-start.25 = (bf16[32,384,128]{2,1,0:T(8,128)(2,1)S(1)}, bf16[32,384,128]{2,1,0:T(8,128)(2,1)}, u32[]{:S(2)}, u32[]{:S(2)}) collective-permute-start(bf16[32,384,128]{2,1,0:T(8,128)(2,1)S(1)} %convolve.1.refs_1_.refs_2_.refs_3_.refs_4_.refs_5_.refs_6_.refs_7_.refs_8_.refs_9_.refs_10_.refs_11, ...), channel_id=1, source_target_pairs={{0,1},{1,0},{2,3},{3,2},{4,5},{5,4},{6,7},{7,6},{8,9},{9,8},{10,11... | collective-permute-start | bytes 9437192 | tf_op jit(solution)/shard_map/ppermute | solution.py:284
  98.4 26.8 %collective-permute-start.24 = (bf16[256,2048]{1,0:T(8,128)(2,1)}, bf16[256,2048]{1,0:T(8,128)(2,1)S(1)}, u32[]{:S(2)}, u32[]{:S(2)}) collective-permute-start(bf16[256,2048]{1,0:T(8,128)(2,1)} %pad_maximum_fusion.1), channel_id=1, source_target_pairs={{0,8},{1,9},{2,10},{3,11},{4,12},{5,13},{6,14},{7,15},{8,16},{9,17... | collective-permute-start | bytes 3145736 | tf_op jit(solution)/shard_map/ppermute | solution.py:287
  98.8 26.4 %collective-permute-start.23 = (bf16[256,2048]{1,0:T(8,128)(2,1)}, bf16[256,2048]{1,0:T(8,128)(2,1)S(1)}, u32[]{:S(2)}, u32[]{:S(2)}) collective-permute-start(bf16[256,2048]{1,0:T(8,128)(2,1)} %collective-permute-done.21.refs_38_.refs_44_), channel_id=1, source_target_pairs={{0,4},{1,5},{2,6},{3,7},{4,0},{5,1},{6,2},{7,3},{8,12},{9,13},{10,... | collective-permute-start | bytes 3145736 | tf_op jit(solution)/shard_map/ppermute | solution.py:284
  100.0 25.3 %collective-permute-start.22 = (bf16[256,2048]{1,0:T(8,128)(2,1)}, bf16[256,2048]{1,0:T(8,128)(2,1)S(1)}, u32[]{:S(2)}, u32[]{:S(2)}) collective-permute-start(bf16[256,2048]{1,0:T(8,128)(2,1)} %collective-permute-done.21.refs_38_.refs_44_), channel_id=1, source_target_pairs={{0,2},{1,3},{2,0},{3,1},{4,6},{5,7},{6,4},{7,5},{8,10},{9,11},{10,... | collective-permute-start | bytes 3145736 | tf_op jit(solution)/shard_map/ppermute | solution.py:284
  125.3 19.3 %collective-permute-start.26 = (bf16[128,2048]{1,0:T(8,128)(2,1)}, bf16[128,2048]{1,0:T(8,128)(2,1)S(1)}, u32[]{:S(2)}, u32[]{:S(2)}) collective-permute-start(bf16[128,2048]{1,0:T(8,128)(2,1)} %collective-permute-done.20.refs_37_.refs_43_), channel_id=1, source_target_pairs={{0,2},{1,3},{2,0},{3,1},{4,6},{5,7},{6,4},{7,5},{8,10},{9,11},{10,... | collective-permute-start | bytes 1572872 | tf_op jit(solution)/shard_map/ppermute | solution.py:284
  126.2 18.4 %collective-permute-start.27 = (bf16[128,2048]{1,0:T(8,128)(2,1)S(1)}, bf16[128,2048]{1,0:T(8,128)(2,1)S(1)}, u32[]{:S(2)}, u32[]{:S(2)}) collective-permute-start(bf16[128,2048]{1,0:T(8,128)(2,1)S(1)} %copy-done.10), channel_id=1, source_target_pairs={{0,4},{1,5},{2,6},{3,7},{4,0},{5,1},{6,2},{7,3},{8,12},{9,13},{10,... | collective-permute-start | bytes 1572872 | tf_op jit(solution)/shard_map/ppermute | solution.py:284
  127.1 25.1 %collective-permute-start.30 = (bf16[256,2048]{1,0:T(8,128)(2,1)S(1)}, bf16[256,2048]{1,0:T(8,128)(2,1)S(1)}, u32[]{:S(2)}, u32[]{:S(2)}) collective-permute-start(bf16[256,2048]{1,0:T(8,128)(2,1)S(1)} %collective-permute-done.24.refs_9_.refs_47_), channel_id=1, source_target_pairs={{0,8},{1,9},{2,10},{3,11},{4,12},{5,13},{6,14},{7,15},{8,16},{9,17... | collective-permute-start | bytes 3145736 | tf_op jit(solution)/shard_map/ppermute | solution.py:287
  132.2 17.6 %collective-permute-start.29 = (bf16[128,2048]{1,0:T(8,128)(2,1)S(1)}, bf16[128,2048]{1,0:T(8,128)(2,1)S(1)}, u32[]{:S(2)}, u32[]{:S(2)}) collective-permute-start(bf16[128,2048]{1,0:T(8,128)(2,1)S(1)} %slice.15), channel_id=1, source_target_pairs={{0,4},{1,5},{2,6},{3,7},{4,0},{5,1},{6,2},{7,3},{8,12},{9,13},{10,... | collective-permute-start | bytes 1572872 | tf_op jit(solution)/shard_map/ppermute | solution.py:284
  132.8 16.9 %collective-permute-start.28 = (bf16[128,2048]{1,0:T(8,128)(2,1)S(1)}, bf16[128,2048]{1,0:T(8,128)(2,1)S(1)}, u32[]{:S(2)}, u32[]{:S(2)}) collective-permute-start(bf16[128,2048]{1,0:T(8,128)(2,1)S(1)} %slice.14), channel_id=1, source_target_pairs={{0,2},{1,3},{2,0},{3,1},{4,6},{5,7},{6,4},{7,5},{8,10},{9,11},{10,... | collective-permute-start | bytes 1572872 | tf_op jit(solution)/shard_map/ppermute | solution.py:284
  156.9 7.1 %collective-permute-start.31 = (bf16[384,2048]{1,0:T(8,128)(2,1)}, bf16[384,2048]{1,0:T(8,128)(2,1)}, u32[]{:S(2)}, u32[]{:S(2)}) collective-permute-start(bf16[384,2048]{1,0:T(8,128)(2,1)} %project.8), channel_id=1, source_target_pairs={{0,1},{1,0},{2,3},{3,2},{4,5},{5,4},{6,7},{7,6},{8,9},{9,8},{10,11... | collective-permute-start | bytes 4718600 | tf_op jit(solution)/shard_map/ppermute | solution.py:284
  (32 other events, 494.5 us)

commit v4 on v3

--- a/solution.py
+++ b/solution.py
@@ -160,7 +160,7 @@
         out_specs=pl.BlockSpec((step // LANES, rows, LANES), lambda i: (i, 0, 0)),
         out_shape=jax.ShapeDtypeStruct((width // LANES, rows, LANES), BF16),
         compiler_params=params(32),
-        cost_estimate=cost(2 * (BLOCK * LANES // members + 3 * LANES) * rows * width * SCALE, 6 * rows * width),
+        cost_estimate=cost(2 * (BLOCK * LANES // members + 3 * LANES) * rows * width * 3 * SCALE, 6 * rows * width),
         name="convolve",
     )(in_hbm(driven), in_hbm(query), col, row, block_state, incoming, skip)
 
@@ -251,7 +251,7 @@
         ),
         out_shape=[shape] * sides,
         compiler_params=params(48),
-        cost_estimate=cost(2 * len(steps) * LANES * sides * rows * wide * SCALE, 4 * sides * rows * wide),
+        cost_estimate=cost(2 * len(steps) * LANES * sides * rows * wide, 4 * sides * rows * wide),
         name="project",
     )(idx, *operands)
 

time: 167 us -> 165 us (0.988)
  waiting for transfers between devices: 48.1 us -> 45.4 us
    ppermute x21, waiting for transfers between devices: 29.1 us -> 26.1 us  [swap(): return lax.ppermute(a, AXES, [(i, i ^ bit) for i in range(devices)])]
    slice x2, local copies, waits for them, and re-layouts: 0.08 us -> 2.16 us  [local(): over_x, over_y = (over_x[depth:], over_y[:depth])]
    unnamed x66 -> x58, local copies, waits for them, and re-layouts: 8.52 us -> 6.65 us
  transfers between devices with their start and end apart: 32 -> 32, of which waited for: 10 -> 11; matrix products, arithmetic and copies ran while one was open for 10% -> 11% of each run, Pallas kernels for 29% -> 30%
where the time goes in v4:
time: 165 us; the launch traced here: 164 us
  Pallas kernels  56.1 us (34%)
  waiting for transfers between devices  45.4 us (28%)
  starting transfers between devices  35.1 us (21%)
  local copies, waits for them, and re-layouts  19.6 us (12%)
  other arithmetic  7.67 us (5%)
    pallas_call x5, Pallas kernels, project(): pl.pallas_call(lambda *refs: project_kernel(sizes, sides, total is not No...  36 us
    ppermute x21, waiting for transfers between devices, swap(): return lax.ppermute(a, AXES, [(i, i ^ bit) for i in range(devices)])  26.1 us
    ppermute x21, starting transfers between devices, swap(): return lax.ppermute(a, AXES, [(i, i ^ bit) for i in range(devices)])  20 us
    ppermute x6, waiting for transfers between devices, ahead(): lax.ppermute(a, AXES, [(i, (i + 8) % devices) for i in range(devices)])  17.8 us
    pallas_call x1, Pallas kernels, convolve(): pl.pallas_call(lambda *refs: conv_kernel(members, poles, blocks, *refs),...  11.6 us
    ppermute x5, starting transfers between devices, scan_send(): return lax.ppermute(total, 'ctx', [(i, i ^ width) for i in range(slabs)])  10.1 us
    unnamed x58, local copies, waits for them, and re-layouts  6.65 us
    pallas_call x1, Pallas kernels, states(): pl.pallas_call(lambda *refs: state_kernel(members, poles, blocks, *refs),...  5.88 us
  transfers between devices with their start and end apart: 32, of which 11 were waited for; matrix products, arithmetic and copies ran while one was open for 11% of the time, Pallas kernels for 30%

profile of v4, /device:TPU:1, one launch (start us, length us, event | category | flops | bytes accessed | tf_op | source)
XLA Modules:
  0.0 164.4 jit_solution(7188112183449176929)
XLA Ops:
  0.0 2.1 %constant_dynamic-slice_fusion.1 = (bf16[128,2048]{1,0:T(8,128)(2,1)}, bf16[128,2048]{1,0:T(8,128)(2,1)S(1)}) fusion(bf16[128,4096]{1,0:T(8,128)(2,1)} %param.23, s32[]{:T(128)S(6)} %select_n.105, s32[]{:T(128)S(6)} %select_n.104), kind=kLoop, calls=%fused_computation.22 | loop fusion | bytes 2097160 | tf_op jit(solution)/shard_map/dynamic_slice | solution.py:294
  2.1 2.1 %collective-permute-start.2 = (bf16[128,2048]{1,0:T(8,128)(2,1)S(1)}, bf16[128,2048]{1,0:T(8,128)(2,1)}, u32[]{:S(2)}, u32[]{:S(2)}) collective-permute-start(bf16[128,2048]{1,0:T(8,128)(2,1)S(1)} %get-tuple-element.120.refs_21_.refs_27_), channel_id=1, source_target_pairs={{0,8},{1,9},{2,10},{3,11},{4,12},{5,13},{6,14},{7,15},{8,16},{9,17... | collective-permute-start | bytes 1572872 | tf_op jit(solution)/shard_map/ppermute | solution.py:287
  4.2 1.2 collective-permute-start.1
  6.7 1.5 collective-permute-start.3
  10.8 5.9 %states.1 = (bf16[384,4096]{1,0:T(8,128)(2,1)}, f32[48,4096]{1,0:T(8,128)S(1)}, f32[16,4096]{1,0:T(8,128)S(1)}) custom-call(bf16[384,4096]{1,0:T(8,128)(2,1)} %bitcast.12, bf16[384,4096]{1,0:T(8,128)(2,1)} %bitcast.13, f32[4096,2]{1,0:T(8,128)S(1)} %copy.33.refs_2_), custom_call_target="tpu_custom_call" | custom-call | flops 6442450944 | bytes 9437184 | tf_op jit(solution)/shard_map/states/pallas_call | solution.py:118
  19.4 1.2 collective-permute-start.4
  20.6 2.9 %collective-permute-start.7 = (f32[16,4096]{1,0:T(8,128)S(1)}, f32[16,4096]{1,0:T(8,128)}, u32[]{:S(2)}, u32[]{:S(2)}) collective-permute-start(f32[16,4096]{1,0:T(8,128)S(1)} %get-tuple-element.65), channel_id=1, source_target_pairs={{0,1},{1,0},{2,3},{3,2},{4,5},{5,4},{6,7},{7,6},{8,9},{9,8},{10,11... | collective-permute-start | bytes 786440 | tf_op jit(solution)/shard_map/ppermute | solution.py:169
  24.1 2.3 %reshape.17 = f32[16,4096]{1,0:T(8,128)} reshape(f32[16,256,16]{2,1,0:T(8,128)S(1)} %broadcast_in_dim.19) | data formatting | bytes 524288 | tf_op jit(solution)/shard_map/reshape | solution.py:405
  29.2 2.4 %collective-permute-done.6.refs_28_.refs_34_ = bf16[128,2048]{1,0:T(8,128)(2,1)S(1)} collective-permute-done((bf16[128,2048]{1,0:T(8,128)(2,1)}, bf16[128,2048]{1,0:T(8,128)(2,1)S(1)}, u32[]{:S(2)}, u32[]{:S(2)}) %collective-permute-start.6) | collective-permute-done | bytes 524320 | tf_op jit(solution)/shard_map/ppermute | solution.py:287
  31.7 2.4 %collective-permute-start.15 = (f32[16,2048]{1,0:T(8,128)S(1)}, f32[16,2048]{1,0:T(8,128)S(1)}, u32[]{:S(2)}, u32[]{:S(2)}) collective-permute-start(f32[16,2048]{1,0:T(8,128)S(1)} %add_select_fusion.1), channel_id=1, source_target_pairs={{0,6},{1,7},{2,4},{3,5},{4,2},{5,3},{6,0},{7,1},{8,14},{9,15},{10,... | collective-permute-start | bytes 393224 | tf_op jit(solution)/shard_map/ppermute | solution.py:169
  34.4 2.2 %pad_maximum_fusion = bf16[256,2048]{1,0:T(8,128)(2,1)} fusion(bf16[128,2048]{1,0:T(8,128)(2,1)S(1)} %collective-permute-done.6.refs_28_.refs_34_, bf16[128,2048]{1,0:T(8,128)(2,1)} %collective-permute-done.2.refs_27_.refs_33_), kind=kLoop, calls=%fused_computation | loop fusion | flops 2097152 | bytes 2097152 | tf_op jit(solution)/shard_map/concatenate | solution.py:327
  36.6 1.3 collective-permute-done.14
  38.1 4.4 %collective-permute-start.16 = (f32[16,2048]{1,0:T(8,128)S(1)}, f32[16,2048]{1,0:T(8,128)S(1)}, u32[]{:S(2)}, u32[]{:S(2)}) collective-permute-start(f32[16,2048]{1,0:T(8,128)S(1)} %select_add_fusion), channel_id=1, source_target_pairs={{0,1},{1,0},{2,3},{3,2},{4,5},{5,4},{6,7},{7,6},{8,9},{9,8},{10,11... | collective-permute-start | bytes 393224 | tf_op jit(solution)/shard_map/ppermute | solution.py:169
  46.0 2.0 %copy.36.refs_2_ = f32[4096,2]{1,0:T(8,128)} copy(f32[4096,2]{0,1:T(2,128)S(1)} %get-tuple-element.122) | data formatting | bytes 65536 | tf_op jit(solution)/shard_map/stack | solution.py:401
  48.1 2.2 %pad_maximum_fusion.1 = bf16[256,2048]{1,0:T(8,128)(2,1)} fusion(bf16[128,2048]{1,0:T(8,128)(2,1)S(1)} %copy-done.13, bf16[128,2048]{1,0:T(8,128)(2,1)} %collective-permute-done.4.refs_24_.refs_30_), kind=kLoop, calls=%fused_computation.1 | loop fusion | flops 2097152 | bytes 2097152 | tf_op jit(solution)/shard_map/concatenate | solution.py:331
  50.3 17.6 %collective-permute-done.9.refs_30_.refs_36_ = bf16[128,2048]{1,0:T(8,128)(2,1)S(1)} collective-permute-done((bf16[128,2048]{1,0:T(8,128)(2,1)}, bf16[128,2048]{1,0:T(8,128)(2,1)S(1)}, u32[]{:S(2)}, u32[]{:S(2)}) %collective-permute-start.9) | collective-permute-done | bytes 524320 | tf_op jit(solution)/shard_map/ppermute | solution.py:284
  68.1 1.6 fusion.13
  69.6 1.3 collective-permute-start.21
  71.5 1.4 collective-permute-start.18
  75.0 11.6 %convolve.1.refs_1_.refs_2_.refs_3_.refs_4_.refs_5_.refs_6_.refs_7_.refs_8_.refs_9_.refs_10_.refs_11_.refs_12_.refs_13_.refs_14_.refs_15_.refs_16_.refs_17_.refs_18_.refs_19_.refs_20_ = bf16[32,384,128]{2,1,0:T(8,128)(2,1)S(1)} custom-call(bf16[384,4096]{1,0:T(8,128)(2,1)} %get-tuple-element.82.refs_0_, bf16[384,4096]{1,0:T(8,128)(2,1)} %bitcast.14, ...), custom_call_target="tpu_custom_call" | custom-call | flops 53150220288 | bytes 9437184 | tf_op jit(solution)/shard_map/convolve/pallas_call | solution.py:148
  88.5 6.3 %collective-permute-done.20.refs_37_.refs_43_ = bf16[128,2048]{1,0:T(8,128)(2,1)} collective-permute-done((bf16[128,2048]{1,0:T(8,128)(2,1)S(1)}, bf16[128,2048]{1,0:T(8,128)(2,1)}, u32[]{:S(2)}, u32[]{:S(2)}) %collective-permute-start.20) | collective-permute-done | bytes 524320 | tf_op jit(solution)/shard_map/ppermute | solution.py:284
  95.3 2.1 %collective-permute-start.25 = (bf16[32,384,128]{2,1,0:T(8,128)(2,1)S(1)}, bf16[32,384,128]{2,1,0:T(8,128)(2,1)}, u32[]{:S(2)}, u32[]{:S(2)}) collective-permute-start(bf16[32,384,128]{2,1,0:T(8,128)(2,1)S(1)} %convolve.1.refs_1_.refs_2_.refs_3_.refs_4_.refs_5_.refs_6_.refs_7_.refs_8_.refs_9_.refs_10_.refs_11, ...), channel_id=1, source_target_pairs={{0,1},{1,0},{2,3},{3,2},{4,5},{5,4},{6,7},{7,6},{8,9},{9,8},{10,11... | collective-permute-start | bytes 9437192 | tf_op jit(solution)/shard_map/ppermute | solution.py:284
  101.6 9.7 %project.5.refs_10_ = f32[384,2048]{1,0:T(8,128)} custom-call(s32[20]{0:T(128)S(1)} %fusion.5.refs_0_, bf16[32,384,128]{2,1,0:T(8,128)(2,1)} %copy-done, bf16[32,384,128]{2,1,0:T(8,128)(2,1)} %copy-done, bf16[32,384,128]{2,1,0:T(8,128)(2,1)} %copy-done, bf16[32,384,128]{2,1,0:T(8,128)(2,1)} %copy-done, bf16[32,384,128]{2,1,0:T(8,128)(2,1)} %copy-done, ...), custom_call_target="tpu_custom_call" | custom-call | flops 4026531840 | bytes 3145728 | tf_op jit(solution)/shard_map/project/pallas_call | solution.py:244
  111.2 13.1 %collective-permute-done.24.refs_9_.refs_47_ = bf16[256,2048]{1,0:T(8,128)(2,1)} collective-permute-done((bf16[256,2048]{1,0:T(8,128)(2,1)}, bf16[256,2048]{1,0:T(8,128)(2,1)}, u32[]{:S(2)}, u32[]{:S(2)}) %collective-permute-start.24) | collective-permute-done | bytes 1048608 | tf_op jit(solution)/shard_map/ppermute | solution.py:287
  126.7 5.6 %project.6.refs_12_ = f32[384,2048]{1,0:T(8,128)} custom-call(s32[6]{0:T(128)S(1)} %fusion.8.refs_0_, bf16[32,384,128]{2,1,0:T(8,128)(2,1)} %copy-done, bf16[32,384,128]{2,1,0:T(8,128)(2,1)} %copy-done, bf16[32,384,128]{2,1,0:T(8,128)(2,1)} %copy-done, bf16[32,384,128]{2,1,0:T(8,128)(2,1)} %copy-done, bf16[32,384,128]{2,1,0:T(8,128)(2,1)} %copy-done, ...), custom_call_target="tpu_custom_call" | custom-call | flops 1207959552 | bytes 3145728 | tf_op jit(solution)/shard_map/project/pallas_call | solution.py:244
  135.5 11.3 %project.7.refs_12_ = f32[384,2048]{1,0:T(8,128)} custom-call(s32[26]{0:T(128)S(1)} %fusion.11.refs_0_, ...), custom_call_target="tpu_custom_call" | custom-call | flops 5234491392 | bytes 3145728 | tf_op jit(solution)/shard_map/project/pallas_call | solution.py:244
  146.9 2.1 %collective-permute-done.29.refs_10_ = bf16[128,2048]{1,0:T(8,128)(2,1)S(1)} collective-permute-done((bf16[128,2048]{1,0:T(8,128)(2,1)S(1)}, bf16[128,2048]{1,0:T(8,128)(2,1)S(1)}, u32[]{:S(2)}, u32[]{:S(2)}) %collective-permute-start.29) | collective-permute-done | bytes 524320 | tf_op jit(solution)/shard_map/ppermute | solution.py:284
  149.0 1.4 collective-permute-done.30.refs_11_
  150.4 4.7 %project.8 = bf16[384,2048]{1,0:T(8,128)(2,1)} custom-call(s32[6]{0:T(128)S(1)} %fusion.2.refs_0_, ...), custom_call_target="tpu_custom_call" | custom-call | flops 1207959552 | bytes 3145728 | tf_op jit(solution)/shard_map/project/pallas_call | solution.py:244
  155.1 1.7 %collective-permute-start.31 = (bf16[384,2048]{1,0:T(8,128)(2,1)}, bf16[384,2048]{1,0:T(8,128)(2,1)}, u32[]{:S(2)}, u32[]{:S(2)}) collective-permute-start(bf16[384,2048]{1,0:T(8,128)(2,1)} %project.8), channel_id=1, source_target_pairs={{0,1},{1,0},{2,3},{3,2},{4,5},{5,4},{6,7},{7,6},{8,9},{9,8},{10,11... | collective-permute-start | bytes 4718600 | tf_op jit(solution)/shard_map/ppermute | solution.py:284
  156.9 4.7 %project.9.whole_ref = bf16[384,4096]{1,0:T(8,128)(2,1)} custom-call(s32[7]{0:T(128)S(1)} %pad_add_fusion.refs_0_, bf16[32,384,128]{2,1,0:T(8,128)(2,1)} %copy-done, bf16[32,384,128]{2,1,0:T(8,128)(2,1)} %copy-done, bf16[32,384,128]{2,1,0:T(8,128)(2,1)} %copy-done, bf16[32,384,128]{2,1,0:T(8,128)(2,1)} %copy-done, bf16[32,384,128]{2,1,0:T(8,128)(2,1)} %copy-done, ...), custom_call_target="tpu_custom_call" | custom-call | flops 1207959552 | bytes 3145728 | tf_op jit(solution)/shard_map/project/pallas_call | solution.py:244
  161.7 2.6 %put.1 = bf16[384,4096]{1,0:T(8,128)(2,1)} custom-call(s32[1]{0:T(128)} %bitcast.side_ref, bf16[384,2048]{1,0:T(8,128)(2,1)} %collective-permute-done.31.half_ref, bf16[384,4096]{1,0:T(8,128)(2,1)} %project.9.whole_ref), custom_call_target="tpu_custom_call", output_to_operand_aliasing={{}: (2, {})} | custom-call | tf_op jit(solution)/shard_map/put/pallas_call | solution.py:384
  (126 shorter events, 28.8 us)
Async XLA Ops:
  2.1 15.9 %collective-permute-start.2 = (bf16[128,2048]{1,0:T(8,128)(2,1)S(1)}, bf16[128,2048]{1,0:T(8,128)(2,1)}, u32[]{:S(2)}, u32[]{:S(2)}) collective-permute-start(bf16[128,2048]{1,0:T(8,128)(2,1)S(1)} %get-tuple-element.120.refs_21_.refs_27_), channel_id=1, source_target_pairs={{0,8},{1,9},{2,10},{3,11},{4,12},{5,13},{6,14},{7,15},{8,16},{9,17... | collective-permute-start | bytes 1572872 | tf_op jit(solution)/shard_map/ppermute | solution.py:287
  4.2 13.8 %collective-permute-start.1 = (bf16[128,2048]{1,0:T(8,128)(2,1)S(1)}, bf16[128,2048]{1,0:T(8,128)(2,1)S(1)}, u32[]{:S(2)}, u32[]{:S(2)}) collective-permute-start(bf16[128,2048]{1,0:T(8,128)(2,1)S(1)} %get-tuple-element.120.refs_21_.refs_27_), channel_id=1, source_target_pairs={{0,4},{1,5},{2,6},{3,7},{4,0},{5,1},{6,2},{7,3},{8,12},{9,13},{10,... | collective-permute-start | bytes 1572872 | tf_op jit(solution)/shard_map/ppermute | solution.py:284
  5.5 12.5 %collective-permute-start = (bf16[128,2048]{1,0:T(8,128)(2,1)S(1)}, bf16[128,2048]{1,0:T(8,128)(2,1)}, u32[]{:S(2)}, u32[]{:S(2)}) collective-permute-start(bf16[128,2048]{1,0:T(8,128)(2,1)S(1)} %get-tuple-element.120.refs_21_.refs_27_), channel_id=1, source_target_pairs={{0,2},{1,3},{2,0},{3,1},{4,6},{5,7},{6,4},{7,5},{8,10},{9,11},{10,... | collective-permute-start | bytes 1572872 | tf_op jit(solution)/shard_map/ppermute | solution.py:284
  6.7 10.9 %collective-permute-start.3 = (bf16[128,2048]{1,0:T(8,128)(2,1)}, bf16[128,2048]{1,0:T(8,128)(2,1)}, u32[]{:S(2)}, u32[]{:S(2)}) collective-permute-start(bf16[128,2048]{1,0:T(8,128)(2,1)} %get-tuple-element.119), channel_id=1, source_target_pairs={{0,1},{1,0},{2,3},{3,2},{4,5},{5,4},{6,7},{7,6},{8,9},{9,8},{10,11... | collective-permute-start | bytes 1572872 | tf_op jit(solution)/shard_map/ppermute | solution.py:284
  18.0 13.6 %collective-permute-start.6 = (bf16[128,2048]{1,0:T(8,128)(2,1)}, bf16[128,2048]{1,0:T(8,128)(2,1)S(1)}, u32[]{:S(2)}, u32[]{:S(2)}) collective-permute-start(bf16[128,2048]{1,0:T(8,128)(2,1)} %collective-permute-done.3.refs_22_.refs_28_), channel_id=1, source_target_pairs={{0,8},{1,9},{2,10},{3,11},{4,12},{5,13},{6,14},{7,15},{8,16},{9,17... | collective-permute-start | bytes 1572872 | tf_op jit(solution)/shard_map/ppermute | solution.py:287
  19.1 12.6 %collective-permute-start.5 = (bf16[128,2048]{1,0:T(8,128)(2,1)}, bf16[128,2048]{1,0:T(8,128)(2,1)}, u32[]{:S(2)}, u32[]{:S(2)}) collective-permute-start(bf16[128,2048]{1,0:T(8,128)(2,1)} %collective-permute-done.3.refs_22_.refs_28_), channel_id=1, source_target_pairs={{0,4},{1,5},{2,6},{3,7},{4,0},{5,1},{6,2},{7,3},{8,12},{9,13},{10,... | collective-permute-start | bytes 1572872 | tf_op jit(solution)/shard_map/ppermute | solution.py:284
  19.4 12.3 %collective-permute-start.4 = (bf16[128,2048]{1,0:T(8,128)(2,1)}, bf16[128,2048]{1,0:T(8,128)(2,1)}, u32[]{:S(2)}, u32[]{:S(2)}) collective-permute-start(bf16[128,2048]{1,0:T(8,128)(2,1)} %collective-permute-done.3.refs_22_.refs_28_), channel_id=1, source_target_pairs={{0,2},{1,3},{2,0},{3,1},{4,6},{5,7},{6,4},{7,5},{8,10},{9,11},{10,... | collective-permute-start | bytes 1572872 | tf_op jit(solution)/shard_map/ppermute | solution.py:284
  20.6 7.7 %collective-permute-start.7 = (f32[16,4096]{1,0:T(8,128)S(1)}, f32[16,4096]{1,0:T(8,128)}, u32[]{:S(2)}, u32[]{:S(2)}) collective-permute-start(f32[16,4096]{1,0:T(8,128)S(1)} %get-tuple-element.65), channel_id=1, source_target_pairs={{0,1},{1,0},{2,3},{3,2},{4,5},{5,4},{6,7},{7,6},{8,9},{9,8},{10,11... | collective-permute-start | bytes 786440 | tf_op jit(solution)/shard_map/ppermute | solution.py:169
  31.7 4.9 %collective-permute-start.15 = (f32[16,2048]{1,0:T(8,128)S(1)}, f32[16,2048]{1,0:T(8,128)S(1)}, u32[]{:S(2)}, u32[]{:S(2)}) collective-permute-start(f32[16,2048]{1,0:T(8,128)S(1)} %add_select_fusion.1), channel_id=1, source_target_pairs={{0,6},{1,7},{2,4},{3,5},{4,2},{5,3},{6,0},{7,1},{8,14},{9,15},{10,... | collective-permute-start | bytes 393224 | tf_op jit(solution)/shard_map/ppermute | solution.py:169
  34.0 3.8 %collective-permute-start.14 = (f32[16,2048]{1,0:T(8,128)S(1)}, f32[16,2048]{1,0:T(8,128)S(1)}, u32[]{:S(2)}, u32[]{:S(2)}) collective-permute-start(f32[16,2048]{1,0:T(8,128)S(1)} %add_select_fusion.1), channel_id=1, source_target_pairs={{0,4},{1,5},{2,6},{3,7},{4,0},{5,1},{6,2},{7,3},{8,12},{9,13},{10,... | collective-permute-start | bytes 393224 | tf_op jit(solution)/shard_map/ppermute | solution.py:169
  34.0 4.0 %collective-permute-start.13 = (f32[16,2048]{1,0:T(8,128)S(1)}, f32[16,2048]{1,0:T(8,128)S(1)}, u32[]{:S(2)}, u32[]{:S(2)}) collective-permute-start(f32[16,2048]{1,0:T(8,128)S(1)} %add_select_fusion.1), channel_id=1, source_target_pairs={{0,2},{1,3},{2,0},{3,1},{4,6},{5,7},{6,4},{7,5},{8,10},{9,11},{10,... | collective-permute-start | bytes 393224 | tf_op jit(solution)/shard_map/ppermute | solution.py:169
  36.6 31.5 %collective-permute-start.12 = (bf16[256,2048]{1,0:T(8,128)(2,1)}, bf16[256,2048]{1,0:T(8,128)(2,1)}, u32[]{:S(2)}, u32[]{:S(2)}) collective-permute-start(bf16[256,2048]{1,0:T(8,128)(2,1)} %pad_maximum_fusion), channel_id=1, source_target_pairs={{0,8},{1,9},{2,10},{3,11},{4,12},{5,13},{6,14},{7,15},{8,16},{9,17... | collective-permute-start | bytes 3145736 | tf_op jit(solution)/shard_map/ppermute | solution.py:287
  38.1 6.8 %collective-permute-start.16 = (f32[16,2048]{1,0:T(8,128)S(1)}, f32[16,2048]{1,0:T(8,128)S(1)}, u32[]{:S(2)}, u32[]{:S(2)}) collective-permute-start(f32[16,2048]{1,0:T(8,128)S(1)} %select_add_fusion), channel_id=1, source_target_pairs={{0,1},{1,0},{2,3},{3,2},{4,5},{5,4},{6,7},{7,6},{8,9},{9,8},{10,11... | collective-permute-start | bytes 393224 | tf_op jit(solution)/shard_map/ppermute | solution.py:169
  43.0 25.0 %collective-permute-start.10 = (bf16[128,2048]{1,0:T(8,128)(2,1)}, bf16[128,2048]{1,0:T(8,128)(2,1)}, u32[]{:S(2)}, u32[]{:S(2)}) collective-permute-start(bf16[128,2048]{1,0:T(8,128)(2,1)} %collective-permute-done.2.refs_27_.refs_33_), channel_id=1, source_target_pairs={{0,2},{1,3},{2,0},{3,1},{4,6},{5,7},{6,4},{7,5},{8,10},{9,11},{10,... | collective-permute-start | bytes 1572872 | tf_op jit(solution)/shard_map/ppermute | solution.py:284
  43.5 24.6 %collective-permute-start.11 = (bf16[128,2048]{1,0:T(8,128)(2,1)S(1)}, bf16[128,2048]{1,0:T(8,128)(2,1)}, u32[]{:S(2)}, u32[]{:S(2)}) collective-permute-start(bf16[128,2048]{1,0:T(8,128)(2,1)S(1)} %collective-permute-done.6.refs_28_.refs_34_), channel_id=1, source_target_pairs={{0,4},{1,5},{2,6},{3,7},{4,0},{5,1},{6,2},{7,3},{8,12},{9,13},{10,... | collective-permute-start | bytes 1572872 | tf_op jit(solution)/shard_map/ppermute | solution.py:284
  44.6 23.3 %collective-permute-start.9 = (bf16[128,2048]{1,0:T(8,128)(2,1)}, bf16[128,2048]{1,0:T(8,128)(2,1)S(1)}, u32[]{:S(2)}, u32[]{:S(2)}) collective-permute-start(bf16[128,2048]{1,0:T(8,128)(2,1)} %collective-permute-done.refs_23_.refs_29_), channel_id=1, source_target_pairs={{0,4},{1,5},{2,6},{3,7},{4,0},{5,1},{6,2},{7,3},{8,12},{9,13},{10,... | collective-permute-start | bytes 1572872 | tf_op jit(solution)/shard_map/ppermute | solution.py:284
  45.0 23.1 %collective-permute-start.8 = (bf16[128,2048]{1,0:T(8,128)(2,1)}, bf16[128,2048]{1,0:T(8,128)(2,1)S(1)}, u32[]{:S(2)}, u32[]{:S(2)}) collective-permute-start(bf16[128,2048]{1,0:T(8,128)(2,1)} %collective-permute-done.5.refs_26_.refs_32_), channel_id=1, source_target_pairs={{0,2},{1,3},{2,0},{3,1},{4,6},{5,7},{6,4},{7,5},{8,10},{9,11},{10,... | collective-permute-start | bytes 1572872 | tf_op jit(solution)/shard_map/ppermute | solution.py:284
  69.6 25.7 %collective-permute-start.21 = (bf16[256,2048]{1,0:T(8,128)(2,1)}, bf16[256,2048]{1,0:T(8,128)(2,1)}, u32[]{:S(2)}, u32[]{:S(2)}) collective-permute-start(bf16[256,2048]{1,0:T(8,128)(2,1)} %collective-permute-done.12.refs_33_.refs_39_), channel_id=1, source_target_pairs={{0,8},{1,9},{2,10},{3,11},{4,12},{5,13},{6,14},{7,15},{8,16},{9,17... | collective-permute-start | bytes 3145736 | tf_op jit(solution)/shard_map/ppermute | solution.py:287
  70.9 15.6 %collective-permute-start.17 = (bf16[128,2048]{1,0:T(8,128)(2,1)}, bf16[128,2048]{1,0:T(8,128)(2,1)S(1)}, u32[]{:S(2)}, u32[]{:S(2)}) collective-permute-start(bf16[128,2048]{1,0:T(8,128)(2,1)} %collective-permute-done.11.refs_32_.refs_38_), channel_id=1, source_target_pairs={{0,2},{1,3},{2,0},{3,1},{4,6},{5,7},{6,4},{7,5},{8,10},{9,11},{10,... | collective-permute-start | bytes 1572872 | tf_op jit(solution)/shard_map/ppermute | solution.py:284
  71.5 15.9 %collective-permute-start.18 = (bf16[128,2048]{1,0:T(8,128)(2,1)}, bf16[128,2048]{1,0:T(8,128)(2,1)S(1)}, u32[]{:S(2)}, u32[]{:S(2)}) collective-permute-start(bf16[128,2048]{1,0:T(8,128)(2,1)} %collective-permute-done.10.refs_31_.refs_37_), channel_id=1, source_target_pairs={{0,4},{1,5},{2,6},{3,7},{4,0},{5,1},{6,2},{7,3},{8,12},{9,13},{10,... | collective-permute-start | bytes 1572872 | tf_op jit(solution)/shard_map/ppermute | solution.py:284
  73.0 21.9 %collective-permute-start.20 = (bf16[128,2048]{1,0:T(8,128)(2,1)S(1)}, bf16[128,2048]{1,0:T(8,128)(2,1)}, u32[]{:S(2)}, u32[]{:S(2)}) collective-permute-start(bf16[128,2048]{1,0:T(8,128)(2,1)S(1)} %get-tuple-element.117), channel_id=1, source_target_pairs={{0,4},{1,5},{2,6},{3,7},{4,0},{5,1},{6,2},{7,3},{8,12},{9,13},{10,... | collective-permute-start | bytes 1572872 | tf_op jit(solution)/shard_map/ppermute | solution.py:284
  73.0 21.8 %collective-permute-start.19 = (bf16[128,2048]{1,0:T(8,128)(2,1)S(1)}, bf16[128,2048]{1,0:T(8,128)(2,1)}, u32[]{:S(2)}, u32[]{:S(2)}) collective-permute-start(bf16[128,2048]{1,0:T(8,128)(2,1)S(1)} %get-tuple-element.118), channel_id=1, source_target_pairs={{0,2},{1,3},{2,0},{3,1},{4,6},{5,7},{6,4},{7,5},{8,10},{9,11},{10,... | collective-permute-start | bytes 1572872 | tf_op jit(solution)/shard_map/ppermute | solution.py:284
  95.3 29.0 %collective-permute-start.25 = (bf16[32,384,128]{2,1,0:T(8,128)(2,1)S(1)}, bf16[32,384,128]{2,1,0:T(8,128)(2,1)}, u32[]{:S(2)}, u32[]{:S(2)}) collective-permute-start(bf16[32,384,128]{2,1,0:T(8,128)(2,1)S(1)} %convolve.1.refs_1_.refs_2_.refs_3_.refs_4_.refs_5_.refs_6_.refs_7_.refs_8_.refs_9_.refs_10_.refs_11, ...), channel_id=1, source_target_pairs={{0,1},{1,0},{2,3},{3,2},{4,5},{5,4},{6,7},{7,6},{8,9},{9,8},{10,11... | collective-permute-start | bytes 9437192 | tf_op jit(solution)/shard_map/ppermute | solution.py:284
  97.4 26.8 %collective-permute-start.24 = (bf16[256,2048]{1,0:T(8,128)(2,1)}, bf16[256,2048]{1,0:T(8,128)(2,1)}, u32[]{:S(2)}, u32[]{:S(2)}) collective-permute-start(bf16[256,2048]{1,0:T(8,128)(2,1)} %pad_maximum_fusion.1), channel_id=1, source_target_pairs={{0,8},{1,9},{2,10},{3,11},{4,12},{5,13},{6,14},{7,15},{8,16},{9,17... | collective-permute-start | bytes 3145736 | tf_op jit(solution)/shard_map/ppermute | solution.py:287
  97.8 26.4 %collective-permute-start.23 = (bf16[256,2048]{1,0:T(8,128)(2,1)}, bf16[256,2048]{1,0:T(8,128)(2,1)}, u32[]{:S(2)}, u32[]{:S(2)}) collective-permute-start(bf16[256,2048]{1,0:T(8,128)(2,1)} %collective-permute-done.21.refs_38_.refs_44_), channel_id=1, source_target_pairs={{0,4},{1,5},{2,6},{3,7},{4,0},{5,1},{6,2},{7,3},{8,12},{9,13},{10,... | collective-permute-start | bytes 3145736 | tf_op jit(solution)/shard_map/ppermute | solution.py:284
  99.0 25.3 %collective-permute-start.22 = (bf16[256,2048]{1,0:T(8,128)(2,1)}, bf16[256,2048]{1,0:T(8,128)(2,1)}, u32[]{:S(2)}, u32[]{:S(2)}) collective-permute-start(bf16[256,2048]{1,0:T(8,128)(2,1)} %collective-permute-done.21.refs_38_.refs_44_), channel_id=1, source_target_pairs={{0,2},{1,3},{2,0},{3,1},{4,6},{5,7},{6,4},{7,5},{8,10},{9,11},{10,... | collective-permute-start | bytes 3145736 | tf_op jit(solution)/shard_map/ppermute | solution.py:284
  124.3 26.1 %collective-permute-start.30 = (bf16[256,2048]{1,0:T(8,128)(2,1)}, bf16[256,2048]{1,0:T(8,128)(2,1)S(1)}, u32[]{:S(2)}, u32[]{:S(2)}) collective-permute-start(bf16[256,2048]{1,0:T(8,128)(2,1)} %collective-permute-done.24.refs_9_.refs_47_), channel_id=1, source_target_pairs={{0,8},{1,9},{2,10},{3,11},{4,12},{5,13},{6,14},{7,15},{8,16},{9,17... | collective-permute-start | bytes 3145736 | tf_op jit(solution)/shard_map/ppermute | solution.py:287
  124.6 22.3 %collective-permute-start.26 = (bf16[128,2048]{1,0:T(8,128)(2,1)}, bf16[128,2048]{1,0:T(8,128)(2,1)S(1)}, u32[]{:S(2)}, u32[]{:S(2)}) collective-permute-start(bf16[128,2048]{1,0:T(8,128)(2,1)} %collective-permute-done.20.refs_37_.refs_43_), channel_id=1, source_target_pairs={{0,2},{1,3},{2,0},{3,1},{4,6},{5,7},{6,4},{7,5},{8,10},{9,11},{10,... | collective-permute-start | bytes 1572872 | tf_op jit(solution)/shard_map/ppermute | solution.py:284
  125.7 21.2 %collective-permute-start.27 = (bf16[128,2048]{1,0:T(8,128)(2,1)}, bf16[128,2048]{1,0:T(8,128)(2,1)S(1)}, u32[]{:S(2)}, u32[]{:S(2)}) collective-permute-start(bf16[128,2048]{1,0:T(8,128)(2,1)} %collective-permute-done.19.refs_36_.refs_42_), channel_id=1, source_target_pairs={{0,4},{1,5},{2,6},{3,7},{4,0},{5,1},{6,2},{7,3},{8,12},{9,13},{10,... | collective-permute-start | bytes 1572872 | tf_op jit(solution)/shard_map/ppermute | solution.py:284
  134.5 14.5 %collective-permute-start.29 = (bf16[128,2048]{1,0:T(8,128)(2,1)S(1)}, bf16[128,2048]{1,0:T(8,128)(2,1)S(1)}, u32[]{:S(2)}, u32[]{:S(2)}) collective-permute-start(bf16[128,2048]{1,0:T(8,128)(2,1)S(1)} %slice.15), channel_id=1, source_target_pairs={{0,4},{1,5},{2,6},{3,7},{4,0},{5,1},{6,2},{7,3},{8,12},{9,13},{10,... | collective-permute-start | bytes 1572872 | tf_op jit(solution)/shard_map/ppermute | solution.py:284
  135.0 14.0 %collective-permute-start.28 = (bf16[128,2048]{1,0:T(8,128)(2,1)S(1)}, bf16[128,2048]{1,0:T(8,128)(2,1)S(1)}, u32[]{:S(2)}, u32[]{:S(2)}) collective-permute-start(bf16[128,2048]{1,0:T(8,128)(2,1)S(1)} %slice.14), channel_id=1, source_target_pairs={{0,2},{1,3},{2,0},{3,1},{4,6},{5,7},{6,4},{7,5},{8,10},{9,11},{10,... | collective-permute-start | bytes 1572872 | tf_op jit(solution)/shard_map/ppermute | solution.py:284
  155.1 6.5 %collective-permute-start.31 = (bf16[384,2048]{1,0:T(8,128)(2,1)}, bf16[384,2048]{1,0:T(8,128)(2,1)}, u32[]{:S(2)}, u32[]{:S(2)}) collective-permute-start(bf16[384,2048]{1,0:T(8,128)(2,1)} %project.8), channel_id=1, source_target_pairs={{0,1},{1,0},{2,3},{3,2},{4,5},{5,4},{6,7},{7,6},{8,9},{9,8},{10,11... | collective-permute-start | bytes 4718600 | tf_op jit(solution)/shard_map/ppermute | solution.py:284
  (28 other events, 422.1 us)
